TPU v7x, 128 devices: a whole 4x4x4 slice. The times are simulated.
128 devices in a mesh: cluster: 8 (over x, core), row: 16 (over z, y).
Axes of the slice: x: 4, y: 4, z: 4, core: 2. Of those that a mesh axis runs over, the one named last changes fastest.
Arguments:
- sources: bfloat16 [32768, 512], P(('cluster', 'row')), may hold values from -12 to 12
- targets: bfloat16 [32768, 512], P(('cluster', 'row')), may hold values from -12 to 12
- source_order: int32 [32768], P(('cluster', 'row')), may hold values from 0 to 255, as said below
- target_order: int32 [32768], P(('cluster', 'row')), may hold values from 0 to 255, as said below
Outputs:
- source_map: bfloat16 [32768, 512], P(('cluster', 'row'))
- target_map: bfloat16 [32768, 512], P(('cluster', 'row'))
Inputs may be any that keep to these rules, and one draw needn't show every extreme that they name: `source_order`: in each aligned block of 256 consecutive rows every value appears exactly once, so each block holds 32 source rows of every co-cluster. `target_order`: in each aligned block of 256 consecutive rows every value appears exactly once, so each block holds 32 target rows of every co-cluster.
All inputs are finite; a program needn't handle non-finite values.
Results may differ from a plain program's by a relative error of at most 0.01.
Values may be sent and summed in bfloat16 or wider, within the bound.
No kernel may reach another device: no remote copies, remote signals or barrier semaphores. Data moves between devices by JAX's collectives and lax.ppermute only.
A program may use at most 64 MiB of HBM per device.

v0:
```python
import functools
import math

import jax
import jax.numpy as jnp
from jax import lax
from jax.experimental import pallas as pl
from jax.experimental.pallas import tpu as pltpu
from jax.sharding import Mesh, PartitionSpec as P


ITERS = 3
entropy_weight = 0.02
AXES = ("xh", "xl", "core", "zh", "zl", "yh", "yl")
SIZES = (2,) * 7
CLUSTER = ("xh", "zh", "yh")
SWAP = [(0, 1), (1, 0)]
ACROSS = [(i, i ^ 3) for i in range(4)]
VMEM_LIMIT = 24 * 1024 * 1024
LANES = 128
STEP = 128


def compact(column):
    rows = [
        jnp.transpose(jnp.broadcast_to(column[a : a + LANES], (LANES, LANES)))[0:1]
        for a in range(0, column.shape[0], LANES)
    ]
    return jnp.concatenate(rows, axis=0)


def combine(parts):
    highest = functools.reduce(jnp.maximum, parts)
    total = functools.reduce(jnp.add, [jnp.exp2(part - highest) for part in parts])
    return highest + jnp.log2(total)


def flip(part, q):
    per = part.shape[0] // 4
    return jnp.concatenate([part[(p ^ q) * per : ((p ^ q) + 1) * per] for p in range(4)], axis=0)


def aligned(parts):
    return [part if q == 0 else flip(part, q) for q, part in enumerate(parts)]


def put_row(row_ref, value):
    for a in range(value.shape[0]):
        row_ref[0:1, a * LANES : (a + 1) * LANES] = value[a : a + 1]


def put_column(column_ref, value):
    for a in range(value.shape[0]):
        spread = jnp.transpose(jnp.broadcast_to(value[a : a + 1], (LANES, LANES)))
        column_ref[a * LANES : (a + 1) * LANES] = spread[:, 0:1]


def row_lse_chunk(scores):
    highest = jnp.max(scores, axis=1, keepdims=True)
    total = jnp.sum(jnp.exp2(scores - highest), axis=1, keepdims=True)
    return highest + jnp.log2(total)


def pack_kernel(so_hbm, s_hbm, to_hbm, t_hbm, out_ref, so_ref, s_ref, to_ref, t_ref, sems):
    copies = [
        pltpu.make_async_copy(source, target, sems.at[n])
        for n, (source, target) in enumerate(
            ((so_hbm, so_ref), (s_hbm, s_ref), (to_hbm, to_ref), (t_hbm, t_ref))
        )
    ]
    for copy in copies:
        copy.start()
    rows = s_ref.shape[0]
    per = rows // 8
    slots = lax.broadcasted_iota(jnp.int32, (rows, rows), 0)
    for part, (order, matrix) in enumerate(((so_ref, s_ref), (to_ref, t_ref))):
        copies[2 * part].wait()
        copies[2 * part + 1].wait()
        chosen = jnp.where(slots == order[...], 1.0, 0.0).astype(jnp.bfloat16)
        moved = jnp.dot(chosen, matrix[...], preferred_element_type=jnp.float32).astype(jnp.bfloat16)
        for k in range(8):
            out_ref[k, part * per : (part + 1) * per, :] = moved[k * per : (k + 1) * per]


def unpack_kernel(so_ref, to_ref, back_ref, s_ref, t_ref):
    rows = s_ref.shape[0]
    per = rows // 8
    slots = lax.broadcasted_iota(jnp.int32, (rows, rows), 0)
    for part, (order, out) in enumerate(((so_ref, s_ref), (to_ref, t_ref))):
        chosen = jnp.where(slots == order[...], 1.0, 0.0).astype(jnp.bfloat16)
        moved = back_ref[:, part * per : (part + 1) * per, :].reshape(rows, out.shape[1])
        out[...] = lax.dot_general(
            chosen, moved, (((0,), (0,)), ((), ())), preferred_element_type=jnp.float32
        ).astype(jnp.bfloat16)


def target_norms(norm_ref, block, start):
    width = block.shape[1]
    for a in range(0, block.shape[0], LANES):
        wide = block[a : a + LANES, :].astype(jnp.float32)
        square = wide * wide
        folded = functools.reduce(jnp.add, [square[:, c : c + LANES] for c in range(0, width, LANES)])
        norm_ref[0:1, start + a : start + a + LANES] = jnp.sum(jnp.transpose(folded), axis=0, keepdims=True)


def score_block(scale, block, norms, targets, target_row):
    inner = lax.dot_general(block, targets, (((1,), (1,)), ((), ())), preferred_element_type=jnp.float32)
    return (2.0 * inner - norms - target_row) * scale


def first_kernel(scale, s0, s1, s2, s3, t0, t1, t2, m_ref, x_ref, y_ref, lse_ref, sn_ref, norm_ref):
    rows = s0.shape[0]
    for q, s in enumerate((s0, s1, s2, s3)):
        x_ref[q * rows : (q + 1) * rows, :] = s[...]
    for q, t in enumerate((t0, t1, t2)):
        y_ref[q * rows : (q + 1) * rows, :] = t[...]
        target_norms(norm_ref, t, q * rows)
    ready = 3 * rows
    for a in range(0, x_ref.shape[0], STEP):
        block = x_ref[a : a + STEP, :]
        wide = block.astype(jnp.float32)
        norms = jnp.sum(wide * wide, axis=1, keepdims=True)
        sn_ref[a : a + STEP] = norms
        scores = score_block(scale, block, norms, y_ref[0:ready, :], norm_ref[...])
        m_ref[a : a + STEP, 0:ready] = scores
        lse_ref[a // LANES : a // LANES + 1, :] = compact(row_lse_chunk(scores))


def second_kernel(scale, x_ref, sn_ref, part_ref, ta, tb, m_in, y_in, m_ref, y_ref, lse_ref, norm_ref):
    rows = 2 * ta.shape[0]
    ready = 3 * rows
    y_ref[ready : ready + rows // 2, :] = ta[...]
    y_ref[ready + rows // 2 : 4 * rows, :] = tb[...]
    t3 = y_ref.at[pl.ds(ready, rows)]
    target_norms(norm_ref, t3, 0)
    for a in range(0, x_ref.shape[0], STEP):
        scores = score_block(scale, x_ref[a : a + STEP, :], sn_ref[a : a + STEP], t3[...], norm_ref[...])
        m_ref[a : a + STEP, ready : 4 * rows] = scores
        g = a // LANES
        lse_ref[g : g + 1, :] = combine([part_ref[g : g + 1, :], compact(row_lse_chunk(scores))])


def row_kernel(log_mass, m_ref, own, mate, pair, lse_ref, g_ref, row_ref):
    potential = log_mass - combine(aligned([own[...], mate[...], pair[0], pair[1]]))
    g_ref[...] = potential
    put_row(row_ref, potential)
    for a in range(0, m_ref.shape[0], STEP):
        scores = m_ref[a : a + STEP, :] + row_ref[...]
        lse_ref[a // LANES : a // LANES + 1, :] = compact(row_lse_chunk(scores))


def column_kernel(log_mass, m_ref, own, mate, pair, lse_ref, f_ref, column_ref):
    potential = log_mass - combine(aligned([own[...], pair[0], mate[...], pair[1]]))
    f_ref[...] = potential
    put_column(column_ref, potential)
    columns = m_ref.shape[1]
    step = 32

    def fold(values, op):
        return functools.reduce(op, [values[b : b + 8] for b in range(0, step, 8)])

    highest = jnp.full((8, columns), -jnp.inf, jnp.float32)
    for a in range(0, m_ref.shape[0], step):
        highest = jnp.maximum(highest, fold(m_ref[a : a + step, :] + column_ref[a : a + step], jnp.maximum))
    highest = jnp.max(highest, axis=0, keepdims=True)
    total = jnp.zeros((8, columns), jnp.float32)
    for a in range(0, m_ref.shape[0], step):
        scores = m_ref[a : a + step, :] + column_ref[a : a + step]
        total = total + fold(jnp.exp2(scores - highest), jnp.add)
    lse = highest + jnp.log2(jnp.sum(total, axis=0, keepdims=True))
    for a in range(lse_ref.shape[0]):
        lse_ref[a : a + 1, :] = lse[:, a * LANES : (a + 1) * LANES]


def target_kernel(m_ref, x_ref, f, c, p1, p2, p3, p0, column_ref, row_ref):
    put_column(column_ref, f[...])
    put_row(row_ref, c[...])
    step = p0.shape[0]
    for a, out_ref in zip(range(0, m_ref.shape[1], step), (p0, p1, p2, p3)):
        scores = m_ref[:, a : a + step] + column_ref[...]
        weights = jnp.exp2(scores - row_ref[:, a : a + step]).astype(jnp.bfloat16)
        out_ref[...] = lax.dot_general(
            weights, x_ref[...], (((0,), (0,)), ((), ())), preferred_element_type=jnp.float32
        ).astype(jnp.bfloat16)


def source_kernel(m_ref, y_ref, g, r, near_ref, far_ref, column_ref, row_ref):
    put_row(row_ref, g[...])
    put_column(column_ref, r[...])
    half = near_ref.shape[0]
    for a in range(0, m_ref.shape[0], STEP):
        out_ref, b = (near_ref, a) if a < half else (far_ref, a - half)
        scores = m_ref[a : a + STEP, :] + row_ref[...]
        weights = jnp.exp2(scores - column_ref[a : a + STEP]).astype(jnp.bfloat16)
        out_ref[b : b + STEP, :] = jnp.dot(
            weights, y_ref[...], preferred_element_type=jnp.float32
        ).astype(jnp.bfloat16)


def join_kernel(p_ref, near_ref, own, mate, pair, out_ref, far_ref, own_ref, mate_ref):
    rows = out_ref.shape[0]
    parts = aligned([own[...], pair[0], mate[...], pair[1]])
    whole = combine(parts)
    top = whole.shape[0] // 2
    put_column(own_ref, jnp.exp2(parts[0] - whole)[:top])
    put_column(mate_ref, jnp.exp2(parts[2] - whole)[:top])
    mine = p_ref[...].astype(jnp.float32) * own_ref[...]
    joined = (mine + near_ref[...].astype(jnp.float32) * mate_ref[...]).astype(jnp.bfloat16)
    out_ref[...] = joined[:rows]
    far_ref[...] = joined[rows:]


def finish_kernel(s_ref, far_ref, t_ref, t1, t2, t3, own, mate, pair, out_ref, c0, c1, c2, c3):
    rows = far_ref.shape[0]
    per = rows // 8
    summed = (s_ref[...].astype(jnp.float32) + far_ref[...].astype(jnp.float32)).astype(jnp.bfloat16)
    parts = []
    for q, part in enumerate((own[...], mate[...], pair[0], pair[1])):
        lines = part.shape[0] // 4
        parts.append(part[q * lines : (q + 1) * lines])
    whole = combine(parts)
    pieces = [t_ref[...], t1[...], t2[...], t3[...]]
    total = None
    for piece, part, column in zip(pieces, parts, (c0, c1, c2, c3)):
        put_column(column, jnp.exp2(part - whole))
        term = piece.astype(jnp.float32) * column[...]
        total = term if total is None else total + term
    total = total.astype(jnp.bfloat16)
    for k in range(8):
        out_ref[k, 0:per, :] = summed[k * per : (k + 1) * per]
        out_ref[k, per : 2 * per, :] = total[k * per : (k + 1) * per]


def swap(value, axis, pairs=SWAP):
    return lax.ppermute(value, axis, pairs)


def whole(sources, targets, source_order, target_order):
    rows, width = sources.shape
    side = 4 * rows
    per = rows // 8
    log_mass = -math.log2(4 * side)
    scale = 1.0 / (width * entropy_weight * math.log(2.0))
    vmem = pl.BlockSpec(memory_space=pltpu.VMEM)
    hbm = pl.BlockSpec(memory_space=pltpu.HBM)
    f32, bf16 = jnp.float32, jnp.bfloat16
    tile = (side // LANES, LANES)
    area = side * side

    def out(shape, dtype):
        return jax.ShapeDtypeStruct(shape, dtype)

    def call(kernel, outs, scratch, args, flops=0, exps=0, aliases=None, spec=vmem, limit=VMEM_LIMIT):
        return pl.pallas_call(
            kernel,
            out_shape=outs,
            in_specs=[spec] * len(args),
            out_specs=[vmem] * len(outs),
            scratch_shapes=scratch,
            input_output_aliases=aliases or {},
            compiler_params=pltpu.CompilerParams(vmem_limit_bytes=limit),
            cost_estimate=pl.CostEstimate(flops=flops, bytes_accessed=4 * area, transcendentals=exps),
        )(*args)

    def column(n):
        return pltpu.VMEM((n, 1), f32)

    def line(n):
        return pltpu.VMEM((1, n), f32)

    flops = 2 * area * width
    source_line, target_line = source_order.reshape(1, rows), target_order.reshape(1, rows)
    order_block, row_block = pltpu.VMEM((1, rows), jnp.int32), pltpu.VMEM((rows, width), bf16)
    (sent,) = call(
        pack_kernel,
        [out((8, 2 * per, width), bf16)],
        [order_block, row_block, order_block, row_block, pltpu.SemaphoreType.DMA((4,))],
        [source_line, sources, target_line, targets],
        spec=hbm,
        limit=60 * 1024 * 1024,
    )
    got = lax.all_to_all(sent, CLUSTER, split_axis=0, concat_axis=0, tiled=True)
    mine = got[:, :per].reshape(rows, width)
    aims = got[:, per:].reshape(rows, width)

    half = rows // 2
    t1 = swap(aims, "yl")
    t2 = swap(aims, "xl")
    s1 = swap(mine, "zl")
    s2 = swap(mine, "core")
    s3 = swap(s1, "core")
    t3a = swap(t2[:half], "yl")
    t3b = swap(t1[half:], "xl")
    matrix, all_sources, all_targets, part, norms = call(
        functools.partial(first_kernel, scale),
        [out((side, side), f32), out((side, width), bf16), out((side, width), bf16), out(tile, f32), out((side, 1), f32)],
        [line(3 * rows)],
        [mine, s1, s2, s3, aims, t1, t2],
        3 * flops // 4,
        area,
    )
    matrix, all_targets, row_part = call(
        functools.partial(second_kernel, scale),
        [out((side, side), f32), out((side, width), bf16), out(tile, f32)],
        [line(rows)],
        [all_sources, norms, part, t3a, t3b, matrix, all_targets],
        flops // 4,
        area // 4,
        {5: 0, 6: 1},
    )

    def exchange_rows(value):
        mate = swap(value, "core")
        pair = swap(jnp.stack([value, mate]), "zl")
        return [value, mate, pair]

    def exchange_columns(value):
        mate = swap(value, "yl")
        pair = swap(jnp.stack([value, mate]), "xl")
        return [value, mate, pair]

    for _ in range(ITERS):
        column_part, source_potential = call(
            functools.partial(column_kernel, log_mass),
            [out(tile, f32), out(tile, f32)],
            [column(side)],
            [matrix] + exchange_rows(row_part),
            0,
            area,
        )
        column_parts = exchange_columns(column_part)
        row_part, target_potential = call(
            functools.partial(row_kernel, log_mass),
            [out(tile, f32), out(tile, f32)],
            [line(side)],
            [matrix] + column_parts,
            0,
            area,
        )

    piece_1, piece_2, piece_3, own_piece = call(
        target_kernel,
        [out((rows, width), bf16)] * 4,
        [column(side), line(side)],
        [matrix, all_sources, source_potential, column_part],
        flops,
        area,
    )
    target_pieces = [own_piece, swap(piece_1, "yl"), swap(piece_2, "xl"), swap(piece_3, ("xl", "yl"), ACROSS)]
    source_near, source_far = call(
        source_kernel,
        [out((2 * rows, width), bf16), out((2 * rows, width), bf16)],
        [column(side), line(side)],
        [matrix, all_targets, target_potential, row_part],
        flops,
        area,
    )
    row_parts = exchange_rows(row_part)
    near = swap(source_far, "core")
    joined_own, joined_far = call(
        join_kernel,
        [out((rows, width), bf16), out((rows, width), bf16)],
        [column(2 * rows)] * 2,
        [source_near, near] + row_parts,
    )
    far = swap(joined_far, "zl")
    (back,) = call(
        finish_kernel,
        [out((8, 2 * per, width), bf16)],
        [column(rows)] * 4,
        [joined_own, far] + target_pieces + column_parts,
    )
    back = lax.all_to_all(back, CLUSTER, split_axis=0, concat_axis=0, tiled=True)
    return call(
        unpack_kernel, [out((rows, width), bf16), out((rows, width), bf16)], [], [source_line, target_line, back]
    )


def solution(mesh):
    split = Mesh(mesh.devices.reshape(SIZES), AXES)
    return jax.shard_map(
        whole,
        mesh=split,
        in_specs=(P(AXES, None), P(AXES, None), P(AXES), P(AXES)),
        out_specs=(P(AXES, None), P(AXES, None)),
        check_vma=False,
    )
```

profile of v0, /device:TPU:1, one launch (start us, length us, event | category | flops | bytes accessed | tf_op | source)
XLA Modules:
  0.0 123.7 jit_solution(12712299619062679489)
XLA Ops:
  0.6 2.3 %shard_map.59 = bf16[8,64,512]{2,1,0:T(8,128)(2,1)} custom-call(s32[1,256]{1,0:T(1,128)} %bitcast.38, bf16[256,512]{1,0:T(8,128)(2,1)} %s_hbm.1, s32[1,256]{1,0:T(1,128)} %bitcast.40, bf16[256,512]{1,0:T(8,128)(2,1)} %t_hbm.1), custom_call_target="tpu_custom_call" | custom-call | bytes 4194304 | tf_op jit(solution)/shard_map/pallas_call | solution.py:254
  2.9 23.5 %all_to_all.10 = bf16[8,64,512]{2,1,0:T(8,128)(2,1)S(1)} all-to-all(bf16[8,64,512]{2,1,0:T(8,128)(2,1)} %shard_map.59), channel_id=1, replica_groups=mesh['xh'=2,'xl'=2,'core'=2,'zh'=2,'zl'=2,'yh'=2,'yl'=2] {'xh','zh','yh'}, dimensions={0} | all-to-all | bytes 1048576 | tf_op jit(solution)/shard_map/all_to_all | solution.py:282
  28.0 3.0 %collective-permute-start.1 = (bf16[256,512]{1,0:T(8,128)(2,1)S(1)}, bf16[256,512]{1,0:T(8,128)(2,1)S(1)}, u32[]{:S(2)}, u32[]{:S(2)}) collective-permute-start(bf16[256,512]{1,0:T(8,128)(2,1)S(1)} %bitcast.22), channel_id=1, source_target_pairs={{0,16},{16,0},{1,17},{17,1},{2,18},{18,2},{3,19},{19,3},{4,20},{20... | collective-permute-start | bytes 786440 | tf_op jit(solution)/shard_map/ppermute | solution.py:235
  31.0 1.2 collective-permute-done.s1
  32.2 3.0 %collective-permute-start.2 = (bf16[256,512]{1,0:T(8,128)(2,1)S(1)}, bf16[256,512]{1,0:T(8,128)(2,1)S(1)}, u32[]{:S(2)}, u32[]{:S(2)}) collective-permute-start(bf16[256,512]{1,0:T(8,128)(2,1)S(1)} %collective-permute-done.s1), channel_id=1, source_target_pairs={{0,16},{16,0},{1,17},{17,1},{2,18},{18,2},{3,19},{19,3},{4,20},{20... | collective-permute-start | bytes 786440 | tf_op jit(solution)/shard_map/ppermute | solution.py:235
  36.4 2.6 %shard_map.60 = (f32[1024,1024]{1,0:T(8,128)S(1)}, bf16[1024,512]{1,0:T(8,128)(2,1)S(1)}, bf16[1024,512]{1,0:T(8,128)(2,1)S(1)}, f32[8,128]{1,0:T(8,128)S(1)}, f32[1024,1]{1,0:T(8,128)S(1)}) custom-call(bf16[256,512]{1,0:T(8,128)(2,1)S(1)} %bitcast.23, bf16[256,512]{1,0:T(8,128)(2,1)S(1)} %collective-permute-done.s1, ...), custom_call_target="tpu_custom_call" | custom-call | flops 805306368 | bytes 4194304 | tf_op jit(solution)/shard_map/pallas_call | solution.py:254
  39.9 1.2 shard_map.61
  41.1 2.1 %collective-permute-start.7 = (f32[8,128]{1,0:T(8,128)S(1)}, f32[8,128]{1,0:T(8,128)S(1)}, u32[]{:S(2)}, u32[]{:S(2)}) collective-permute-start(f32[8,128]{1,0:T(8,128)S(1)} %get-tuple-element.33.own), channel_id=1, source_target_pairs={{0,16},{16,0},{1,17},{17,1},{2,18},{18,2},{3,19},{19,3},{4,20},{20... | collective-permute-start | bytes 12296 | tf_op jit(solution)/shard_map/ppermute | solution.py:235
  44.7 1.8 %collective-permute-done.8.pair = f32[2,8,128]{2,1,0:T(8,128)S(1)} collective-permute-done((f32[2,8,128]{2,1,0:T(8,128)S(1)}, f32[2,8,128]{2,1,0:T(8,128)S(1)}, u32[]{:S(2)}, u32[]{:S(2)}) %collective-permute-start.8) | collective-permute-done | bytes 8224 | tf_op jit(solution)/shard_map/ppermute | solution.py:235
  46.5 1.2 shard_map.62
  48.8 1.4 %collective-permute-done.9.mate = f32[8,128]{1,0:T(8,128)S(1)} collective-permute-done((f32[8,128]{1,0:T(8,128)S(1)}, f32[8,128]{1,0:T(8,128)S(1)}, u32[]{:S(2)}, u32[]{:S(2)}) %collective-permute-start.9) | collective-permute-done | bytes 4128 | tf_op jit(solution)/shard_map/ppermute | solution.py:235
  51.2 1.5 %collective-permute-done.10.pair = f32[2,8,128]{2,1,0:T(8,128)S(1)} collective-permute-done((f32[2,8,128]{2,1,0:T(8,128)S(1)}, f32[2,8,128]{2,1,0:T(8,128)S(1)}, u32[]{:S(2)}, u32[]{:S(2)}) %collective-permute-start.10) | collective-permute-done | bytes 8224 | tf_op jit(solution)/shard_map/ppermute | solution.py:235
  52.7 1.2 %shard_map.63 = (f32[8,128]{1,0:T(8,128)S(1)}, f32[8,128]{1,0:T(8,128)}) custom-call(f32[1024,1024]{1,0:T(8,128)S(1)} %get-tuple-element.31.m_ref, f32[8,128]{1,0:T(8,128)S(1)} %get-tuple-element.34.own, f32[8,128]{1,0:T(8,128)S(1)} %collective-permute-done.9.mate, f32[2,8,128]{2,1,0:T(8,128)S(1)} %collective-permute-done.10.pair), custom_call_target="tpu_custom_call" | custom-call | bytes 4194304 | tf_op jit(solution)/shard_map/pallas_call | solution.py:254
  54.0 3.8 %collective-permute-start.11 = (f32[8,128]{1,0:T(8,128)S(1)}, f32[8,128]{1,0:T(8,128)S(1)}, u32[]{:S(2)}, u32[]{:S(2)}) collective-permute-start(f32[8,128]{1,0:T(8,128)S(1)} %get-tuple-element.35.own), channel_id=1, source_target_pairs={{0,16},{16,0},{1,17},{17,1},{2,18},{18,2},{3,19},{19,3},{4,20},{20... | collective-permute-start | bytes 12296 | tf_op jit(solution)/shard_map/ppermute | solution.py:235
  59.4 1.8 %collective-permute-done.12.pair = f32[2,8,128]{2,1,0:T(8,128)S(1)} collective-permute-done((f32[2,8,128]{2,1,0:T(8,128)S(1)}, f32[2,8,128]{2,1,0:T(8,128)S(1)}, u32[]{:S(2)}, u32[]{:S(2)}) %collective-permute-start.12) | collective-permute-done | bytes 8224 | tf_op jit(solution)/shard_map/ppermute | solution.py:235
  61.2 1.2 shard_map.64
  63.5 1.4 %collective-permute-done.13.mate = f32[8,128]{1,0:T(8,128)S(1)} collective-permute-done((f32[8,128]{1,0:T(8,128)S(1)}, f32[8,128]{1,0:T(8,128)S(1)}, u32[]{:S(2)}, u32[]{:S(2)}) %collective-permute-start.13) | collective-permute-done | bytes 4128 | tf_op jit(solution)/shard_map/ppermute | solution.py:235
  65.8 1.5 %collective-permute-done.14.pair = f32[2,8,128]{2,1,0:T(8,128)S(1)} collective-permute-done((f32[2,8,128]{2,1,0:T(8,128)S(1)}, f32[2,8,128]{2,1,0:T(8,128)S(1)}, u32[]{:S(2)}, u32[]{:S(2)}) %collective-permute-start.14) | collective-permute-done | bytes 8224 | tf_op jit(solution)/shard_map/ppermute | solution.py:235
  67.4 1.2 %shard_map.65 = (f32[8,128]{1,0:T(8,128)S(1)}, f32[8,128]{1,0:T(8,128)}) custom-call(f32[1024,1024]{1,0:T(8,128)S(1)} %get-tuple-element.31.m_ref, f32[8,128]{1,0:T(8,128)S(1)} %get-tuple-element.36.own, f32[8,128]{1,0:T(8,128)S(1)} %collective-permute-done.13.mate, f32[2,8,128]{2,1,0:T(8,128)S(1)} %collective-permute-done.14.pair), custom_call_target="tpu_custom_call" | custom-call | bytes 4194304 | tf_op jit(solution)/shard_map/pallas_call | solution.py:254
  68.6 3.8 %collective-permute-start.15 = (f32[8,128]{1,0:T(8,128)S(1)}, f32[8,128]{1,0:T(8,128)S(1)}, u32[]{:S(2)}, u32[]{:S(2)}) collective-permute-start(f32[8,128]{1,0:T(8,128)S(1)} %get-tuple-element.37.own), channel_id=1, source_target_pairs={{0,16},{16,0},{1,17},{17,1},{2,18},{18,2},{3,19},{19,3},{4,20},{20... | collective-permute-start | bytes 12296 | tf_op jit(solution)/shard_map/ppermute | solution.py:235
  74.0 1.8 %collective-permute-done.16.pair = f32[2,8,128]{2,1,0:T(8,128)S(1)} collective-permute-done((f32[2,8,128]{2,1,0:T(8,128)S(1)}, f32[2,8,128]{2,1,0:T(8,128)S(1)}, u32[]{:S(2)}, u32[]{:S(2)}) %collective-permute-start.16) | collective-permute-done | bytes 8224 | tf_op jit(solution)/shard_map/ppermute | solution.py:235
  78.1 1.4 %collective-permute-done.17.mate = f32[8,128]{1,0:T(8,128)S(1)} collective-permute-done((f32[8,128]{1,0:T(8,128)S(1)}, f32[8,128]{1,0:T(8,128)S(1)}, u32[]{:S(2)}, u32[]{:S(2)}) %collective-permute-start.17) | collective-permute-done | bytes 4128 | tf_op jit(solution)/shard_map/ppermute | solution.py:235
  80.5 1.5 %collective-permute-done.18.pair = f32[2,8,128]{2,1,0:T(8,128)S(1)} collective-permute-done((f32[2,8,128]{2,1,0:T(8,128)S(1)}, f32[2,8,128]{2,1,0:T(8,128)S(1)}, u32[]{:S(2)}, u32[]{:S(2)}) %collective-permute-start.18) | collective-permute-done | bytes 8224 | tf_op jit(solution)/shard_map/ppermute | solution.py:235
  82.0 1.3 %shard_map.67 = (f32[8,128]{1,0:T(8,128)S(1)}, f32[8,128]{1,0:T(8,128)S(1)}) custom-call(f32[1024,1024]{1,0:T(8,128)S(1)} %get-tuple-element.31.m_ref, f32[8,128]{1,0:T(8,128)S(1)} %get-tuple-element.38.own.c, f32[8,128]{1,0:T(8,128)S(1)} %collective-permute-done.17.mate, f32[2,8,128]{2,1,0:T(8,128)S(1)} %collective-permute-done.18.pair), custom_call_target="tpu_custom_call" | custom-call | bytes 4194304 | tf_op jit(solution)/shard_map/pallas_call | solution.py:254
  83.3 1.7 %shard_map.68 = (bf16[512,512]{1,0:T(8,128)(2,1)S(1)}, bf16[512,512]{1,0:T(8,128)(2,1)S(1)}) custom-call(f32[1024,1024]{1,0:T(8,128)S(1)} %get-tuple-element.31.m_ref, bf16[1024,512]{1,0:T(8,128)(2,1)S(1)} %get-tuple-element.32.y_ref, f32[8,128]{1,0:T(8,128)S(1)} %get-tuple-element.39.g, f32[8,128]{1,0:T(8,128)S(1)} %get-tuple-element.40.r.own), custom_call_target="tpu_custom_call" | custom-call | flops 1073741824 | bytes 4194304 | tf_op jit(solution)/shard_map/pallas_call | solution.py:254
  85.0 3.9 %collective-permute-start.19 = (bf16[512,512]{1,0:T(8,128)(2,1)S(1)}, bf16[512,512]{1,0:T(8,128)(2,1)S(1)}, u32[]{:S(2)}, u32[]{:S(2)}) collective-permute-start(bf16[512,512]{1,0:T(8,128)(2,1)S(1)} %get-tuple-element.42), channel_id=1, source_target_pairs={{0,16},{16,0},{1,17},{17,1},{2,18},{18,2},{3,19},{19,3},{4,20},{20... | collective-permute-start | bytes 1572872 | tf_op jit(solution)/shard_map/ppermute | solution.py:235
  88.9 1.4 %collective-permute-done.20.mate = f32[8,128]{1,0:T(8,128)S(1)} collective-permute-done((f32[8,128]{1,0:T(8,128)S(1)}, f32[8,128]{1,0:T(8,128)S(1)}, u32[]{:S(2)}, u32[]{:S(2)}) %collective-permute-start.20) | collective-permute-done | bytes 4128 | tf_op jit(solution)/shard_map/ppermute | solution.py:235
  91.1 2.3 %shard_map.70 = (bf16[256,512]{1,0:T(8,128)(2,1)S(1)}, bf16[256,512]{1,0:T(8,128)(2,1)S(1)}, bf16[256,512]{1,0:T(8,128)(2,1)S(1)}, bf16[256,512]{1,0:T(8,128)(2,1)S(1)}) custom-call(f32[1024,1024]{1,0:T(8,128)S(1)} %get-tuple-element.31.m_ref, bf16[1024,512]{1,0:T(8,128)(2,1)S(1)} %get-tuple-element.26.x_ref, f32[8,128]{1,0:T(8,128)S(1)} %get-tuple-element.45.f, ...), custom_call_target="tpu_custom_call" | custom-call | flops 1073741824 | bytes 4194304 | tf_op jit(solution)/shard_map/pallas_call | solution.py:254
  94.9 1.3 %collective-permute-start.25 = (bf16[256,512]{1,0:T(8,128)(2,1)S(1)}, bf16[256,512]{1,0:T(8,128)(2,1)S(1)}, u32[]{:S(2)}, u32[]{:S(2)}) collective-permute-start(bf16[256,512]{1,0:T(8,128)(2,1)S(1)} %get-tuple-element.49), channel_id=1, source_target_pairs={{0,33},{1,32},{32,1},{33,0},{2,35},{3,34},{34,3},{35,2},{4,37},{5,... | collective-permute-start | bytes 786440 | tf_op jit(solution)/shard_map/ppermute | solution.py:235
  97.5 3.2 %collective-permute-done.23.t1 = bf16[256,512]{1,0:T(8,128)(2,1)S(1)} collective-permute-done((bf16[256,512]{1,0:T(8,128)(2,1)S(1)}, bf16[256,512]{1,0:T(8,128)(2,1)S(1)}, u32[]{:S(2)}, u32[]{:S(2)}) %collective-permute-start.23) | collective-permute-done | bytes 262176 | tf_op jit(solution)/shard_map/ppermute | solution.py:235
  101.5 5.7 %collective-permute-done.25.t3 = bf16[256,512]{1,0:T(8,128)(2,1)S(1)} collective-permute-done((bf16[256,512]{1,0:T(8,128)(2,1)S(1)}, bf16[256,512]{1,0:T(8,128)(2,1)S(1)}, u32[]{:S(2)}, u32[]{:S(2)}) %collective-permute-start.25) | collective-permute-done | bytes 262176 | tf_op jit(solution)/shard_map/ppermute | solution.py:235
  107.9 14.8 %all_to_all.11.back_ref = bf16[8,64,512]{2,1,0:T(8,128)(2,1)S(1)} all-to-all(bf16[8,64,512]{2,1,0:T(8,128)(2,1)S(1)} %shard_map.71), channel_id=1, replica_groups=mesh['xh'=2,'xl'=2,'core'=2,'zh'=2,'zl'=2,'yh'=2,'yl'=2] {'xh','zh','yh'}, dimensions={0} | all-to-all | bytes 1048576 | tf_op jit(solution)/shard_map/all_to_all | solution.py:373
  (50 shorter events, 21.9 us)
Async XLA Ops:
  26.4 5.8 %collective-permute-start = (bf16[256,512]{1,0:T(8,128)(2,1)S(1)}, bf16[256,512]{1,0:T(8,128)(2,1)S(1)}, u32[]{:S(2)}, u32[]{:S(2)}) collective-permute-start(bf16[256,512]{1,0:T(8,128)(2,1)S(1)} %bitcast.21), channel_id=1, source_target_pairs={{0,4},{4,0},{1,5},{5,1},{2,6},{6,2},{3,7},{7,3},{8,12},{12,8},{9,1... | collective-permute-start | bytes 786440 | tf_op jit(solution)/shard_map/ppermute | solution.py:235
  27.3 8.0 %collective-permute-start.4 = (bf16[256,512]{1,0:T(8,128)(2,1)S(1)}, bf16[256,512]{1,0:T(8,128)(2,1)S(1)}, u32[]{:S(2)}, u32[]{:S(2)}) collective-permute-start(bf16[256,512]{1,0:T(8,128)(2,1)S(1)} %bitcast.18), channel_id=1, source_target_pairs={{0,32},{32,0},{1,33},{33,1},{2,34},{34,2},{3,35},{35,3},{4,36},{36... | collective-permute-start | bytes 786440 | tf_op jit(solution)/shard_map/ppermute | solution.py:235
  27.6 8.2 %collective-permute-start.3 = (bf16[256,512]{1,0:T(8,128)(2,1)S(1)}, bf16[256,512]{1,0:T(8,128)(2,1)S(1)}, u32[]{:S(2)}, u32[]{:S(2)}) collective-permute-start(bf16[256,512]{1,0:T(8,128)(2,1)S(1)} %bitcast.19), channel_id=1, source_target_pairs={{0,1},{1,0},{2,3},{3,2},{4,5},{5,4},{6,7},{7,6},{8,9},{9,8},{10,11... | collective-permute-start | bytes 786440 | tf_op jit(solution)/shard_map/ppermute | solution.py:235
  28.0 8.2 %collective-permute-start.1 = (bf16[256,512]{1,0:T(8,128)(2,1)S(1)}, bf16[256,512]{1,0:T(8,128)(2,1)S(1)}, u32[]{:S(2)}, u32[]{:S(2)}) collective-permute-start(bf16[256,512]{1,0:T(8,128)(2,1)S(1)} %bitcast.22), channel_id=1, source_target_pairs={{0,16},{16,0},{1,17},{17,1},{2,18},{18,2},{3,19},{19,3},{4,20},{20... | collective-permute-start | bytes 786440 | tf_op jit(solution)/shard_map/ppermute | solution.py:235
  32.2 4.2 %collective-permute-start.2 = (bf16[256,512]{1,0:T(8,128)(2,1)S(1)}, bf16[256,512]{1,0:T(8,128)(2,1)S(1)}, u32[]{:S(2)}, u32[]{:S(2)}) collective-permute-start(bf16[256,512]{1,0:T(8,128)(2,1)S(1)} %collective-permute-done.s1), channel_id=1, source_target_pairs={{0,16},{16,0},{1,17},{17,1},{2,18},{18,2},{3,19},{19,3},{4,20},{20... | collective-permute-start | bytes 786440 | tf_op jit(solution)/shard_map/ppermute | solution.py:235
  35.3 4.3 %collective-permute-start.5 = (bf16[128,512]{1,0:T(8,128)(2,1)S(1)}, bf16[128,512]{1,0:T(8,128)(2,1)S(1)}, u32[]{:S(2)}, u32[]{:S(2)}) collective-permute-start(bf16[128,512]{1,0:T(8,128)(2,1)S(1)} %slice.18), channel_id=1, source_target_pairs={{0,1},{1,0},{2,3},{3,2},{4,5},{5,4},{6,7},{7,6},{8,9},{9,8},{10,11... | collective-permute-start | bytes 393224 | tf_op jit(solution)/shard_map/ppermute | solution.py:235
  35.7 4.2 %collective-permute-start.6 = (bf16[128,512]{1,0:T(8,128)(2,1)S(1)}, bf16[128,512]{1,0:T(8,128)(2,1)S(1)}, u32[]{:S(2)}, u32[]{:S(2)}) collective-permute-start(bf16[128,512]{1,0:T(8,128)(2,1)S(1)} %slice.19), channel_id=1, source_target_pairs={{0,32},{32,0},{1,33},{33,1},{2,34},{34,2},{3,35},{35,3},{4,36},{36... | collective-permute-start | bytes 393224 | tf_op jit(solution)/shard_map/ppermute | solution.py:235
  41.1 2.9 %collective-permute-start.7 = (f32[8,128]{1,0:T(8,128)S(1)}, f32[8,128]{1,0:T(8,128)S(1)}, u32[]{:S(2)}, u32[]{:S(2)}) collective-permute-start(f32[8,128]{1,0:T(8,128)S(1)} %get-tuple-element.33.own), channel_id=1, source_target_pairs={{0,16},{16,0},{1,17},{17,1},{2,18},{18,2},{3,19},{19,3},{4,20},{20... | collective-permute-start | bytes 12296 | tf_op jit(solution)/shard_map/ppermute | solution.py:235
  44.0 2.5 %collective-permute-start.8 = (f32[2,8,128]{2,1,0:T(8,128)S(1)}, f32[2,8,128]{2,1,0:T(8,128)S(1)}, u32[]{:S(2)}, u32[]{:S(2)}) collective-permute-start(f32[2,8,128]{2,1,0:T(8,128)S(1)} %pad_maximum_fusion), channel_id=1, source_target_pairs={{0,4},{4,0},{1,5},{5,1},{2,6},{6,2},{3,7},{7,3},{8,12},{12,8},{9,1... | collective-permute-start | bytes 24584 | tf_op jit(solution)/shard_map/ppermute | solution.py:235
  47.7 2.5 %collective-permute-start.9 = (f32[8,128]{1,0:T(8,128)S(1)}, f32[8,128]{1,0:T(8,128)S(1)}, u32[]{:S(2)}, u32[]{:S(2)}) collective-permute-start(f32[8,128]{1,0:T(8,128)S(1)} %get-tuple-element.34.own), channel_id=1, source_target_pairs={{0,1},{1,0},{2,3},{3,2},{4,5},{5,4},{6,7},{7,6},{8,9},{9,8},{10,11... | collective-permute-start | bytes 12296 | tf_op jit(solution)/shard_map/ppermute | solution.py:235
  50.2 2.5 %collective-permute-start.10 = (f32[2,8,128]{2,1,0:T(8,128)S(1)}, f32[2,8,128]{2,1,0:T(8,128)S(1)}, u32[]{:S(2)}, u32[]{:S(2)}) collective-permute-start(f32[2,8,128]{2,1,0:T(8,128)S(1)} %pad_maximum_fusion.1), channel_id=1, source_target_pairs={{0,32},{32,0},{1,33},{33,1},{2,34},{34,2},{3,35},{35,3},{4,36},{36... | collective-permute-start | bytes 24584 | tf_op jit(solution)/shard_map/ppermute | solution.py:235
  54.0 4.7 %collective-permute-start.11 = (f32[8,128]{1,0:T(8,128)S(1)}, f32[8,128]{1,0:T(8,128)S(1)}, u32[]{:S(2)}, u32[]{:S(2)}) collective-permute-start(f32[8,128]{1,0:T(8,128)S(1)} %get-tuple-element.35.own), channel_id=1, source_target_pairs={{0,16},{16,0},{1,17},{17,1},{2,18},{18,2},{3,19},{19,3},{4,20},{20... | collective-permute-start | bytes 12296 | tf_op jit(solution)/shard_map/ppermute | solution.py:235
  58.7 2.5 %collective-permute-start.12 = (f32[2,8,128]{2,1,0:T(8,128)S(1)}, f32[2,8,128]{2,1,0:T(8,128)S(1)}, u32[]{:S(2)}, u32[]{:S(2)}) collective-permute-start(f32[2,8,128]{2,1,0:T(8,128)S(1)} %pad_maximum_fusion.2), channel_id=1, source_target_pairs={{0,4},{4,0},{1,5},{5,1},{2,6},{6,2},{3,7},{7,3},{8,12},{12,8},{9,1... | collective-permute-start | bytes 24584 | tf_op jit(solution)/shard_map/ppermute | solution.py:235
  62.3 2.5 %collective-permute-start.13 = (f32[8,128]{1,0:T(8,128)S(1)}, f32[8,128]{1,0:T(8,128)S(1)}, u32[]{:S(2)}, u32[]{:S(2)}) collective-permute-start(f32[8,128]{1,0:T(8,128)S(1)} %get-tuple-element.36.own), channel_id=1, source_target_pairs={{0,1},{1,0},{2,3},{3,2},{4,5},{5,4},{6,7},{7,6},{8,9},{9,8},{10,11... | collective-permute-start | bytes 12296 | tf_op jit(solution)/shard_map/ppermute | solution.py:235
  64.9 2.5 %collective-permute-start.14 = (f32[2,8,128]{2,1,0:T(8,128)S(1)}, f32[2,8,128]{2,1,0:T(8,128)S(1)}, u32[]{:S(2)}, u32[]{:S(2)}) collective-permute-start(f32[2,8,128]{2,1,0:T(8,128)S(1)} %pad_maximum_fusion.3), channel_id=1, source_target_pairs={{0,32},{32,0},{1,33},{33,1},{2,34},{34,2},{3,35},{35,3},{4,36},{36... | collective-permute-start | bytes 24584 | tf_op jit(solution)/shard_map/ppermute | solution.py:235
  68.6 4.7 %collective-permute-start.15 = (f32[8,128]{1,0:T(8,128)S(1)}, f32[8,128]{1,0:T(8,128)S(1)}, u32[]{:S(2)}, u32[]{:S(2)}) collective-permute-start(f32[8,128]{1,0:T(8,128)S(1)} %get-tuple-element.37.own), channel_id=1, source_target_pairs={{0,16},{16,0},{1,17},{17,1},{2,18},{18,2},{3,19},{19,3},{4,20},{20... | collective-permute-start | bytes 12296 | tf_op jit(solution)/shard_map/ppermute | solution.py:235
  73.3 2.5 %collective-permute-start.16 = (f32[2,8,128]{2,1,0:T(8,128)S(1)}, f32[2,8,128]{2,1,0:T(8,128)S(1)}, u32[]{:S(2)}, u32[]{:S(2)}) collective-permute-start(f32[2,8,128]{2,1,0:T(8,128)S(1)} %pad_maximum_fusion.4), channel_id=1, source_target_pairs={{0,4},{4,0},{1,5},{5,1},{2,6},{6,2},{3,7},{7,3},{8,12},{12,8},{9,1... | collective-permute-start | bytes 24584 | tf_op jit(solution)/shard_map/ppermute | solution.py:235
  77.0 2.5 %collective-permute-start.17 = (f32[8,128]{1,0:T(8,128)S(1)}, f32[8,128]{1,0:T(8,128)S(1)}, u32[]{:S(2)}, u32[]{:S(2)}) collective-permute-start(f32[8,128]{1,0:T(8,128)S(1)} %get-tuple-element.38.own.c), channel_id=1, source_target_pairs={{0,1},{1,0},{2,3},{3,2},{4,5},{5,4},{6,7},{7,6},{8,9},{9,8},{10,11... | collective-permute-start | bytes 12296 | tf_op jit(solution)/shard_map/ppermute | solution.py:235
  79.5 2.5 %collective-permute-start.18 = (f32[2,8,128]{2,1,0:T(8,128)S(1)}, f32[2,8,128]{2,1,0:T(8,128)S(1)}, u32[]{:S(2)}, u32[]{:S(2)}) collective-permute-start(f32[2,8,128]{2,1,0:T(8,128)S(1)} %pad_maximum_fusion.5), channel_id=1, source_target_pairs={{0,32},{32,0},{1,33},{33,1},{2,34},{34,2},{3,35},{35,3},{4,36},{36... | collective-permute-start | bytes 24584 | tf_op jit(solution)/shard_map/ppermute | solution.py:235
  85.0 11.2 %collective-permute-start.19 = (bf16[512,512]{1,0:T(8,128)(2,1)S(1)}, bf16[512,512]{1,0:T(8,128)(2,1)S(1)}, u32[]{:S(2)}, u32[]{:S(2)}) collective-permute-start(bf16[512,512]{1,0:T(8,128)(2,1)S(1)} %get-tuple-element.42), channel_id=1, source_target_pairs={{0,16},{16,0},{1,17},{17,1},{2,18},{18,2},{3,19},{19,3},{4,20},{20... | collective-permute-start | bytes 1572872 | tf_op jit(solution)/shard_map/ppermute | solution.py:235
  88.8 1.5 %collective-permute-start.20 = (f32[8,128]{1,0:T(8,128)S(1)}, f32[8,128]{1,0:T(8,128)S(1)}, u32[]{:S(2)}, u32[]{:S(2)}) collective-permute-start(f32[8,128]{1,0:T(8,128)S(1)} %get-tuple-element.40.r.own), channel_id=1, source_target_pairs={{0,16},{16,0},{1,17},{17,1},{2,18},{18,2},{3,19},{19,3},{4,20},{20... | collective-permute-start | bytes 12296 | tf_op jit(solution)/shard_map/ppermute | solution.py:235
  90.4 5.8 %collective-permute-start.21 = (f32[2,8,128]{2,1,0:T(8,128)S(1)}, f32[2,8,128]{2,1,0:T(8,128)S(1)}, u32[]{:S(2)}, u32[]{:S(2)}) collective-permute-start(f32[2,8,128]{2,1,0:T(8,128)S(1)} %pad_maximum_fusion.6), channel_id=1, source_target_pairs={{0,4},{4,0},{1,5},{5,1},{2,6},{6,2},{3,7},{7,3},{8,12},{12,8},{9,1... | collective-permute-start | bytes 24584 | tf_op jit(solution)/shard_map/ppermute | solution.py:235
  91.1 31.6 %copy-start = (s32[256]{0:T(256)S(1)}, s32[256]{0:T(256)}, u32[]{:S(2)}) copy-start(s32[256]{0:T(256)} %param.6) | copy-start | bytes 3076
  91.1 31.6 %copy-start.1 = (s32[256]{0:T(256)S(1)}, s32[256]{0:T(256)}, u32[]{:S(2)}) copy-start(s32[256]{0:T(256)} %param.7) | copy-start | bytes 3076
  93.5 7.3 %collective-permute-start.23 = (bf16[256,512]{1,0:T(8,128)(2,1)S(1)}, bf16[256,512]{1,0:T(8,128)(2,1)S(1)}, u32[]{:S(2)}, u32[]{:S(2)}) collective-permute-start(bf16[256,512]{1,0:T(8,128)(2,1)S(1)} %get-tuple-element.47), channel_id=1, source_target_pairs={{0,1},{1,0},{2,3},{3,2},{4,5},{5,4},{6,7},{7,6},{8,9},{9,8},{10,11... | collective-permute-start | bytes 786440 | tf_op jit(solution)/shard_map/ppermute | solution.py:235
  94.6 6.9 %collective-permute-start.24 = (bf16[256,512]{1,0:T(8,128)(2,1)S(1)}, bf16[256,512]{1,0:T(8,128)(2,1)S(1)}, u32[]{:S(2)}, u32[]{:S(2)}) collective-permute-start(bf16[256,512]{1,0:T(8,128)(2,1)S(1)} %get-tuple-element.48), channel_id=1, source_target_pairs={{0,32},{32,0},{1,33},{33,1},{2,34},{34,2},{3,35},{35,3},{4,36},{36... | collective-permute-start | bytes 786440 | tf_op jit(solution)/shard_map/ppermute | solution.py:235
  94.9 12.3 %collective-permute-start.25 = (bf16[256,512]{1,0:T(8,128)(2,1)S(1)}, bf16[256,512]{1,0:T(8,128)(2,1)S(1)}, u32[]{:S(2)}, u32[]{:S(2)}) collective-permute-start(bf16[256,512]{1,0:T(8,128)(2,1)S(1)} %get-tuple-element.49), channel_id=1, source_target_pairs={{0,33},{1,32},{32,1},{33,0},{2,35},{3,34},{34,3},{35,2},{4,37},{5,... | collective-permute-start | bytes 786440 | tf_op jit(solution)/shard_map/ppermute | solution.py:235
  96.7 10.6 %collective-permute-start.22 = (bf16[256,512]{1,0:T(8,128)(2,1)S(1)}, bf16[256,512]{1,0:T(8,128)(2,1)S(1)}, u32[]{:S(2)}, u32[]{:S(2)}) collective-permute-start(bf16[256,512]{1,0:T(8,128)(2,1)S(1)} %get-tuple-element.44), channel_id=1, source_target_pairs={{0,4},{4,0},{1,5},{5,1},{2,6},{6,2},{3,7},{7,3},{8,12},{12,8},{9,1... | collective-permute-start | bytes 786440 | tf_op jit(solution)/shard_map/ppermute | solution.py:235
where the time goes:
time: 126 us; the launch traced here: 124 us
  blocking collectives  38.3 us (30%)
  starting transfers between devices  35 us (28%)
  waiting for transfers between devices  30.2 us (24%)
  Pallas kernels  19.5 us (15%)
    ppermute x26, starting transfers between devices, swap(): return lax.ppermute(value, axis, pairs)  35 us
    ppermute x26, waiting for transfers between devices, swap(): return lax.ppermute(value, axis, pairs)  30.2 us
    all_to_all x1, blocking collectives, whole(): got = lax.all_to_all(sent, CLUSTER, split_axis=0, concat_axis=0, tiled=True)  23.5 us
    pallas_call x14, Pallas kernels, call(): pl.pallas_call(kernel, out_shape=outs, in_specs=[spec] * len(args), out_s...  19.5 us
    all_to_all x1, blocking collectives, whole(): lax.all_to_all(back, CLUSTER, split_axis=0, concat_axis=0, tiled=True)  14.8 us
  transfers between devices with their start and end apart: 26, of which 20 were waited for; matrix products, arithmetic and copies ran while one was open for 0% of the time, Pallas kernels for 4%

commit v1 on v0

v1 whole, which is shorter than its diff:
```python
import functools
import itertools
import math

import jax
import jax.numpy as jnp
from jax import lax
from jax.experimental import pallas as pl
from jax.experimental.pallas import tpu as pltpu
from jax.sharding import Mesh, PartitionSpec as P


ITERS = 3
entropy_weight = 0.02
AXES = ("xh", "xl", "core", "zh", "zl", "yh", "yl")
SIZES = (2,) * 7
SWAP = [(0, 1), (1, 0)]
ACROSS = [(i, i ^ 3) for i in range(4)]
VMEM_LIMIT = 24 * 1024 * 1024
LANES = 128
STEP = 128


def compact(column):
    rows = [
        jnp.transpose(jnp.broadcast_to(column[a : a + LANES], (LANES, LANES)))[0:1]
        for a in range(0, column.shape[0], LANES)
    ]
    return jnp.concatenate(rows, axis=0)


def combine(parts):
    highest = functools.reduce(jnp.maximum, parts)
    total = functools.reduce(jnp.add, [jnp.exp2(part - highest) for part in parts])
    return highest + jnp.log2(total)


def flip(part, q):
    per = part.shape[0] // 4
    return jnp.concatenate([part[(p ^ q) * per : ((p ^ q) + 1) * per] for p in range(4)], axis=0)


def aligned(parts):
    return [part if q == 0 else flip(part, q) for q, part in enumerate(parts)]


def put_row(row_ref, value):
    for a in range(value.shape[0]):
        row_ref[0:1, a * LANES : (a + 1) * LANES] = value[a : a + 1]


def put_column(column_ref, value):
    for a in range(value.shape[0]):
        spread = jnp.transpose(jnp.broadcast_to(value[a : a + 1], (LANES, LANES)))
        column_ref[a * LANES : (a + 1) * LANES] = spread[:, 0:1]


def row_lse_chunk(scores):
    highest = jnp.max(scores, axis=1, keepdims=True)
    total = jnp.sum(jnp.exp2(scores - highest), axis=1, keepdims=True)
    return highest + jnp.log2(total)


def pack_kernel(so_hbm, s_hbm, to_hbm, t_hbm, out_ref, so_ref, s_ref, to_ref, t_ref, sems):
    copies = [
        pltpu.make_async_copy(source, target, sems.at[n])
        for n, (source, target) in enumerate(
            ((so_hbm, so_ref), (s_hbm, s_ref), (to_hbm, to_ref), (t_hbm, t_ref))
        )
    ]
    for copy in copies:
        copy.start()
    rows = s_ref.shape[0]
    per = rows // 8
    slots = lax.broadcasted_iota(jnp.int32, (rows, rows), 0)
    for part, (order, matrix) in enumerate(((so_ref, s_ref), (to_ref, t_ref))):
        copies[2 * part].wait()
        copies[2 * part + 1].wait()
        chosen = jnp.where(slots == order[...], 1.0, 0.0).astype(jnp.bfloat16)
        moved = jnp.dot(chosen, matrix[...], preferred_element_type=jnp.float32).astype(jnp.bfloat16)
        for k in range(8):
            out_ref[k, part * per : (part + 1) * per, :] = moved[k * per : (k + 1) * per]


def unpack_kernel(so_ref, to_ref, back_ref, s_ref, t_ref):
    rows = s_ref.shape[0]
    per = rows // 8
    slots = lax.broadcasted_iota(jnp.int32, (rows, rows), 0)
    for part, (order, out) in enumerate(((so_ref, s_ref), (to_ref, t_ref))):
        chosen = jnp.where(slots == order[...], 1.0, 0.0).astype(jnp.bfloat16)
        moved = back_ref[:, part * per : (part + 1) * per, :].reshape(rows, out.shape[1])
        out[...] = lax.dot_general(
            chosen, moved, (((0,), (0,)), ((), ())), preferred_element_type=jnp.float32
        ).astype(jnp.bfloat16)


def target_norms(norm_ref, block, start):
    width = block.shape[1]
    for a in range(0, block.shape[0], LANES):
        wide = block[a : a + LANES, :].astype(jnp.float32)
        square = wide * wide
        folded = functools.reduce(jnp.add, [square[:, c : c + LANES] for c in range(0, width, LANES)])
        norm_ref[0:1, start + a : start + a + LANES] = jnp.sum(jnp.transpose(folded), axis=0, keepdims=True)


def score_rows(scale, rows, x_ref, y_ref, line_ref, m_ref, lse_ref):
    for a in rows:
        block = x_ref[a : a + STEP, :]
        wide = block.astype(jnp.float32)
        norms = jnp.sum(wide * wide, axis=1, keepdims=True)
        inner = lax.dot_general(block, y_ref[...], (((1,), (1,)), ((), ())), preferred_element_type=jnp.float32)
        scores = (2.0 * inner - norms - line_ref[...]) * scale
        m_ref[a : a + STEP, :] = scores
        lse_ref[a // LANES : a // LANES + 1, :] = compact(row_lse_chunk(scores))


def first_kernel(scale, s0, s1, s2, t0, t1, t2, t3, m_ref, x_ref, y_ref, lse_ref, line_ref):
    rows = s0.shape[0]
    for q, s in enumerate((s0, s1, s2)):
        x_ref[q * rows : (q + 1) * rows, :] = s[...]
    for q, t in enumerate((t0, t1, t2, t3)):
        y_ref[q * rows : (q + 1) * rows, :] = t[...]
        target_norms(line_ref, t, q * rows)
    score_rows(scale, range(0, 3 * rows, STEP), x_ref, y_ref, line_ref, m_ref, lse_ref)


def second_kernel(scale, y_ref, line_ref, part_ref, sa, sb, m_in, x_in, m_ref, x_ref, lse_ref):
    half = sa.shape[0]
    ready = 6 * half
    x_ref[ready : ready + half, :] = sa[...]
    x_ref[ready + half : ready + 2 * half, :] = sb[...]
    lines = ready // LANES
    lse_ref[0:lines, :] = part_ref[0:lines, :]
    score_rows(scale, range(ready, ready + 2 * half, STEP), x_ref, y_ref, line_ref, m_ref, lse_ref)


def row_kernel(log_mass, m_ref, c0, c1, c2, c3, lse_ref, row_ref):
    put_row(row_ref, log_mass - combine(aligned([c0[...], c1[...], c2[...], c3[...]])))
    for a in range(0, m_ref.shape[0], STEP):
        scores = m_ref[a : a + STEP, :] + row_ref[...]
        lse_ref[a // LANES : a // LANES + 1, :] = compact(row_lse_chunk(scores))


def column_kernel(log_mass, m_ref, r0, r1, r2, r3, lse_ref, f_ref, column_ref):
    potential = log_mass - combine(aligned([r0[...], r1[...], r2[...], r3[...]]))
    f_ref[...] = potential
    put_column(column_ref, potential)
    columns = m_ref.shape[1]
    step = 32

    def fold(values, op):
        return functools.reduce(op, [values[b : b + 8] for b in range(0, step, 8)])

    highest = jnp.full((8, columns), -jnp.inf, jnp.float32)
    for a in range(0, m_ref.shape[0], step):
        highest = jnp.maximum(highest, fold(m_ref[a : a + step, :] + column_ref[a : a + step], jnp.maximum))
    highest = jnp.max(highest, axis=0, keepdims=True)
    total = jnp.zeros((8, columns), jnp.float32)
    for a in range(0, m_ref.shape[0], step):
        scores = m_ref[a : a + step, :] + column_ref[a : a + step]
        total = total + fold(jnp.exp2(scores - highest), jnp.add)
    lse = highest + jnp.log2(jnp.sum(total, axis=0, keepdims=True))
    for a in range(lse_ref.shape[0]):
        lse_ref[a : a + 1, :] = lse[:, a * LANES : (a + 1) * LANES]


def target_kernel(m_ref, x_ref, f, c, near_ref, far_ref, column_ref, row_ref):
    put_column(column_ref, f[...])
    put_row(row_ref, c[...])
    step = 256
    half = near_ref.shape[0]
    for a in range(0, m_ref.shape[1], step):
        out_ref, b = (near_ref, a) if a < half else (far_ref, a - half)
        scores = m_ref[:, a : a + step] + column_ref[...]
        weights = jnp.exp2(scores - row_ref[:, a : a + step]).astype(jnp.bfloat16)
        out_ref[b : b + step, :] = lax.dot_general(
            weights, x_ref[...], (((0,), (0,)), ((), ())), preferred_element_type=jnp.float32
        ).astype(jnp.bfloat16)


def source_kernel(log_mass, m_ref, y_ref, c0, c1, c2, c3, p0, p1, p2, p3, lse_ref, row_ref):
    put_row(row_ref, log_mass - combine(aligned([c0[...], c1[...], c2[...], c3[...]])))
    rows = p0.shape[0]
    for a in range(0, m_ref.shape[0], STEP):
        scores = m_ref[a : a + STEP, :] + row_ref[...]
        highest = jnp.max(scores, axis=1, keepdims=True)
        raised = jnp.exp2(scores - highest)
        total = jnp.sum(raised, axis=1, keepdims=True)
        mapped = jnp.dot(raised.astype(jnp.bfloat16), y_ref[...], preferred_element_type=jnp.float32)
        out_ref, b = (p0, p1, p2, p3)[a // rows], a % rows
        out_ref[b : b + STEP, :] = (mapped / total).astype(jnp.bfloat16)
        lse_ref[a // LANES : a // LANES + 1, :] = compact(highest + jnp.log2(total))


def join_kernel(p_ref, near_ref, c0, c1, c2, c3, out_ref, far_ref, own_ref, mate_ref):
    rows = out_ref.shape[0]
    parts = aligned([c0[...], c1[...], c2[...], c3[...]])
    whole = combine(parts)
    top = whole.shape[0] // 2
    put_column(own_ref, jnp.exp2(parts[0] - whole)[:top])
    put_column(mate_ref, jnp.exp2(parts[2] - whole)[:top])
    mine = p_ref[...].astype(jnp.float32) * own_ref[...]
    joined = (mine + near_ref[...].astype(jnp.float32) * mate_ref[...]).astype(jnp.bfloat16)
    out_ref[...] = joined[:rows]
    far_ref[...] = joined[rows:]


def finish_kernel(t_ref, far_ref, s0, s1, s2, s3, r0, r1, r2, r3, out_ref, w0, w1, w2, w3):
    rows = t_ref.shape[0]
    per = rows // 8
    parts = []
    for q, part in enumerate((r0, r1, r2, r3)):
        lines = part.shape[0] // 4
        parts.append(part[q * lines : (q + 1) * lines, :])
    whole = combine(parts)
    total = None
    for piece, part, column in zip((s0, s1, s2, s3), parts, (w0, w1, w2, w3)):
        put_column(column, jnp.exp2(part - whole))
        term = piece[...].astype(jnp.float32) * column[...]
        total = term if total is None else total + term
    total = total.astype(jnp.bfloat16)
    summed = (t_ref[...].astype(jnp.float32) + far_ref[...].astype(jnp.float32)).astype(jnp.bfloat16)
    for k in range(8):
        out_ref[k, 0:per, :] = total[k * per : (k + 1) * per]
        out_ref[k, per : 2 * per, :] = summed[k * per : (k + 1) * per]


def swap(value, axis, pairs=SWAP):
    return lax.ppermute(value, axis, pairs)


def place_of(xh, xl, core, zh, zl, yh, yl):
    index = 0
    for bit in (xh, xl, core, zh, zl, yh, yl):
        index = 2 * index + bit
    return index


def groups():
    return [
        [
            place_of(xh, gx ^ xh, core, zh, gz ^ zh, yh, gy ^ yh)
            for xh, zh, yh in itertools.product((0, 1), repeat=3)
        ]
        for gx, core, gz, gy in itertools.product((0, 1), repeat=4)
    ]


def across(value):
    return lax.all_to_all(value, AXES, split_axis=0, concat_axis=0, axis_index_groups=groups(), tiled=True)


def whole(sources, targets, source_order, target_order):
    rows, width = sources.shape
    side = 4 * rows
    per = rows // 8
    log_mass = -math.log2(4 * side)
    scale = 1.0 / (width * entropy_weight * math.log(2.0))
    vmem = pl.BlockSpec(memory_space=pltpu.VMEM)
    hbm = pl.BlockSpec(memory_space=pltpu.HBM)
    f32, bf16 = jnp.float32, jnp.bfloat16
    tile = (side // LANES, LANES)
    area = side * side

    def out(shape, dtype):
        return jax.ShapeDtypeStruct(shape, dtype)

    def call(kernel, outs, scratch, args, flops=0, exps=0, aliases=None, spec=vmem, limit=VMEM_LIMIT):
        return pl.pallas_call(
            kernel,
            out_shape=outs,
            in_specs=[spec] * len(args),
            out_specs=[vmem] * len(outs),
            scratch_shapes=scratch,
            input_output_aliases=aliases or {},
            compiler_params=pltpu.CompilerParams(vmem_limit_bytes=limit),
            cost_estimate=pl.CostEstimate(flops=flops, bytes_accessed=4 * area, transcendentals=exps),
        )(*args)

    def column(n):
        return pltpu.VMEM((n, 1), f32)

    def line(n):
        return pltpu.VMEM((1, n), f32)

    flops = 2 * area * width
    source_line, target_line = source_order.reshape(1, rows), target_order.reshape(1, rows)
    order_block, row_block = pltpu.VMEM((1, rows), jnp.int32), pltpu.VMEM((rows, width), bf16)
    (sent,) = call(
        pack_kernel,
        [out((8, 2 * per, width), bf16)],
        [order_block, row_block, order_block, row_block, pltpu.SemaphoreType.DMA((4,))],
        [source_line, sources, target_line, targets],
        spec=hbm,
        limit=60 * 1024 * 1024,
    )
    got = across(sent)
    mine = got[:, :per].reshape(rows, width)
    aims = got[:, per:].reshape(rows, width)

    half = rows // 2
    s1 = swap(mine, "yl")
    s2 = swap(mine, "xl")
    t1 = swap(aims, "zl")
    t2 = swap(aims, "core")
    t3 = swap(t1, "core")
    s3a = swap(s2[:half], "yl")
    s3b = swap(s1[half:], "xl")
    matrix, all_sources, all_targets, part, norms = call(
        functools.partial(first_kernel, scale),
        [out((side, side), f32), out((side, width), bf16), out((side, width), bf16), out(tile, f32), out((1, side), f32)],
        [],
        [mine, s1, s2, aims, t1, t2, t3],
        3 * flops // 4,
        area,
    )
    matrix, all_sources, row_part = call(
        functools.partial(second_kernel, scale),
        [out((side, side), f32), out((side, width), bf16), out(tile, f32)],
        [],
        [all_targets, norms, part, s3a, s3b, matrix, all_sources],
        flops // 4,
        area // 4,
        {5: 0, 6: 1},
    )

    def exchange(value, slow, fast):
        both = swap(value, (slow, fast), ACROSS)
        second = swap(value, slow)
        first = swap(value, fast)
        return [value, first, second, both]

    for repeat in range(ITERS):
        column_part, source_potential = call(
            functools.partial(column_kernel, log_mass),
            [out(tile, f32), out(tile, f32)],
            [column(side)],
            [matrix] + exchange(row_part, "xl", "yl"),
            0,
            area,
        )
        column_parts = exchange(column_part, "core", "zl")
        if repeat < ITERS - 1:
            (row_part,) = call(
                functools.partial(row_kernel, log_mass),
                [out(tile, f32)],
                [line(side)],
                [matrix] + column_parts,
                0,
                area,
            )

    target_near, target_far = call(
        target_kernel,
        [out((2 * rows, width), bf16)] * 2,
        [column(side), line(side)],
        [matrix, all_sources, source_potential, column_part],
        flops,
        area,
    )
    near = swap(target_far, "core")
    own_piece, piece_1, piece_2, piece_3, row_part = call(
        functools.partial(source_kernel, log_mass),
        [out((rows, width), bf16)] * 4 + [out(tile, f32)],
        [line(side)],
        [matrix, all_targets] + column_parts,
        flops,
        area,
    )
    source_pieces = [own_piece, swap(piece_1, "yl"), swap(piece_2, "xl"), swap(piece_3, ("xl", "yl"), ACROSS)]
    row_parts = exchange(row_part, "xl", "yl")
    joined_own, joined_far = call(
        join_kernel, [out((rows, width), bf16)] * 2, [column(2 * rows)] * 2, [target_near, near] + column_parts
    )
    far = swap(joined_far, "zl")
    (back,) = call(
        finish_kernel,
        [out((8, 2 * per, width), bf16)],
        [column(rows)] * 4,
        [joined_own, far] + source_pieces + row_parts,
    )
    return call(
        unpack_kernel,
        [out((rows, width), bf16), out((rows, width), bf16)],
        [],
        [source_line, target_line, across(back)],
    )


def solution(mesh):
    split = Mesh(mesh.devices.reshape(SIZES), AXES)
    return jax.shard_map(
        whole,
        mesh=split,
        in_specs=(P(AXES, None), P(AXES, None), P(AXES), P(AXES)),
        out_specs=(P(AXES, None), P(AXES, None)),
        check_vma=False,
    )
```

time: 126 us -> 122 us (0.968)
  the two profiles are of different devices: /device:TPU:1 before, /device:TPU:0 now
where the time goes in v1:
time: 122 us
  blocking collectives  37.2 us (30%)
  waiting for transfers between devices  35.6 us (29%)
  starting transfers between devices  29.4 us (24%)
  Pallas kernels  18.4 us (15%)
    all_to_all x2, blocking collectives, across(): lax.all_to_all(value, AXES, split_axis=0, concat_axis=0, axis_index_group...  37.2 us
    ppermute x33, waiting for transfers between devices, swap(): return lax.ppermute(value, axis, pairs)  35.6 us
    ppermute x33, starting transfers between devices, swap(): return lax.ppermute(value, axis, pairs)  29.4 us
    pallas_call x13, Pallas kernels, call(): pl.pallas_call(kernel, out_shape=outs, in_specs=[spec] * len(args), out_s...  18.4 us
  transfers between devices with their start and end apart: 33, of which 21 were waited for; matrix products, arithmetic and copies ran while one was open for 0% of the time, Pallas kernels for 4%

profile of v1, /device:TPU:0, one launch (start us, length us, event | category | flops | bytes accessed | tf_op | source)
XLA Modules:
  0.0 121.6 jit_solution(11241362678597545033)
XLA Ops:
  0.6 2.2 %shard_map.59 = bf16[8,64,512]{2,1,0:T(8,128)(2,1)} custom-call(s32[1,256]{1,0:T(1,128)} %bitcast.10, bf16[256,512]{1,0:T(8,128)(2,1)} %s_hbm.1, s32[1,256]{1,0:T(1,128)} %bitcast.12, bf16[256,512]{1,0:T(8,128)(2,1)} %t_hbm.1), custom_call_target="tpu_custom_call" | custom-call | bytes 4194304 | tf_op jit(solution)/shard_map/pallas_call | solution.py:269
  2.9 23.1 %all_to_all.10 = bf16[8,64,512]{2,1,0:T(8,128)(2,1)S(1)} all-to-all(bf16[8,64,512]{2,1,0:T(8,128)(2,1)} %shard_map.59), channel_id=1, replica_groups={{0,3,12,15,96,99,108,111},{1,2,13,14,97,98,109,110},{4,7,8,11,100,103,1..., dimensions={0} | all-to-all | bytes 1048576 | tf_op jit(solution)/shard_map/all_to_all | solution.py:250
  26.4 6.3 %collective-permute-done.2.t1 = bf16[256,512]{1,0:T(8,128)(2,1)S(1)} collective-permute-done((bf16[256,512]{1,0:T(8,128)(2,1)S(1)}, bf16[256,512]{1,0:T(8,128)(2,1)S(1)}, u32[]{:S(2)}, u32[]{:S(2)}) %collective-permute-start.2) | collective-permute-done | bytes 262176 | tf_op jit(solution)/shard_map/ppermute | solution.py:229
  32.9 1.8 %collective-permute-start.6 = (bf16[128,512]{1,0:T(8,128)(2,1)S(1)}, bf16[128,512]{1,0:T(8,128)(2,1)S(1)}, u32[]{:S(2)}, u32[]{:S(2)}) collective-permute-start(bf16[128,512]{1,0:T(8,128)(2,1)S(1)} %slice.19), channel_id=1, source_target_pairs={{0,32},{32,0},{1,33},{33,1},{2,34},{34,2},{3,35},{35,3},{4,36},{36... | collective-permute-start | bytes 393224 | tf_op jit(solution)/shard_map/ppermute | solution.py:229
  34.7 2.6 %shard_map.60 = (f32[1024,1024]{1,0:T(8,128)S(1)}, bf16[1024,512]{1,0:T(8,128)(2,1)S(1)}, bf16[1024,512]{1,0:T(8,128)(2,1)S(1)}, f32[8,128]{1,0:T(8,128)S(1)}, f32[1,1024]{1,0:T(1,128)S(1)}) custom-call(bf16[256,512]{1,0:T(8,128)(2,1)S(1)} %bitcast.9, bf16[256,512]{1,0:T(8,128)(2,1)S(1)} %collective-permute-done.s1, ...), custom_call_target="tpu_custom_call" | custom-call | flops 805306368 | bytes 4194304 | tf_op jit(solution)/shard_map/pallas_call | solution.py:269
  37.3 1.4 %collective-permute-done.5.sa = bf16[128,512]{1,0:T(8,128)(2,1)S(1)} collective-permute-done((bf16[128,512]{1,0:T(8,128)(2,1)S(1)}, bf16[128,512]{1,0:T(8,128)(2,1)S(1)}, u32[]{:S(2)}, u32[]{:S(2)}) %collective-permute-start.5) | collective-permute-done | bytes 131104 | tf_op jit(solution)/shard_map/ppermute | solution.py:229
  40.0 1.5 %collective-permute-start.9 = (f32[8,128]{1,0:T(8,128)S(1)}, f32[8,128]{1,0:T(8,128)S(1)}, u32[]{:S(2)}, u32[]{:S(2)}) collective-permute-start(f32[8,128]{1,0:T(8,128)S(1)} %get-tuple-element.30.r0), channel_id=1, source_target_pairs={{0,33},{1,32},{32,1},{33,0},{2,35},{3,34},{34,3},{35,2},{4,37},{5,... | collective-permute-start | bytes 12296 | tf_op jit(solution)/shard_map/ppermute | solution.py:229
  41.5 1.7 %collective-permute-start.8 = (f32[8,128]{1,0:T(8,128)S(1)}, f32[8,128]{1,0:T(8,128)S(1)}, u32[]{:S(2)}, u32[]{:S(2)}) collective-permute-start(f32[8,128]{1,0:T(8,128)S(1)} %get-tuple-element.30.r0), channel_id=1, source_target_pairs={{0,32},{32,0},{1,33},{33,1},{2,34},{34,2},{3,35},{35,3},{4,36},{36... | collective-permute-start | bytes 12296 | tf_op jit(solution)/shard_map/ppermute | solution.py:229
  45.1 1.7 %collective-permute-done.7.r1 = f32[8,128]{1,0:T(8,128)S(1)} collective-permute-done((f32[8,128]{1,0:T(8,128)S(1)}, f32[8,128]{1,0:T(8,128)S(1)}, u32[]{:S(2)}, u32[]{:S(2)}) %collective-permute-start.7) | collective-permute-done | bytes 4128 | tf_op jit(solution)/shard_map/ppermute | solution.py:229
  48.1 1.3 %collective-permute-start.11 = (f32[8,128]{1,0:T(8,128)S(1)}, f32[8,128]{1,0:T(8,128)S(1)}, u32[]{:S(2)}, u32[]{:S(2)}) collective-permute-start(f32[8,128]{1,0:T(8,128)S(1)} %get-tuple-element.31.c0), channel_id=1, source_target_pairs={{0,16},{16,0},{1,17},{17,1},{2,18},{18,2},{3,19},{19,3},{4,20},{20... | collective-permute-start | bytes 12296 | tf_op jit(solution)/shard_map/ppermute | solution.py:229
  51.1 1.9 %collective-permute-done.10.c1 = f32[8,128]{1,0:T(8,128)S(1)} collective-permute-done((f32[8,128]{1,0:T(8,128)S(1)}, f32[8,128]{1,0:T(8,128)S(1)}, u32[]{:S(2)}, u32[]{:S(2)}) %collective-permute-start.10) | collective-permute-done | bytes 4128 | tf_op jit(solution)/shard_map/ppermute | solution.py:229
  53.0 1.2 %shard_map.63.r0 = f32[8,128]{1,0:T(8,128)S(1)} custom-call(f32[1024,1024]{1,0:T(8,128)S(1)} %get-tuple-element.28.m_ref, f32[8,128]{1,0:T(8,128)S(1)} %get-tuple-element.31.c0, f32[8,128]{1,0:T(8,128)S(1)} %collective-permute-done.10.c1, f32[8,128]{1,0:T(8,128)S(1)} %collective-permute-done.11.c2, f32[8,128]{1,0:T(8,128)S(1)} %collective-permute-done.12.c3), custom_call_target="tpu_custom_call" | custom-call | bytes 4194304 | tf_op jit(solution)/shard_map/pallas_call | solution.py:269
  54.2 2.8 %collective-permute-start.15 = (f32[8,128]{1,0:T(8,128)S(1)}, f32[8,128]{1,0:T(8,128)S(1)}, u32[]{:S(2)}, u32[]{:S(2)}) collective-permute-start(f32[8,128]{1,0:T(8,128)S(1)} %shard_map.63.r0), channel_id=1, source_target_pairs={{0,33},{1,32},{32,1},{33,0},{2,35},{3,34},{34,3},{35,2},{4,37},{5,... | collective-permute-start | bytes 12296 | tf_op jit(solution)/shard_map/ppermute | solution.py:229
  58.8 1.8 %collective-permute-done.14.r2 = f32[8,128]{1,0:T(8,128)S(1)} collective-permute-done((f32[8,128]{1,0:T(8,128)S(1)}, f32[8,128]{1,0:T(8,128)S(1)}, u32[]{:S(2)}, u32[]{:S(2)}) %collective-permute-start.14) | collective-permute-done | bytes 4128 | tf_op jit(solution)/shard_map/ppermute | solution.py:229
  62.1 2.0 %collective-permute-start.16 = (f32[8,128]{1,0:T(8,128)S(1)}, f32[8,128]{1,0:T(8,128)S(1)}, u32[]{:S(2)}, u32[]{:S(2)}) collective-permute-start(f32[8,128]{1,0:T(8,128)S(1)} %get-tuple-element.32.c0), channel_id=1, source_target_pairs={{0,4},{4,0},{1,5},{5,1},{2,6},{6,2},{3,7},{7,3},{8,12},{12,8},{9,1... | collective-permute-start | bytes 12296 | tf_op jit(solution)/shard_map/ppermute | solution.py:229
  65.8 1.2 %shard_map.65.r0 = f32[8,128]{1,0:T(8,128)S(1)} custom-call(f32[1024,1024]{1,0:T(8,128)S(1)} %get-tuple-element.28.m_ref, f32[8,128]{1,0:T(8,128)S(1)} %get-tuple-element.32.c0, f32[8,128]{1,0:T(8,128)S(1)} %collective-permute-done.16.c1, f32[8,128]{1,0:T(8,128)S(1)} %collective-permute-done.17.c2, f32[8,128]{1,0:T(8,128)S(1)} %collective-permute-done.18.c3), custom_call_target="tpu_custom_call" | custom-call | bytes 4194304 | tf_op jit(solution)/shard_map/pallas_call | solution.py:269
  67.1 1.5 %collective-permute-start.21 = (f32[8,128]{1,0:T(8,128)S(1)}, f32[8,128]{1,0:T(8,128)S(1)}, u32[]{:S(2)}, u32[]{:S(2)}) collective-permute-start(f32[8,128]{1,0:T(8,128)S(1)} %shard_map.65.r0), channel_id=1, source_target_pairs={{0,33},{1,32},{32,1},{33,0},{2,35},{3,34},{34,3},{35,2},{4,37},{5,... | collective-permute-start | bytes 12296 | tf_op jit(solution)/shard_map/ppermute | solution.py:229
  68.6 1.4 %collective-permute-start.20 = (f32[8,128]{1,0:T(8,128)S(1)}, f32[8,128]{1,0:T(8,128)S(1)}, u32[]{:S(2)}, u32[]{:S(2)}) collective-permute-start(f32[8,128]{1,0:T(8,128)S(1)} %shard_map.65.r0), channel_id=1, source_target_pairs={{0,32},{32,0},{1,33},{33,1},{2,34},{34,2},{3,35},{35,3},{4,36},{36... | collective-permute-start | bytes 12296 | tf_op jit(solution)/shard_map/ppermute | solution.py:229
  72.2 1.4 %collective-permute-done.19.r1 = f32[8,128]{1,0:T(8,128)S(1)} collective-permute-done((f32[8,128]{1,0:T(8,128)S(1)}, f32[8,128]{1,0:T(8,128)S(1)}, u32[]{:S(2)}, u32[]{:S(2)}) %collective-permute-start.19) | collective-permute-done | bytes 4128 | tf_op jit(solution)/shard_map/ppermute | solution.py:229
  74.7 2.3 %shard_map.67 = (bf16[512,512]{1,0:T(8,128)(2,1)S(1)}, bf16[512,512]{1,0:T(8,128)(2,1)S(1)}) custom-call(f32[1024,1024]{1,0:T(8,128)S(1)} %get-tuple-element.28.m_ref, bf16[1024,512]{1,0:T(8,128)(2,1)S(1)} %get-tuple-element.29.x_ref, f32[8,128]{1,0:T(8,128)S(1)} %get-tuple-element.33.f, f32[8,128]{1,0:T(8,128)S(1)} %get-tuple-element.34.c.c0), custom_call_target="tpu_custom_call" | custom-call | flops 1073741824 | bytes 4194304 | tf_op jit(solution)/shard_map/pallas_call | solution.py:269
  77.1 1.3 %collective-permute-start.25 = (f32[8,128]{1,0:T(8,128)S(1)}, f32[8,128]{1,0:T(8,128)S(1)}, u32[]{:S(2)}, u32[]{:S(2)}) collective-permute-start(f32[8,128]{1,0:T(8,128)S(1)} %get-tuple-element.34.c.c0), channel_id=1, source_target_pairs={{0,20},{4,16},{16,4},{20,0},{1,21},{5,17},{17,5},{21,1},{2,22},{6,... | collective-permute-start | bytes 12296 | tf_op jit(solution)/shard_map/ppermute | solution.py:229
  80.2 1.9 %collective-permute-done.23.c1 = f32[8,128]{1,0:T(8,128)S(1)} collective-permute-done((f32[8,128]{1,0:T(8,128)S(1)}, f32[8,128]{1,0:T(8,128)S(1)}, u32[]{:S(2)}, u32[]{:S(2)}) %collective-permute-start.23) | collective-permute-done | bytes 4128 | tf_op jit(solution)/shard_map/ppermute | solution.py:229
  82.1 2.0 %shard_map.69 = (bf16[256,512]{1,0:T(8,128)(2,1)S(1)}, bf16[256,512]{1,0:T(8,128)(2,1)S(1)}, bf16[256,512]{1,0:T(8,128)(2,1)S(1)}, bf16[256,512]{1,0:T(8,128)(2,1)S(1)}, f32[8,128]{1,0:T(8,128)S(1)}) custom-call(f32[1024,1024]{1,0:T(8,128)S(1)} %get-tuple-element.28.m_ref, bf16[1024,512]{1,0:T(8,128)(2,1)S(1)} %get-tuple-element.23.y_ref, ...), custom_call_target="tpu_custom_call" | custom-call | flops 1073741824 | bytes 4194304 | tf_op jit(solution)/shard_map/pallas_call | solution.py:269
  84.2 1.3 %collective-permute-start.27 = (bf16[256,512]{1,0:T(8,128)(2,1)S(1)}, bf16[256,512]{1,0:T(8,128)(2,1)S(1)}, u32[]{:S(2)}, u32[]{:S(2)}) collective-permute-start(bf16[256,512]{1,0:T(8,128)(2,1)S(1)} %get-tuple-element.40), channel_id=1, source_target_pairs={{0,1},{1,0},{2,3},{3,2},{4,5},{5,4},{6,7},{7,6},{8,9},{9,8},{10,11... | collective-permute-start | bytes 786440 | tf_op jit(solution)/shard_map/ppermute | solution.py:229
  85.5 2.0 %collective-permute-start.28 = (bf16[256,512]{1,0:T(8,128)(2,1)S(1)}, bf16[256,512]{1,0:T(8,128)(2,1)S(1)}, u32[]{:S(2)}, u32[]{:S(2)}) collective-permute-start(bf16[256,512]{1,0:T(8,128)(2,1)S(1)} %get-tuple-element.41), channel_id=1, source_target_pairs={{0,32},{32,0},{1,33},{33,1},{2,34},{34,2},{3,35},{35,3},{4,36},{36... | collective-permute-start | bytes 786440 | tf_op jit(solution)/shard_map/ppermute | solution.py:229
  89.2 2.2 %collective-permute-start.32 = (f32[8,128]{1,0:T(8,128)S(1)}, f32[8,128]{1,0:T(8,128)S(1)}, u32[]{:S(2)}, u32[]{:S(2)}) collective-permute-start(f32[8,128]{1,0:T(8,128)S(1)} %get-tuple-element.43.r0), channel_id=1, source_target_pairs={{0,33},{1,32},{32,1},{33,0},{2,35},{3,34},{34,3},{35,2},{4,37},{5,... | collective-permute-start | bytes 12296 | tf_op jit(solution)/shard_map/ppermute | solution.py:229
  91.3 7.3 %collective-permute-done.32.r3 = f32[8,128]{1,0:T(8,128)S(1)} collective-permute-done((f32[8,128]{1,0:T(8,128)S(1)}, f32[8,128]{1,0:T(8,128)S(1)}, u32[]{:S(2)}, u32[]{:S(2)}) %collective-permute-start.32) | collective-permute-done | bytes 4128 | tf_op jit(solution)/shard_map/ppermute | solution.py:229
  98.6 1.6 %collective-permute-start.31 = (f32[8,128]{1,0:T(8,128)S(1)}, f32[8,128]{1,0:T(8,128)S(1)}, u32[]{:S(2)}, u32[]{:S(2)}) collective-permute-start(f32[8,128]{1,0:T(8,128)S(1)} %get-tuple-element.43.r0), channel_id=1, source_target_pairs={{0,32},{32,0},{1,33},{33,1},{2,34},{34,2},{3,35},{35,3},{4,36},{36... | collective-permute-start | bytes 12296 | tf_op jit(solution)/shard_map/ppermute | solution.py:229
  100.2 2.0 %collective-permute-done.31.r2 = f32[8,128]{1,0:T(8,128)S(1)} collective-permute-done((f32[8,128]{1,0:T(8,128)S(1)}, f32[8,128]{1,0:T(8,128)S(1)}, u32[]{:S(2)}, u32[]{:S(2)}) %collective-permute-start.31) | collective-permute-done | bytes 4128 | tf_op jit(solution)/shard_map/ppermute | solution.py:229
  102.2 1.5 %collective-permute-start.30 = (f32[8,128]{1,0:T(8,128)S(1)}, f32[8,128]{1,0:T(8,128)S(1)}, u32[]{:S(2)}, u32[]{:S(2)}) collective-permute-start(f32[8,128]{1,0:T(8,128)S(1)} %get-tuple-element.43.r0), channel_id=1, source_target_pairs={{0,1},{1,0},{2,3},{3,2},{4,5},{5,4},{6,7},{7,6},{8,9},{9,8},{10,11... | collective-permute-start | bytes 12296 | tf_op jit(solution)/shard_map/ppermute | solution.py:229
  103.7 2.1 %collective-permute-done.30.r1 = f32[8,128]{1,0:T(8,128)S(1)} collective-permute-done((f32[8,128]{1,0:T(8,128)S(1)}, f32[8,128]{1,0:T(8,128)S(1)}, u32[]{:S(2)}, u32[]{:S(2)}) %collective-permute-start.30) | collective-permute-done | bytes 4128 | tf_op jit(solution)/shard_map/ppermute | solution.py:229
  106.4 14.1 %all_to_all.11.back_ref = bf16[8,64,512]{2,1,0:T(8,128)(2,1)S(1)} all-to-all(bf16[8,64,512]{2,1,0:T(8,128)(2,1)S(1)} %shard_map.70), channel_id=1, replica_groups={{0,3,12,15,96,99,108,111},{1,2,13,14,97,98,109,110},{4,7,8,11,100,103,1..., dimensions={0} | all-to-all | bytes 1048576 | tf_op jit(solution)/shard_map/all_to_all | solution.py:250
  (56 shorter events, 20.4 us)
Async XLA Ops:
  26.1 6.6 %collective-permute-start.2 = (bf16[256,512]{1,0:T(8,128)(2,1)S(1)}, bf16[256,512]{1,0:T(8,128)(2,1)S(1)}, u32[]{:S(2)}, u32[]{:S(2)}) collective-permute-start(bf16[256,512]{1,0:T(8,128)(2,1)S(1)} %bitcast.4), channel_id=1, source_target_pairs={{0,4},{4,0},{1,5},{5,1},{2,6},{6,2},{3,7},{7,3},{8,12},{12,8},{9,1... | collective-permute-start | bytes 786440 | tf_op jit(solution)/shard_map/ppermute | solution.py:229
  26.2 6.6 %collective-permute-start.1 = (bf16[256,512]{1,0:T(8,128)(2,1)S(1)}, bf16[256,512]{1,0:T(8,128)(2,1)S(1)}, u32[]{:S(2)}, u32[]{:S(2)}) collective-permute-start(bf16[256,512]{1,0:T(8,128)(2,1)S(1)} %bitcast.7), channel_id=1, source_target_pairs={{0,32},{32,0},{1,33},{33,1},{2,34},{34,2},{3,35},{35,3},{4,36},{36... | collective-permute-start | bytes 786440 | tf_op jit(solution)/shard_map/ppermute | solution.py:229
  26.2 6.6 %collective-permute-start = (bf16[256,512]{1,0:T(8,128)(2,1)S(1)}, bf16[256,512]{1,0:T(8,128)(2,1)S(1)}, u32[]{:S(2)}, u32[]{:S(2)}) collective-permute-start(bf16[256,512]{1,0:T(8,128)(2,1)S(1)} %bitcast.8), channel_id=1, source_target_pairs={{0,1},{1,0},{2,3},{3,2},{4,5},{5,4},{6,7},{7,6},{8,9},{9,8},{10,11... | collective-permute-start | bytes 786440 | tf_op jit(solution)/shard_map/ppermute | solution.py:229
  26.3 8.4 %collective-permute-start.3 = (bf16[256,512]{1,0:T(8,128)(2,1)S(1)}, bf16[256,512]{1,0:T(8,128)(2,1)S(1)}, u32[]{:S(2)}, u32[]{:S(2)}) collective-permute-start(bf16[256,512]{1,0:T(8,128)(2,1)S(1)} %bitcast.5), channel_id=1, source_target_pairs={{0,16},{16,0},{1,17},{17,1},{2,18},{18,2},{3,19},{19,3},{4,20},{20... | collective-permute-start | bytes 786440 | tf_op jit(solution)/shard_map/ppermute | solution.py:229
  32.7 2.0 %collective-permute-start.4 = (bf16[256,512]{1,0:T(8,128)(2,1)S(1)}, bf16[256,512]{1,0:T(8,128)(2,1)S(1)}, u32[]{:S(2)}, u32[]{:S(2)}) collective-permute-start(bf16[256,512]{1,0:T(8,128)(2,1)S(1)} %collective-permute-done.2.t1), channel_id=1, source_target_pairs={{0,16},{16,0},{1,17},{17,1},{2,18},{18,2},{3,19},{19,3},{4,20},{20... | collective-permute-start | bytes 786440 | tf_op jit(solution)/shard_map/ppermute | solution.py:229
  32.8 5.9 %collective-permute-start.5 = (bf16[128,512]{1,0:T(8,128)(2,1)S(1)}, bf16[128,512]{1,0:T(8,128)(2,1)S(1)}, u32[]{:S(2)}, u32[]{:S(2)}) collective-permute-start(bf16[128,512]{1,0:T(8,128)(2,1)S(1)} %slice.18), channel_id=1, source_target_pairs={{0,1},{1,0},{2,3},{3,2},{4,5},{5,4},{6,7},{7,6},{8,9},{9,8},{10,11... | collective-permute-start | bytes 393224 | tf_op jit(solution)/shard_map/ppermute | solution.py:229
  32.9 5.9 %collective-permute-start.6 = (bf16[128,512]{1,0:T(8,128)(2,1)S(1)}, bf16[128,512]{1,0:T(8,128)(2,1)S(1)}, u32[]{:S(2)}, u32[]{:S(2)}) collective-permute-start(bf16[128,512]{1,0:T(8,128)(2,1)S(1)} %slice.19), channel_id=1, source_target_pairs={{0,32},{32,0},{1,33},{33,1},{2,34},{34,2},{3,35},{35,3},{4,36},{36... | collective-permute-start | bytes 393224 | tf_op jit(solution)/shard_map/ppermute | solution.py:229
  40.0 4.6 %collective-permute-start.9 = (f32[8,128]{1,0:T(8,128)S(1)}, f32[8,128]{1,0:T(8,128)S(1)}, u32[]{:S(2)}, u32[]{:S(2)}) collective-permute-start(f32[8,128]{1,0:T(8,128)S(1)} %get-tuple-element.30.r0), channel_id=1, source_target_pairs={{0,33},{1,32},{32,1},{33,0},{2,35},{3,34},{34,3},{35,2},{4,37},{5,... | collective-permute-start | bytes 12296 | tf_op jit(solution)/shard_map/ppermute | solution.py:229
  41.5 3.6 %collective-permute-start.8 = (f32[8,128]{1,0:T(8,128)S(1)}, f32[8,128]{1,0:T(8,128)S(1)}, u32[]{:S(2)}, u32[]{:S(2)}) collective-permute-start(f32[8,128]{1,0:T(8,128)S(1)} %get-tuple-element.30.r0), channel_id=1, source_target_pairs={{0,32},{32,0},{1,33},{33,1},{2,34},{34,2},{3,35},{35,3},{4,36},{36... | collective-permute-start | bytes 12296 | tf_op jit(solution)/shard_map/ppermute | solution.py:229
  43.2 3.6 %collective-permute-start.7 = (f32[8,128]{1,0:T(8,128)S(1)}, f32[8,128]{1,0:T(8,128)S(1)}, u32[]{:S(2)}, u32[]{:S(2)}) collective-permute-start(f32[8,128]{1,0:T(8,128)S(1)} %get-tuple-element.30.r0), channel_id=1, source_target_pairs={{0,1},{1,0},{2,3},{3,2},{4,5},{5,4},{6,7},{7,6},{8,9},{9,8},{10,11... | collective-permute-start | bytes 12296 | tf_op jit(solution)/shard_map/ppermute | solution.py:229
  48.0 3.1 %collective-permute-start.12 = (f32[8,128]{1,0:T(8,128)S(1)}, f32[8,128]{1,0:T(8,128)S(1)}, u32[]{:S(2)}, u32[]{:S(2)}) collective-permute-start(f32[8,128]{1,0:T(8,128)S(1)} %get-tuple-element.31.c0), channel_id=1, source_target_pairs={{0,20},{4,16},{16,4},{20,0},{1,21},{5,17},{17,5},{21,1},{2,22},{6,... | collective-permute-start | bytes 12296 | tf_op jit(solution)/shard_map/ppermute | solution.py:229
  48.1 3.0 %collective-permute-start.11 = (f32[8,128]{1,0:T(8,128)S(1)}, f32[8,128]{1,0:T(8,128)S(1)}, u32[]{:S(2)}, u32[]{:S(2)}) collective-permute-start(f32[8,128]{1,0:T(8,128)S(1)} %get-tuple-element.31.c0), channel_id=1, source_target_pairs={{0,16},{16,0},{1,17},{17,1},{2,18},{18,2},{3,19},{19,3},{4,20},{20... | collective-permute-start | bytes 12296 | tf_op jit(solution)/shard_map/ppermute | solution.py:229
  49.4 3.6 %collective-permute-start.10 = (f32[8,128]{1,0:T(8,128)S(1)}, f32[8,128]{1,0:T(8,128)S(1)}, u32[]{:S(2)}, u32[]{:S(2)}) collective-permute-start(f32[8,128]{1,0:T(8,128)S(1)} %get-tuple-element.31.c0), channel_id=1, source_target_pairs={{0,4},{4,0},{1,5},{5,1},{2,6},{6,2},{3,7},{7,3},{8,12},{12,8},{9,1... | collective-permute-start | bytes 12296 | tf_op jit(solution)/shard_map/ppermute | solution.py:229
  54.2 4.6 %collective-permute-start.15 = (f32[8,128]{1,0:T(8,128)S(1)}, f32[8,128]{1,0:T(8,128)S(1)}, u32[]{:S(2)}, u32[]{:S(2)}) collective-permute-start(f32[8,128]{1,0:T(8,128)S(1)} %shard_map.63.r0), channel_id=1, source_target_pairs={{0,33},{1,32},{32,1},{33,0},{2,35},{3,34},{34,3},{35,2},{4,37},{5,... | collective-permute-start | bytes 12296 | tf_op jit(solution)/shard_map/ppermute | solution.py:229
  57.0 3.6 %collective-permute-start.14 = (f32[8,128]{1,0:T(8,128)S(1)}, f32[8,128]{1,0:T(8,128)S(1)}, u32[]{:S(2)}, u32[]{:S(2)}) collective-permute-start(f32[8,128]{1,0:T(8,128)S(1)} %shard_map.63.r0), channel_id=1, source_target_pairs={{0,32},{32,0},{1,33},{33,1},{2,34},{34,2},{3,35},{35,3},{4,36},{36... | collective-permute-start | bytes 12296 | tf_op jit(solution)/shard_map/ppermute | solution.py:229
  57.0 3.6 %collective-permute-start.13 = (f32[8,128]{1,0:T(8,128)S(1)}, f32[8,128]{1,0:T(8,128)S(1)}, u32[]{:S(2)}, u32[]{:S(2)}) collective-permute-start(f32[8,128]{1,0:T(8,128)S(1)} %shard_map.63.r0), channel_id=1, source_target_pairs={{0,1},{1,0},{2,3},{3,2},{4,5},{5,4},{6,7},{7,6},{8,9},{9,8},{10,11... | collective-permute-start | bytes 12296 | tf_op jit(solution)/shard_map/ppermute | solution.py:229
  61.8 3.1 %collective-permute-start.18 = (f32[8,128]{1,0:T(8,128)S(1)}, f32[8,128]{1,0:T(8,128)S(1)}, u32[]{:S(2)}, u32[]{:S(2)}) collective-permute-start(f32[8,128]{1,0:T(8,128)S(1)} %get-tuple-element.32.c0), channel_id=1, source_target_pairs={{0,20},{4,16},{16,4},{20,0},{1,21},{5,17},{17,5},{21,1},{2,22},{6,... | collective-permute-start | bytes 12296 | tf_op jit(solution)/shard_map/ppermute | solution.py:229
  61.9 3.0 %collective-permute-start.17 = (f32[8,128]{1,0:T(8,128)S(1)}, f32[8,128]{1,0:T(8,128)S(1)}, u32[]{:S(2)}, u32[]{:S(2)}) collective-permute-start(f32[8,128]{1,0:T(8,128)S(1)} %get-tuple-element.32.c0), channel_id=1, source_target_pairs={{0,16},{16,0},{1,17},{17,1},{2,18},{18,2},{3,19},{19,3},{4,20},{20... | collective-permute-start | bytes 12296 | tf_op jit(solution)/shard_map/ppermute | solution.py:229
  62.1 3.8 %collective-permute-start.16 = (f32[8,128]{1,0:T(8,128)S(1)}, f32[8,128]{1,0:T(8,128)S(1)}, u32[]{:S(2)}, u32[]{:S(2)}) collective-permute-start(f32[8,128]{1,0:T(8,128)S(1)} %get-tuple-element.32.c0), channel_id=1, source_target_pairs={{0,4},{4,0},{1,5},{5,1},{2,6},{6,2},{3,7},{7,3},{8,12},{12,8},{9,1... | collective-permute-start | bytes 12296 | tf_op jit(solution)/shard_map/ppermute | solution.py:229
  67.1 4.6 %collective-permute-start.21 = (f32[8,128]{1,0:T(8,128)S(1)}, f32[8,128]{1,0:T(8,128)S(1)}, u32[]{:S(2)}, u32[]{:S(2)}) collective-permute-start(f32[8,128]{1,0:T(8,128)S(1)} %shard_map.65.r0), channel_id=1, source_target_pairs={{0,33},{1,32},{32,1},{33,0},{2,35},{3,34},{34,3},{35,2},{4,37},{5,... | collective-permute-start | bytes 12296 | tf_op jit(solution)/shard_map/ppermute | solution.py:229
  68.6 3.6 %collective-permute-start.20 = (f32[8,128]{1,0:T(8,128)S(1)}, f32[8,128]{1,0:T(8,128)S(1)}, u32[]{:S(2)}, u32[]{:S(2)}) collective-permute-start(f32[8,128]{1,0:T(8,128)S(1)} %shard_map.65.r0), channel_id=1, source_target_pairs={{0,32},{32,0},{1,33},{33,1},{2,34},{34,2},{3,35},{35,3},{4,36},{36... | collective-permute-start | bytes 12296 | tf_op jit(solution)/shard_map/ppermute | solution.py:229
  70.0 3.6 %collective-permute-start.19 = (f32[8,128]{1,0:T(8,128)S(1)}, f32[8,128]{1,0:T(8,128)S(1)}, u32[]{:S(2)}, u32[]{:S(2)}) collective-permute-start(f32[8,128]{1,0:T(8,128)S(1)} %shard_map.65.r0), channel_id=1, source_target_pairs={{0,1},{1,0},{2,3},{3,2},{4,5},{5,4},{6,7},{7,6},{8,9},{9,8},{10,11... | collective-permute-start | bytes 12296 | tf_op jit(solution)/shard_map/ppermute | solution.py:229
  77.0 10.7 %collective-permute-start.22 = (bf16[512,512]{1,0:T(8,128)(2,1)S(1)}, bf16[512,512]{1,0:T(8,128)(2,1)S(1)}, u32[]{:S(2)}, u32[]{:S(2)}) collective-permute-start(bf16[512,512]{1,0:T(8,128)(2,1)S(1)} %get-tuple-element.36), channel_id=1, source_target_pairs={{0,16},{16,0},{1,17},{17,1},{2,18},{18,2},{3,19},{19,3},{4,20},{20... | collective-permute-start | bytes 1572872 | tf_op jit(solution)/shard_map/ppermute | solution.py:229
  77.1 3.1 %collective-permute-start.25 = (f32[8,128]{1,0:T(8,128)S(1)}, f32[8,128]{1,0:T(8,128)S(1)}, u32[]{:S(2)}, u32[]{:S(2)}) collective-permute-start(f32[8,128]{1,0:T(8,128)S(1)} %get-tuple-element.34.c.c0), channel_id=1, source_target_pairs={{0,20},{4,16},{16,4},{20,0},{1,21},{5,17},{17,5},{21,1},{2,22},{6,... | collective-permute-start | bytes 12296 | tf_op jit(solution)/shard_map/ppermute | solution.py:229
  78.5 3.6 %collective-permute-start.23 = (f32[8,128]{1,0:T(8,128)S(1)}, f32[8,128]{1,0:T(8,128)S(1)}, u32[]{:S(2)}, u32[]{:S(2)}) collective-permute-start(f32[8,128]{1,0:T(8,128)S(1)} %get-tuple-element.34.c.c0), channel_id=1, source_target_pairs={{0,4},{4,0},{1,5},{5,1},{2,6},{6,2},{3,7},{7,3},{8,12},{12,8},{9,1... | collective-permute-start | bytes 12296 | tf_op jit(solution)/shard_map/ppermute | solution.py:229
  84.2 21.7 %collective-permute-start.27 = (bf16[256,512]{1,0:T(8,128)(2,1)S(1)}, bf16[256,512]{1,0:T(8,128)(2,1)S(1)}, u32[]{:S(2)}, u32[]{:S(2)}) collective-permute-start(bf16[256,512]{1,0:T(8,128)(2,1)S(1)} %get-tuple-element.40), channel_id=1, source_target_pairs={{0,1},{1,0},{2,3},{3,2},{4,5},{5,4},{6,7},{7,6},{8,9},{9,8},{10,11... | collective-permute-start | bytes 786440 | tf_op jit(solution)/shard_map/ppermute | solution.py:229
  85.5 20.3 %collective-permute-start.28 = (bf16[256,512]{1,0:T(8,128)(2,1)S(1)}, bf16[256,512]{1,0:T(8,128)(2,1)S(1)}, u32[]{:S(2)}, u32[]{:S(2)}) collective-permute-start(bf16[256,512]{1,0:T(8,128)(2,1)S(1)} %get-tuple-element.41), channel_id=1, source_target_pairs={{0,32},{32,0},{1,33},{33,1},{2,34},{34,2},{3,35},{35,3},{4,36},{36... | collective-permute-start | bytes 786440 | tf_op jit(solution)/shard_map/ppermute | solution.py:229
  87.5 18.3 %collective-permute-start.29 = (bf16[256,512]{1,0:T(8,128)(2,1)S(1)}, bf16[256,512]{1,0:T(8,128)(2,1)S(1)}, u32[]{:S(2)}, u32[]{:S(2)}) collective-permute-start(bf16[256,512]{1,0:T(8,128)(2,1)S(1)} %get-tuple-element.42), channel_id=1, source_target_pairs={{0,33},{1,32},{32,1},{33,0},{2,35},{3,34},{34,3},{35,2},{4,37},{5,... | collective-permute-start | bytes 786440 | tf_op jit(solution)/shard_map/ppermute | solution.py:229
  88.2 17.6 %collective-permute-start.26 = (bf16[256,512]{1,0:T(8,128)(2,1)S(1)}, bf16[256,512]{1,0:T(8,128)(2,1)S(1)}, u32[]{:S(2)}, u32[]{:S(2)}) collective-permute-start(bf16[256,512]{1,0:T(8,128)(2,1)S(1)} %get-tuple-element.38), channel_id=1, source_target_pairs={{0,4},{4,0},{1,5},{5,1},{2,6},{6,2},{3,7},{7,3},{8,12},{12,8},{9,1... | collective-permute-start | bytes 786440 | tf_op jit(solution)/shard_map/ppermute | solution.py:229
  89.2 9.4 %collective-permute-start.32 = (f32[8,128]{1,0:T(8,128)S(1)}, f32[8,128]{1,0:T(8,128)S(1)}, u32[]{:S(2)}, u32[]{:S(2)}) collective-permute-start(f32[8,128]{1,0:T(8,128)S(1)} %get-tuple-element.43.r0), channel_id=1, source_target_pairs={{0,33},{1,32},{32,1},{33,0},{2,35},{3,34},{34,3},{35,2},{4,37},{5,... | collective-permute-start | bytes 12296 | tf_op jit(solution)/shard_map/ppermute | solution.py:229
  98.6 3.6 %collective-permute-start.31 = (f32[8,128]{1,0:T(8,128)S(1)}, f32[8,128]{1,0:T(8,128)S(1)}, u32[]{:S(2)}, u32[]{:S(2)}) collective-permute-start(f32[8,128]{1,0:T(8,128)S(1)} %get-tuple-element.43.r0), channel_id=1, source_target_pairs={{0,32},{32,0},{1,33},{33,1},{2,34},{34,2},{3,35},{35,3},{4,36},{36... | collective-permute-start | bytes 12296 | tf_op jit(solution)/shard_map/ppermute | solution.py:229
  102.2 3.6 %collective-permute-start.30 = (f32[8,128]{1,0:T(8,128)S(1)}, f32[8,128]{1,0:T(8,128)S(1)}, u32[]{:S(2)}, u32[]{:S(2)}) collective-permute-start(f32[8,128]{1,0:T(8,128)S(1)} %get-tuple-element.43.r0), channel_id=1, source_target_pairs={{0,1},{1,0},{2,3},{3,2},{4,5},{5,4},{6,7},{7,6},{8,9},{9,8},{10,11... | collective-permute-start | bytes 12296 | tf_op jit(solution)/shard_map/ppermute | solution.py:229
  (3 other events, 88.8 us)

commit v2 on v1

--- a/solution.py
+++ b/solution.py
@@ -19,6 +19,7 @@
 VMEM_LIMIT = 24 * 1024 * 1024
 LANES = 128
 STEP = 128
+SPLIT = ((3,), (1, 2, 0))
 
 
 def compact(column):
@@ -178,18 +179,18 @@
         ).astype(jnp.bfloat16)
 
 
-def source_kernel(log_mass, m_ref, y_ref, c0, c1, c2, c3, p0, p1, p2, p3, lse_ref, row_ref):
+def source_kernel(log_mass, blocks, m_ref, y_ref, c0, c1, c2, c3, *refs):
+    *pieces, lse_ref, row_ref = refs
     put_row(row_ref, log_mass - combine(aligned([c0[...], c1[...], c2[...], c3[...]])))
-    rows = p0.shape[0]
-    for a in range(0, m_ref.shape[0], STEP):
+    rows = pieces[0].shape[0]
+    for place, a in enumerate(a for q in blocks for a in range(q * rows, (q + 1) * rows, STEP)):
         scores = m_ref[a : a + STEP, :] + row_ref[...]
         highest = jnp.max(scores, axis=1, keepdims=True)
         raised = jnp.exp2(scores - highest)
         total = jnp.sum(raised, axis=1, keepdims=True)
         mapped = jnp.dot(raised.astype(jnp.bfloat16), y_ref[...], preferred_element_type=jnp.float32)
-        out_ref, b = (p0, p1, p2, p3)[a // rows], a % rows
-        out_ref[b : b + STEP, :] = (mapped / total).astype(jnp.bfloat16)
-        lse_ref[a // LANES : a // LANES + 1, :] = compact(highest + jnp.log2(total))
+        pieces[place * STEP // rows][a % rows : a % rows + STEP, :] = (mapped / total).astype(jnp.bfloat16)
+        lse_ref[place : place + 1, :] = compact(highest + jnp.log2(total))
 
 
 def join_kernel(p_ref, near_ref, c0, c1, c2, c3, out_ref, far_ref, own_ref, mate_ref):
@@ -359,14 +360,23 @@
         area,
     )
     near = swap(target_far, "core")
-    own_piece, piece_1, piece_2, piece_3, row_part = call(
-        functools.partial(source_kernel, log_mass),
-        [out((rows, width), bf16)] * 4 + [out(tile, f32)],
-        [line(side)],
-        [matrix, all_targets] + column_parts,
-        flops,
-        area,
-    )
+    made = {}
+    lines = []
+    for blocks in SPLIT:
+        results = call(
+            functools.partial(source_kernel, log_mass, blocks),
+            [out((rows, width), bf16)] * len(blocks) + [out((tile[0] * len(blocks) // 4, LANES), f32)],
+            [line(side)],
+            [matrix, all_targets] + column_parts,
+            flops * len(blocks) // 4,
+            area * len(blocks) // 4,
+        )
+        made.update(zip(blocks, results))
+        lines.append(results[-1])
+    own_piece, piece_1, piece_2, piece_3 = [made[q] for q in range(4)]
+    order = [q for blocks in SPLIT for q in blocks]
+    joint = jnp.concatenate(lines, axis=0).reshape(4, -1, LANES)
+    row_part = jnp.concatenate([joint[order.index(q)] for q in range(4)], axis=0)
     source_pieces = [own_piece, swap(piece_1, "yl"), swap(piece_2, "xl"), swap(piece_3, ("xl", "yl"), ACROSS)]
     row_parts = exchange(row_part, "xl", "yl")
     joined_own, joined_far = call(

time: 122 us -> 120 us (0.984)
    ppermute x33, waiting for transfers between devices: 35.6 us -> 34.4 us  [swap(): return lax.ppermute(value, axis, pairs)]
    pallas_call x13 -> x14, Pallas kernels: 18.4 us -> 18.6 us  [call(): pl.pallas_call(kernel, out_shape=outs, in_specs=[spec] * len(args), out_s...]
where the time goes in v2:
time: 120 us
  blocking collectives  37.2 us (31%)
  waiting for transfers between devices  34.4 us (29%)
  starting transfers between devices  28.8 us (24%)
  Pallas kernels  18.6 us (16%)
    all_to_all x2, blocking collectives, across(): lax.all_to_all(value, AXES, split_axis=0, concat_axis=0, axis_index_group...  37.2 us
    ppermute x33, waiting for transfers between devices, swap(): return lax.ppermute(value, axis, pairs)  34.4 us
    ppermute x33, starting transfers between devices, swap(): return lax.ppermute(value, axis, pairs)  28.8 us
    pallas_call x14, Pallas kernels, call(): pl.pallas_call(kernel, out_shape=outs, in_specs=[spec] * len(args), out_s...  18.6 us
  transfers between devices with their start and end apart: 33, of which 21 were waited for; matrix products, arithmetic and copies ran while one was open for 0% of the time, Pallas kernels for 4%

profile of v2, /device:TPU:0, one launch (start us, length us, event | category | flops | bytes accessed | tf_op | source)
XLA Modules:
  0.0 120.0 jit_solution(15817437262585925764)
XLA Ops:
  0.6 2.3 %shard_map.59 = bf16[8,64,512]{2,1,0:T(8,128)(2,1)} custom-call(s32[1,256]{1,0:T(1,128)} %bitcast.10, bf16[256,512]{1,0:T(8,128)(2,1)} %s_hbm.1, s32[1,256]{1,0:T(1,128)} %bitcast.12, bf16[256,512]{1,0:T(8,128)(2,1)} %t_hbm.1), custom_call_target="tpu_custom_call" | custom-call | bytes 4194304 | tf_op jit(solution)/shard_map/pallas_call | solution.py:270
  2.9 23.1 %all_to_all.10 = bf16[8,64,512]{2,1,0:T(8,128)(2,1)S(1)} all-to-all(bf16[8,64,512]{2,1,0:T(8,128)(2,1)} %shard_map.59), channel_id=1, replica_groups={{0,3,12,15,96,99,108,111},{1,2,13,14,97,98,109,110},{4,7,8,11,100,103,1..., dimensions={0} | all-to-all | bytes 1048576 | tf_op jit(solution)/shard_map/all_to_all | solution.py:251
  26.5 6.3 %collective-permute-done.2.t1 = bf16[256,512]{1,0:T(8,128)(2,1)S(1)} collective-permute-done((bf16[256,512]{1,0:T(8,128)(2,1)S(1)}, bf16[256,512]{1,0:T(8,128)(2,1)S(1)}, u32[]{:S(2)}, u32[]{:S(2)}) %collective-permute-start.2) | collective-permute-done | bytes 262176 | tf_op jit(solution)/shard_map/ppermute | solution.py:230
  32.9 1.8 %collective-permute-start.6 = (bf16[128,512]{1,0:T(8,128)(2,1)S(1)}, bf16[128,512]{1,0:T(8,128)(2,1)S(1)}, u32[]{:S(2)}, u32[]{:S(2)}) collective-permute-start(bf16[128,512]{1,0:T(8,128)(2,1)S(1)} %slice.37), channel_id=1, source_target_pairs={{0,32},{32,0},{1,33},{33,1},{2,34},{34,2},{3,35},{35,3},{4,36},{36... | collective-permute-start | bytes 393224 | tf_op jit(solution)/shard_map/ppermute | solution.py:230
  34.8 2.6 %shard_map.60 = (f32[1024,1024]{1,0:T(8,128)S(1)}, bf16[1024,512]{1,0:T(8,128)(2,1)S(1)}, bf16[1024,512]{1,0:T(8,128)(2,1)S(1)}, f32[8,128]{1,0:T(8,128)S(1)}, f32[1,1024]{1,0:T(1,128)S(1)}) custom-call(bf16[256,512]{1,0:T(8,128)(2,1)S(1)} %bitcast.9, bf16[256,512]{1,0:T(8,128)(2,1)S(1)} %collective-permute-done.s1, ...), custom_call_target="tpu_custom_call" | custom-call | flops 805306368 | bytes 4194304 | tf_op jit(solution)/shard_map/pallas_call | solution.py:270
  37.3 1.4 %collective-permute-done.5.sa = bf16[128,512]{1,0:T(8,128)(2,1)S(1)} collective-permute-done((bf16[128,512]{1,0:T(8,128)(2,1)S(1)}, bf16[128,512]{1,0:T(8,128)(2,1)S(1)}, u32[]{:S(2)}, u32[]{:S(2)}) %collective-permute-start.5) | collective-permute-done | bytes 131104 | tf_op jit(solution)/shard_map/ppermute | solution.py:230
  40.0 1.5 %collective-permute-start.9 = (f32[8,128]{1,0:T(8,128)S(1)}, f32[8,128]{1,0:T(8,128)S(1)}, u32[]{:S(2)}, u32[]{:S(2)}) collective-permute-start(f32[8,128]{1,0:T(8,128)S(1)} %get-tuple-element.31.r0), channel_id=1, source_target_pairs={{0,33},{1,32},{32,1},{33,0},{2,35},{3,34},{34,3},{35,2},{4,37},{5,... | collective-permute-start | bytes 12296 | tf_op jit(solution)/shard_map/ppermute | solution.py:230
  41.5 1.7 %collective-permute-start.8 = (f32[8,128]{1,0:T(8,128)S(1)}, f32[8,128]{1,0:T(8,128)S(1)}, u32[]{:S(2)}, u32[]{:S(2)}) collective-permute-start(f32[8,128]{1,0:T(8,128)S(1)} %get-tuple-element.31.r0), channel_id=1, source_target_pairs={{0,32},{32,0},{1,33},{33,1},{2,34},{34,2},{3,35},{35,3},{4,36},{36... | collective-permute-start | bytes 12296 | tf_op jit(solution)/shard_map/ppermute | solution.py:230
  45.1 1.7 %collective-permute-done.7.r1 = f32[8,128]{1,0:T(8,128)S(1)} collective-permute-done((f32[8,128]{1,0:T(8,128)S(1)}, f32[8,128]{1,0:T(8,128)S(1)}, u32[]{:S(2)}, u32[]{:S(2)}) %collective-permute-start.7) | collective-permute-done | bytes 4128 | tf_op jit(solution)/shard_map/ppermute | solution.py:230
  46.8 1.2 shard_map.62
  48.1 1.3 %collective-permute-start.11 = (f32[8,128]{1,0:T(8,128)S(1)}, f32[8,128]{1,0:T(8,128)S(1)}, u32[]{:S(2)}, u32[]{:S(2)}) collective-permute-start(f32[8,128]{1,0:T(8,128)S(1)} %get-tuple-element.32.c0), channel_id=1, source_target_pairs={{0,16},{16,0},{1,17},{17,1},{2,18},{18,2},{3,19},{19,3},{4,20},{20... | collective-permute-start | bytes 12296 | tf_op jit(solution)/shard_map/ppermute | solution.py:230
  51.1 1.9 %collective-permute-done.10.c1 = f32[8,128]{1,0:T(8,128)S(1)} collective-permute-done((f32[8,128]{1,0:T(8,128)S(1)}, f32[8,128]{1,0:T(8,128)S(1)}, u32[]{:S(2)}, u32[]{:S(2)}) %collective-permute-start.10) | collective-permute-done | bytes 4128 | tf_op jit(solution)/shard_map/ppermute | solution.py:230
  53.0 1.2 %shard_map.63.r0 = f32[8,128]{1,0:T(8,128)S(1)} custom-call(f32[1024,1024]{1,0:T(8,128)S(1)} %get-tuple-element.29.m_ref, f32[8,128]{1,0:T(8,128)S(1)} %get-tuple-element.32.c0, f32[8,128]{1,0:T(8,128)S(1)} %collective-permute-done.10.c1, f32[8,128]{1,0:T(8,128)S(1)} %collective-permute-done.11.c2, f32[8,128]{1,0:T(8,128)S(1)} %collective-permute-done.12.c3), custom_call_target="tpu_custom_call" | custom-call | bytes 4194304 | tf_op jit(solution)/shard_map/pallas_call | solution.py:270
  54.2 2.8 %collective-permute-start.15 = (f32[8,128]{1,0:T(8,128)S(1)}, f32[8,128]{1,0:T(8,128)S(1)}, u32[]{:S(2)}, u32[]{:S(2)}) collective-permute-start(f32[8,128]{1,0:T(8,128)S(1)} %shard_map.63.r0), channel_id=1, source_target_pairs={{0,33},{1,32},{32,1},{33,0},{2,35},{3,34},{34,3},{35,2},{4,37},{5,... | collective-permute-start | bytes 12296 | tf_op jit(solution)/shard_map/ppermute | solution.py:230
  58.8 1.8 %collective-permute-done.14.r2 = f32[8,128]{1,0:T(8,128)S(1)} collective-permute-done((f32[8,128]{1,0:T(8,128)S(1)}, f32[8,128]{1,0:T(8,128)S(1)}, u32[]{:S(2)}, u32[]{:S(2)}) %collective-permute-start.14) | collective-permute-done | bytes 4128 | tf_op jit(solution)/shard_map/ppermute | solution.py:230
  62.1 2.0 %collective-permute-start.16 = (f32[8,128]{1,0:T(8,128)S(1)}, f32[8,128]{1,0:T(8,128)S(1)}, u32[]{:S(2)}, u32[]{:S(2)}) collective-permute-start(f32[8,128]{1,0:T(8,128)S(1)} %get-tuple-element.33.c0), channel_id=1, source_target_pairs={{0,4},{4,0},{1,5},{5,1},{2,6},{6,2},{3,7},{7,3},{8,12},{12,8},{9,1... | collective-permute-start | bytes 12296 | tf_op jit(solution)/shard_map/ppermute | solution.py:230
  65.9 1.2 %shard_map.65.r0 = f32[8,128]{1,0:T(8,128)S(1)} custom-call(f32[1024,1024]{1,0:T(8,128)S(1)} %get-tuple-element.29.m_ref, f32[8,128]{1,0:T(8,128)S(1)} %get-tuple-element.33.c0, f32[8,128]{1,0:T(8,128)S(1)} %collective-permute-done.16.c1, f32[8,128]{1,0:T(8,128)S(1)} %collective-permute-done.17.c2, f32[8,128]{1,0:T(8,128)S(1)} %collective-permute-done.18.c3), custom_call_target="tpu_custom_call" | custom-call | bytes 4194304 | tf_op jit(solution)/shard_map/pallas_call | solution.py:270
  67.1 1.5 %collective-permute-start.21 = (f32[8,128]{1,0:T(8,128)S(1)}, f32[8,128]{1,0:T(8,128)S(1)}, u32[]{:S(2)}, u32[]{:S(2)}) collective-permute-start(f32[8,128]{1,0:T(8,128)S(1)} %shard_map.65.r0), channel_id=1, source_target_pairs={{0,33},{1,32},{32,1},{33,0},{2,35},{3,34},{34,3},{35,2},{4,37},{5,... | collective-permute-start | bytes 12296 | tf_op jit(solution)/shard_map/ppermute | solution.py:230
  68.6 1.4 %collective-permute-start.20 = (f32[8,128]{1,0:T(8,128)S(1)}, f32[8,128]{1,0:T(8,128)S(1)}, u32[]{:S(2)}, u32[]{:S(2)}) collective-permute-start(f32[8,128]{1,0:T(8,128)S(1)} %shard_map.65.r0), channel_id=1, source_target_pairs={{0,32},{32,0},{1,33},{33,1},{2,34},{34,2},{3,35},{35,3},{4,36},{36... | collective-permute-start | bytes 12296 | tf_op jit(solution)/shard_map/ppermute | solution.py:230
  72.2 1.4 %collective-permute-done.19.r1 = f32[8,128]{1,0:T(8,128)S(1)} collective-permute-done((f32[8,128]{1,0:T(8,128)S(1)}, f32[8,128]{1,0:T(8,128)S(1)}, u32[]{:S(2)}, u32[]{:S(2)}) %collective-permute-start.19) | collective-permute-done | bytes 4128 | tf_op jit(solution)/shard_map/ppermute | solution.py:230
  74.8 2.3 %shard_map.67 = (bf16[512,512]{1,0:T(8,128)(2,1)S(1)}, bf16[512,512]{1,0:T(8,128)(2,1)S(1)}) custom-call(f32[1024,1024]{1,0:T(8,128)S(1)} %get-tuple-element.29.m_ref, bf16[1024,512]{1,0:T(8,128)(2,1)S(1)} %get-tuple-element.30.x_ref, f32[8,128]{1,0:T(8,128)S(1)} %get-tuple-element.34.f, f32[8,128]{1,0:T(8,128)S(1)} %get-tuple-element.35.c.c0), custom_call_target="tpu_custom_call" | custom-call | flops 1073741824 | bytes 4194304 | tf_op jit(solution)/shard_map/pallas_call | solution.py:270
  77.1 1.3 %collective-permute-start.25 = (f32[8,128]{1,0:T(8,128)S(1)}, f32[8,128]{1,0:T(8,128)S(1)}, u32[]{:S(2)}, u32[]{:S(2)}) collective-permute-start(f32[8,128]{1,0:T(8,128)S(1)} %get-tuple-element.35.c.c0), channel_id=1, source_target_pairs={{0,20},{4,16},{16,4},{20,0},{1,21},{5,17},{17,5},{21,1},{2,22},{6,... | collective-permute-start | bytes 12296 | tf_op jit(solution)/shard_map/ppermute | solution.py:230
  80.2 1.9 %collective-permute-done.23.c1 = f32[8,128]{1,0:T(8,128)S(1)} collective-permute-done((f32[8,128]{1,0:T(8,128)S(1)}, f32[8,128]{1,0:T(8,128)S(1)}, u32[]{:S(2)}, u32[]{:S(2)}) %collective-permute-start.23) | collective-permute-done | bytes 4128 | tf_op jit(solution)/shard_map/ppermute | solution.py:230
  82.8 2.8 %collective-permute-start.29 = (bf16[256,512]{1,0:T(8,128)(2,1)S(1)}, bf16[256,512]{1,0:T(8,128)(2,1)S(1)}, u32[]{:S(2)}, u32[]{:S(2)}) collective-permute-start(bf16[256,512]{1,0:T(8,128)(2,1)S(1)} %get-tuple-element.43), channel_id=1, source_target_pairs={{0,33},{1,32},{32,1},{33,0},{2,35},{3,34},{34,3},{35,2},{4,37},{5,... | collective-permute-start | bytes 786440 | tf_op jit(solution)/shard_map/ppermute | solution.py:230
  85.6 1.6 %shard_map.69 = (bf16[256,512]{1,0:T(8,128)(2,1)S(1)}, bf16[256,512]{1,0:T(8,128)(2,1)S(1)}, bf16[256,512]{1,0:T(8,128)(2,1)S(1)}, f32[6,128]{1,0:T(8,128)S(1)}) custom-call(f32[1024,1024]{1,0:T(8,128)S(1)} %get-tuple-element.29.m_ref, bf16[1024,512]{1,0:T(8,128)(2,1)S(1)} %get-tuple-element.24.y_ref, f32[8,128]{1,0:T(8,128)S(1)} %get-tuple-element.35.c.c0, ...), custom_call_target="tpu_custom_call" | custom-call | flops 805306368 | bytes 4194304 | tf_op jit(solution)/shard_map/pallas_call | solution.py:270
  89.5 2.3 %collective-permute-start.32 = (f32[8,128]{1,0:T(8,128)S(1)}, f32[8,128]{1,0:T(8,128)S(1)}, u32[]{:S(2)}, u32[]{:S(2)}) collective-permute-start(f32[8,128]{1,0:T(8,128)S(1)} %pad_maximum_fusion.r0), channel_id=1, source_target_pairs={{0,33},{1,32},{32,1},{33,0},{2,35},{3,34},{34,3},{35,2},{4,37},{5,... | collective-permute-start | bytes 12296 | tf_op jit(solution)/shard_map/ppermute | solution.py:230
  91.7 5.3 %collective-permute-done.32.r3 = f32[8,128]{1,0:T(8,128)S(1)} collective-permute-done((f32[8,128]{1,0:T(8,128)S(1)}, f32[8,128]{1,0:T(8,128)S(1)}, u32[]{:S(2)}, u32[]{:S(2)}) %collective-permute-start.32) | collective-permute-done | bytes 4128 | tf_op jit(solution)/shard_map/ppermute | solution.py:230
  97.0 1.2 %collective-permute-start.31 = (f32[8,128]{1,0:T(8,128)S(1)}, f32[8,128]{1,0:T(8,128)S(1)}, u32[]{:S(2)}, u32[]{:S(2)}) collective-permute-start(f32[8,128]{1,0:T(8,128)S(1)} %pad_maximum_fusion.r0), channel_id=1, source_target_pairs={{0,32},{32,0},{1,33},{33,1},{2,34},{34,2},{3,35},{35,3},{4,36},{36... | collective-permute-start | bytes 12296 | tf_op jit(solution)/shard_map/ppermute | solution.py:230
  98.2 2.4 %collective-permute-done.31.r2 = f32[8,128]{1,0:T(8,128)S(1)} collective-permute-done((f32[8,128]{1,0:T(8,128)S(1)}, f32[8,128]{1,0:T(8,128)S(1)}, u32[]{:S(2)}, u32[]{:S(2)}) %collective-permute-start.31) | collective-permute-done | bytes 4128 | tf_op jit(solution)/shard_map/ppermute | solution.py:230
  100.6 1.2 %collective-permute-start.30 = (f32[8,128]{1,0:T(8,128)S(1)}, f32[8,128]{1,0:T(8,128)S(1)}, u32[]{:S(2)}, u32[]{:S(2)}) collective-permute-start(f32[8,128]{1,0:T(8,128)S(1)} %pad_maximum_fusion.r0), channel_id=1, source_target_pairs={{0,1},{1,0},{2,3},{3,2},{4,5},{5,4},{6,7},{7,6},{8,9},{9,8},{10,11... | collective-permute-start | bytes 12296 | tf_op jit(solution)/shard_map/ppermute | solution.py:230
  101.8 2.4 %collective-permute-done.30.r1 = f32[8,128]{1,0:T(8,128)S(1)} collective-permute-done((f32[8,128]{1,0:T(8,128)S(1)}, f32[8,128]{1,0:T(8,128)S(1)}, u32[]{:S(2)}, u32[]{:S(2)}) %collective-permute-start.30) | collective-permute-done | bytes 4128 | tf_op jit(solution)/shard_map/ppermute | solution.py:230
  104.8 14.1 %all_to_all.11.back_ref = bf16[8,64,512]{2,1,0:T(8,128)(2,1)S(1)} all-to-all(bf16[8,64,512]{2,1,0:T(8,128)(2,1)S(1)} %shard_map.71), channel_id=1, replica_groups={{0,3,12,15,96,99,108,111},{1,2,13,14,97,98,109,110},{4,7,8,11,100,103,1..., dimensions={0} | all-to-all | bytes 1048576 | tf_op jit(solution)/shard_map/all_to_all | solution.py:251
  (60 shorter events, 20.5 us)
Async XLA Ops:
  26.1 6.6 %collective-permute-start.2 = (bf16[256,512]{1,0:T(8,128)(2,1)S(1)}, bf16[256,512]{1,0:T(8,128)(2,1)S(1)}, u32[]{:S(2)}, u32[]{:S(2)}) collective-permute-start(bf16[256,512]{1,0:T(8,128)(2,1)S(1)} %bitcast.4), channel_id=1, source_target_pairs={{0,4},{4,0},{1,5},{5,1},{2,6},{6,2},{3,7},{7,3},{8,12},{12,8},{9,1... | collective-permute-start | bytes 786440 | tf_op jit(solution)/shard_map/ppermute | solution.py:230
  26.2 6.6 %collective-permute-start.1 = (bf16[256,512]{1,0:T(8,128)(2,1)S(1)}, bf16[256,512]{1,0:T(8,128)(2,1)S(1)}, u32[]{:S(2)}, u32[]{:S(2)}) collective-permute-start(bf16[256,512]{1,0:T(8,128)(2,1)S(1)} %bitcast.7), channel_id=1, source_target_pairs={{0,32},{32,0},{1,33},{33,1},{2,34},{34,2},{3,35},{35,3},{4,36},{36... | collective-permute-start | bytes 786440 | tf_op jit(solution)/shard_map/ppermute | solution.py:230
  26.3 6.6 %collective-permute-start = (bf16[256,512]{1,0:T(8,128)(2,1)S(1)}, bf16[256,512]{1,0:T(8,128)(2,1)S(1)}, u32[]{:S(2)}, u32[]{:S(2)}) collective-permute-start(bf16[256,512]{1,0:T(8,128)(2,1)S(1)} %bitcast.8), channel_id=1, source_target_pairs={{0,1},{1,0},{2,3},{3,2},{4,5},{5,4},{6,7},{7,6},{8,9},{9,8},{10,11... | collective-permute-start | bytes 786440 | tf_op jit(solution)/shard_map/ppermute | solution.py:230
  26.4 8.4 %collective-permute-start.3 = (bf16[256,512]{1,0:T(8,128)(2,1)S(1)}, bf16[256,512]{1,0:T(8,128)(2,1)S(1)}, u32[]{:S(2)}, u32[]{:S(2)}) collective-permute-start(bf16[256,512]{1,0:T(8,128)(2,1)S(1)} %bitcast.5), channel_id=1, source_target_pairs={{0,16},{16,0},{1,17},{17,1},{2,18},{18,2},{3,19},{19,3},{4,20},{20... | collective-permute-start | bytes 786440 | tf_op jit(solution)/shard_map/ppermute | solution.py:230
  32.7 2.0 %collective-permute-start.4 = (bf16[256,512]{1,0:T(8,128)(2,1)S(1)}, bf16[256,512]{1,0:T(8,128)(2,1)S(1)}, u32[]{:S(2)}, u32[]{:S(2)}) collective-permute-start(bf16[256,512]{1,0:T(8,128)(2,1)S(1)} %collective-permute-done.2.t1), channel_id=1, source_target_pairs={{0,16},{16,0},{1,17},{17,1},{2,18},{18,2},{3,19},{19,3},{4,20},{20... | collective-permute-start | bytes 786440 | tf_op jit(solution)/shard_map/ppermute | solution.py:230
  32.8 5.9 %collective-permute-start.5 = (bf16[128,512]{1,0:T(8,128)(2,1)S(1)}, bf16[128,512]{1,0:T(8,128)(2,1)S(1)}, u32[]{:S(2)}, u32[]{:S(2)}) collective-permute-start(bf16[128,512]{1,0:T(8,128)(2,1)S(1)} %slice.36), channel_id=1, source_target_pairs={{0,1},{1,0},{2,3},{3,2},{4,5},{5,4},{6,7},{7,6},{8,9},{9,8},{10,11... | collective-permute-start | bytes 393224 | tf_op jit(solution)/shard_map/ppermute | solution.py:230
  32.9 5.9 %collective-permute-start.6 = (bf16[128,512]{1,0:T(8,128)(2,1)S(1)}, bf16[128,512]{1,0:T(8,128)(2,1)S(1)}, u32[]{:S(2)}, u32[]{:S(2)}) collective-permute-start(bf16[128,512]{1,0:T(8,128)(2,1)S(1)} %slice.37), channel_id=1, source_target_pairs={{0,32},{32,0},{1,33},{33,1},{2,34},{34,2},{3,35},{35,3},{4,36},{36... | collective-permute-start | bytes 393224 | tf_op jit(solution)/shard_map/ppermute | solution.py:230
  40.0 4.6 %collective-permute-start.9 = (f32[8,128]{1,0:T(8,128)S(1)}, f32[8,128]{1,0:T(8,128)S(1)}, u32[]{:S(2)}, u32[]{:S(2)}) collective-permute-start(f32[8,128]{1,0:T(8,128)S(1)} %get-tuple-element.31.r0), channel_id=1, source_target_pairs={{0,33},{1,32},{32,1},{33,0},{2,35},{3,34},{34,3},{35,2},{4,37},{5,... | collective-permute-start | bytes 12296 | tf_op jit(solution)/shard_map/ppermute | solution.py:230
  41.5 3.6 %collective-permute-start.8 = (f32[8,128]{1,0:T(8,128)S(1)}, f32[8,128]{1,0:T(8,128)S(1)}, u32[]{:S(2)}, u32[]{:S(2)}) collective-permute-start(f32[8,128]{1,0:T(8,128)S(1)} %get-tuple-element.31.r0), channel_id=1, source_target_pairs={{0,32},{32,0},{1,33},{33,1},{2,34},{34,2},{3,35},{35,3},{4,36},{36... | collective-permute-start | bytes 12296 | tf_op jit(solution)/shard_map/ppermute | solution.py:230
  43.2 3.6 %collective-permute-start.7 = (f32[8,128]{1,0:T(8,128)S(1)}, f32[8,128]{1,0:T(8,128)S(1)}, u32[]{:S(2)}, u32[]{:S(2)}) collective-permute-start(f32[8,128]{1,0:T(8,128)S(1)} %get-tuple-element.31.r0), channel_id=1, source_target_pairs={{0,1},{1,0},{2,3},{3,2},{4,5},{5,4},{6,7},{7,6},{8,9},{9,8},{10,11... | collective-permute-start | bytes 12296 | tf_op jit(solution)/shard_map/ppermute | solution.py:230
  48.0 3.1 %collective-permute-start.12 = (f32[8,128]{1,0:T(8,128)S(1)}, f32[8,128]{1,0:T(8,128)S(1)}, u32[]{:S(2)}, u32[]{:S(2)}) collective-permute-start(f32[8,128]{1,0:T(8,128)S(1)} %get-tuple-element.32.c0), channel_id=1, source_target_pairs={{0,20},{4,16},{16,4},{20,0},{1,21},{5,17},{17,5},{21,1},{2,22},{6,... | collective-permute-start | bytes 12296 | tf_op jit(solution)/shard_map/ppermute | solution.py:230
  48.1 3.0 %collective-permute-start.11 = (f32[8,128]{1,0:T(8,128)S(1)}, f32[8,128]{1,0:T(8,128)S(1)}, u32[]{:S(2)}, u32[]{:S(2)}) collective-permute-start(f32[8,128]{1,0:T(8,128)S(1)} %get-tuple-element.32.c0), channel_id=1, source_target_pairs={{0,16},{16,0},{1,17},{17,1},{2,18},{18,2},{3,19},{19,3},{4,20},{20... | collective-permute-start | bytes 12296 | tf_op jit(solution)/shard_map/ppermute | solution.py:230
  49.4 3.6 %collective-permute-start.10 = (f32[8,128]{1,0:T(8,128)S(1)}, f32[8,128]{1,0:T(8,128)S(1)}, u32[]{:S(2)}, u32[]{:S(2)}) collective-permute-start(f32[8,128]{1,0:T(8,128)S(1)} %get-tuple-element.32.c0), channel_id=1, source_target_pairs={{0,4},{4,0},{1,5},{5,1},{2,6},{6,2},{3,7},{7,3},{8,12},{12,8},{9,1... | collective-permute-start | bytes 12296 | tf_op jit(solution)/shard_map/ppermute | solution.py:230
  54.2 4.6 %collective-permute-start.15 = (f32[8,128]{1,0:T(8,128)S(1)}, f32[8,128]{1,0:T(8,128)S(1)}, u32[]{:S(2)}, u32[]{:S(2)}) collective-permute-start(f32[8,128]{1,0:T(8,128)S(1)} %shard_map.63.r0), channel_id=1, source_target_pairs={{0,33},{1,32},{32,1},{33,0},{2,35},{3,34},{34,3},{35,2},{4,37},{5,... | collective-permute-start | bytes 12296 | tf_op jit(solution)/shard_map/ppermute | solution.py:230
  57.0 3.6 %collective-permute-start.14 = (f32[8,128]{1,0:T(8,128)S(1)}, f32[8,128]{1,0:T(8,128)S(1)}, u32[]{:S(2)}, u32[]{:S(2)}) collective-permute-start(f32[8,128]{1,0:T(8,128)S(1)} %shard_map.63.r0), channel_id=1, source_target_pairs={{0,32},{32,0},{1,33},{33,1},{2,34},{34,2},{3,35},{35,3},{4,36},{36... | collective-permute-start | bytes 12296 | tf_op jit(solution)/shard_map/ppermute | solution.py:230
  57.0 3.6 %collective-permute-start.13 = (f32[8,128]{1,0:T(8,128)S(1)}, f32[8,128]{1,0:T(8,128)S(1)}, u32[]{:S(2)}, u32[]{:S(2)}) collective-permute-start(f32[8,128]{1,0:T(8,128)S(1)} %shard_map.63.r0), channel_id=1, source_target_pairs={{0,1},{1,0},{2,3},{3,2},{4,5},{5,4},{6,7},{7,6},{8,9},{9,8},{10,11... | collective-permute-start | bytes 12296 | tf_op jit(solution)/shard_map/ppermute | solution.py:230
  61.8 3.1 %collective-permute-start.18 = (f32[8,128]{1,0:T(8,128)S(1)}, f32[8,128]{1,0:T(8,128)S(1)}, u32[]{:S(2)}, u32[]{:S(2)}) collective-permute-start(f32[8,128]{1,0:T(8,128)S(1)} %get-tuple-element.33.c0), channel_id=1, source_target_pairs={{0,20},{4,16},{16,4},{20,0},{1,21},{5,17},{17,5},{21,1},{2,22},{6,... | collective-permute-start | bytes 12296 | tf_op jit(solution)/shard_map/ppermute | solution.py:230
  61.9 3.0 %collective-permute-start.17 = (f32[8,128]{1,0:T(8,128)S(1)}, f32[8,128]{1,0:T(8,128)S(1)}, u32[]{:S(2)}, u32[]{:S(2)}) collective-permute-start(f32[8,128]{1,0:T(8,128)S(1)} %get-tuple-element.33.c0), channel_id=1, source_target_pairs={{0,16},{16,0},{1,17},{17,1},{2,18},{18,2},{3,19},{19,3},{4,20},{20... | collective-permute-start | bytes 12296 | tf_op jit(solution)/shard_map/ppermute | solution.py:230
  62.1 3.8 %collective-permute-start.16 = (f32[8,128]{1,0:T(8,128)S(1)}, f32[8,128]{1,0:T(8,128)S(1)}, u32[]{:S(2)}, u32[]{:S(2)}) collective-permute-start(f32[8,128]{1,0:T(8,128)S(1)} %get-tuple-element.33.c0), channel_id=1, source_target_pairs={{0,4},{4,0},{1,5},{5,1},{2,6},{6,2},{3,7},{7,3},{8,12},{12,8},{9,1... | collective-permute-start | bytes 12296 | tf_op jit(solution)/shard_map/ppermute | solution.py:230
  67.1 4.6 %collective-permute-start.21 = (f32[8,128]{1,0:T(8,128)S(1)}, f32[8,128]{1,0:T(8,128)S(1)}, u32[]{:S(2)}, u32[]{:S(2)}) collective-permute-start(f32[8,128]{1,0:T(8,128)S(1)} %shard_map.65.r0), channel_id=1, source_target_pairs={{0,33},{1,32},{32,1},{33,0},{2,35},{3,34},{34,3},{35,2},{4,37},{5,... | collective-permute-start | bytes 12296 | tf_op jit(solution)/shard_map/ppermute | solution.py:230
  68.6 3.6 %collective-permute-start.20 = (f32[8,128]{1,0:T(8,128)S(1)}, f32[8,128]{1,0:T(8,128)S(1)}, u32[]{:S(2)}, u32[]{:S(2)}) collective-permute-start(f32[8,128]{1,0:T(8,128)S(1)} %shard_map.65.r0), channel_id=1, source_target_pairs={{0,32},{32,0},{1,33},{33,1},{2,34},{34,2},{3,35},{35,3},{4,36},{36... | collective-permute-start | bytes 12296 | tf_op jit(solution)/shard_map/ppermute | solution.py:230
  70.0 3.6 %collective-permute-start.19 = (f32[8,128]{1,0:T(8,128)S(1)}, f32[8,128]{1,0:T(8,128)S(1)}, u32[]{:S(2)}, u32[]{:S(2)}) collective-permute-start(f32[8,128]{1,0:T(8,128)S(1)} %shard_map.65.r0), channel_id=1, source_target_pairs={{0,1},{1,0},{2,3},{3,2},{4,5},{5,4},{6,7},{7,6},{8,9},{9,8},{10,11... | collective-permute-start | bytes 12296 | tf_op jit(solution)/shard_map/ppermute | solution.py:230
  77.0 11.0 %collective-permute-start.22 = (bf16[512,512]{1,0:T(8,128)(2,1)S(1)}, bf16[512,512]{1,0:T(8,128)(2,1)S(1)}, u32[]{:S(2)}, u32[]{:S(2)}) collective-permute-start(bf16[512,512]{1,0:T(8,128)(2,1)S(1)} %get-tuple-element.37), channel_id=1, source_target_pairs={{0,16},{16,0},{1,17},{17,1},{2,18},{18,2},{3,19},{19,3},{4,20},{20... | collective-permute-start | bytes 1572872 | tf_op jit(solution)/shard_map/ppermute | solution.py:230
  77.1 3.1 %collective-permute-start.25 = (f32[8,128]{1,0:T(8,128)S(1)}, f32[8,128]{1,0:T(8,128)S(1)}, u32[]{:S(2)}, u32[]{:S(2)}) collective-permute-start(f32[8,128]{1,0:T(8,128)S(1)} %get-tuple-element.35.c.c0), channel_id=1, source_target_pairs={{0,20},{4,16},{16,4},{20,0},{1,21},{5,17},{17,5},{21,1},{2,22},{6,... | collective-permute-start | bytes 12296 | tf_op jit(solution)/shard_map/ppermute | solution.py:230
  78.5 3.6 %collective-permute-start.23 = (f32[8,128]{1,0:T(8,128)S(1)}, f32[8,128]{1,0:T(8,128)S(1)}, u32[]{:S(2)}, u32[]{:S(2)}) collective-permute-start(f32[8,128]{1,0:T(8,128)S(1)} %get-tuple-element.35.c.c0), channel_id=1, source_target_pairs={{0,4},{4,0},{1,5},{5,1},{2,6},{6,2},{3,7},{7,3},{8,12},{12,8},{9,1... | collective-permute-start | bytes 12296 | tf_op jit(solution)/shard_map/ppermute | solution.py:230
  82.8 21.5 %collective-permute-start.29 = (bf16[256,512]{1,0:T(8,128)(2,1)S(1)}, bf16[256,512]{1,0:T(8,128)(2,1)S(1)}, u32[]{:S(2)}, u32[]{:S(2)}) collective-permute-start(bf16[256,512]{1,0:T(8,128)(2,1)S(1)} %get-tuple-element.43), channel_id=1, source_target_pairs={{0,33},{1,32},{32,1},{33,0},{2,35},{3,34},{34,3},{35,2},{4,37},{5,... | collective-permute-start | bytes 786440 | tf_op jit(solution)/shard_map/ppermute | solution.py:230
  87.2 17.1 %collective-permute-start.27 = (bf16[256,512]{1,0:T(8,128)(2,1)S(1)}, bf16[256,512]{1,0:T(8,128)(2,1)S(1)}, u32[]{:S(2)}, u32[]{:S(2)}) collective-permute-start(bf16[256,512]{1,0:T(8,128)(2,1)S(1)} %get-tuple-element.41), channel_id=1, source_target_pairs={{0,1},{1,0},{2,3},{3,2},{4,5},{5,4},{6,7},{7,6},{8,9},{9,8},{10,11... | collective-permute-start | bytes 786440 | tf_op jit(solution)/shard_map/ppermute | solution.py:230
  87.3 17.0 %collective-permute-start.28 = (bf16[256,512]{1,0:T(8,128)(2,1)S(1)}, bf16[256,512]{1,0:T(8,128)(2,1)S(1)}, u32[]{:S(2)}, u32[]{:S(2)}) collective-permute-start(bf16[256,512]{1,0:T(8,128)(2,1)S(1)} %get-tuple-element.42), channel_id=1, source_target_pairs={{0,32},{32,0},{1,33},{33,1},{2,34},{34,2},{3,35},{35,3},{4,36},{36... | collective-permute-start | bytes 786440 | tf_op jit(solution)/shard_map/ppermute | solution.py:230
  88.5 15.7 %collective-permute-start.26 = (bf16[256,512]{1,0:T(8,128)(2,1)S(1)}, bf16[256,512]{1,0:T(8,128)(2,1)S(1)}, u32[]{:S(2)}, u32[]{:S(2)}) collective-permute-start(bf16[256,512]{1,0:T(8,128)(2,1)S(1)} %get-tuple-element.39), channel_id=1, source_target_pairs={{0,4},{4,0},{1,5},{5,1},{2,6},{6,2},{3,7},{7,3},{8,12},{12,8},{9,1... | collective-permute-start | bytes 786440 | tf_op jit(solution)/shard_map/ppermute | solution.py:230
  89.5 7.5 %collective-permute-start.32 = (f32[8,128]{1,0:T(8,128)S(1)}, f32[8,128]{1,0:T(8,128)S(1)}, u32[]{:S(2)}, u32[]{:S(2)}) collective-permute-start(f32[8,128]{1,0:T(8,128)S(1)} %pad_maximum_fusion.r0), channel_id=1, source_target_pairs={{0,33},{1,32},{32,1},{33,0},{2,35},{3,34},{34,3},{35,2},{4,37},{5,... | collective-permute-start | bytes 12296 | tf_op jit(solution)/shard_map/ppermute | solution.py:230
  97.0 3.6 %collective-permute-start.31 = (f32[8,128]{1,0:T(8,128)S(1)}, f32[8,128]{1,0:T(8,128)S(1)}, u32[]{:S(2)}, u32[]{:S(2)}) collective-permute-start(f32[8,128]{1,0:T(8,128)S(1)} %pad_maximum_fusion.r0), channel_id=1, source_target_pairs={{0,32},{32,0},{1,33},{33,1},{2,34},{34,2},{3,35},{35,3},{4,36},{36... | collective-permute-start | bytes 12296 | tf_op jit(solution)/shard_map/ppermute | solution.py:230
  100.6 3.6 %collective-permute-start.30 = (f32[8,128]{1,0:T(8,128)S(1)}, f32[8,128]{1,0:T(8,128)S(1)}, u32[]{:S(2)}, u32[]{:S(2)}) collective-permute-start(f32[8,128]{1,0:T(8,128)S(1)} %pad_maximum_fusion.r0), channel_id=1, source_target_pairs={{0,1},{1,0},{2,3},{3,2},{4,5},{5,4},{6,7},{7,6},{8,9},{9,8},{10,11... | collective-permute-start | bytes 12296 | tf_op jit(solution)/shard_map/ppermute | solution.py:230
  (3 other events, 74.2 us)

commit v3 on v2

--- a/solution.py
+++ b/solution.py
@@ -19,15 +19,15 @@
 VMEM_LIMIT = 24 * 1024 * 1024
 LANES = 128
 STEP = 128
-SPLIT = ((3,), (1, 2, 0))
-
-
-def compact(column):
-    rows = [
-        jnp.transpose(jnp.broadcast_to(column[a : a + LANES], (LANES, LANES)))[0:1]
-        for a in range(0, column.shape[0], LANES)
-    ]
-    return jnp.concatenate(rows, axis=0)
+SPLIT = ((3,), (1,), (2, 0))
+
+
+def compact(columns):
+    lane = lax.broadcasted_iota(jnp.int32, (LANES, LANES), 1)
+    held = jnp.zeros((LANES, LANES), jnp.float32)
+    for n, column in enumerate(columns):
+        held = jnp.where(lane == n, column, held)
+    return jnp.transpose(held)[0 : len(columns)]
 
 
 def combine(parts):
@@ -51,9 +51,16 @@
 
 
 def put_column(column_ref, value):
-    for a in range(value.shape[0]):
-        spread = jnp.transpose(jnp.broadcast_to(value[a : a + 1], (LANES, LANES)))
-        column_ref[a * LANES : (a + 1) * LANES] = spread[:, 0:1]
+    column_ref[:, 0 : value.shape[0]] = jnp.transpose(value)
+
+
+def column_of(column_ref, a, count):
+    n, b = a // LANES, a % LANES
+    return column_ref[b : b + count, n : n + 1]
+
+
+def over_blocks(column_ref, rows, make):
+    return jnp.concatenate([make(a, column_of(column_ref, a, LANES)) for a in range(0, rows, LANES)], axis=0)
 
 
 def row_lse_chunk(scores):
@@ -105,6 +112,7 @@
 
 
 def score_rows(scale, rows, x_ref, y_ref, line_ref, m_ref, lse_ref):
+    found = []
     for a in rows:
         block = x_ref[a : a + STEP, :]
         wide = block.astype(jnp.float32)
@@ -112,7 +120,9 @@
         inner = lax.dot_general(block, y_ref[...], (((1,), (1,)), ((), ())), preferred_element_type=jnp.float32)
         scores = (2.0 * inner - norms - line_ref[...]) * scale
         m_ref[a : a + STEP, :] = scores
-        lse_ref[a // LANES : a // LANES + 1, :] = compact(row_lse_chunk(scores))
+        found.append(row_lse_chunk(scores))
+    first = rows[0] // LANES
+    lse_ref[first : first + len(found), :] = compact(found)
 
 
 def first_kernel(scale, s0, s1, s2, t0, t1, t2, t3, m_ref, x_ref, y_ref, lse_ref, line_ref):
@@ -125,21 +135,18 @@
     score_rows(scale, range(0, 3 * rows, STEP), x_ref, y_ref, line_ref, m_ref, lse_ref)
 
 
-def second_kernel(scale, y_ref, line_ref, part_ref, sa, sb, m_in, x_in, m_ref, x_ref, lse_ref):
-    half = sa.shape[0]
-    ready = 6 * half
-    x_ref[ready : ready + half, :] = sa[...]
-    x_ref[ready + half : ready + 2 * half, :] = sb[...]
-    lines = ready // LANES
-    lse_ref[0:lines, :] = part_ref[0:lines, :]
-    score_rows(scale, range(ready, ready + 2 * half, STEP), x_ref, y_ref, line_ref, m_ref, lse_ref)
+def second_kernel(scale, ready, y_ref, line_ref, part_ref, sb, m_in, x_in, m_ref, x_ref, lse_ref):
+    half = sb.shape[0]
+    x_ref[ready : ready + half, :] = sb[...]
+    lse_ref[...] = part_ref[...]
+    score_rows(scale, range(ready, ready + half, STEP), x_ref, y_ref, line_ref, m_ref, lse_ref)
 
 
 def row_kernel(log_mass, m_ref, c0, c1, c2, c3, lse_ref, row_ref):
     put_row(row_ref, log_mass - combine(aligned([c0[...], c1[...], c2[...], c3[...]])))
-    for a in range(0, m_ref.shape[0], STEP):
-        scores = m_ref[a : a + STEP, :] + row_ref[...]
-        lse_ref[a // LANES : a // LANES + 1, :] = compact(row_lse_chunk(scores))
+    lse_ref[...] = compact(
+        [row_lse_chunk(m_ref[a : a + STEP, :] + row_ref[...]) for a in range(0, m_ref.shape[0], STEP)]
+    )
 
 
 def column_kernel(log_mass, m_ref, r0, r1, r2, r3, lse_ref, f_ref, column_ref):
@@ -154,26 +161,31 @@
 
     highest = jnp.full((8, columns), -jnp.inf, jnp.float32)
     for a in range(0, m_ref.shape[0], step):
-        highest = jnp.maximum(highest, fold(m_ref[a : a + step, :] + column_ref[a : a + step], jnp.maximum))
+        highest = jnp.maximum(highest, fold(m_ref[a : a + step, :] + column_of(column_ref, a, step), jnp.maximum))
     highest = jnp.max(highest, axis=0, keepdims=True)
     total = jnp.zeros((8, columns), jnp.float32)
     for a in range(0, m_ref.shape[0], step):
-        scores = m_ref[a : a + step, :] + column_ref[a : a + step]
+        scores = m_ref[a : a + step, :] + column_of(column_ref, a, step)
         total = total + fold(jnp.exp2(scores - highest), jnp.add)
     lse = highest + jnp.log2(jnp.sum(total, axis=0, keepdims=True))
     for a in range(lse_ref.shape[0]):
         lse_ref[a : a + 1, :] = lse[:, a * LANES : (a + 1) * LANES]
 
 
-def target_kernel(m_ref, x_ref, f, c, near_ref, far_ref, column_ref, row_ref):
+def target_kernel(first, m_ref, x_ref, f, c, out_ref, column_ref, row_ref):
     put_column(column_ref, f[...])
     put_row(row_ref, c[...])
     step = 256
-    half = near_ref.shape[0]
-    for a in range(0, m_ref.shape[1], step):
-        out_ref, b = (near_ref, a) if a < half else (far_ref, a - half)
-        scores = m_ref[:, a : a + step] + column_ref[...]
-        weights = jnp.exp2(scores - row_ref[:, a : a + step]).astype(jnp.bfloat16)
+    half = out_ref.shape[0]
+    for b in range(0, half, step):
+        a = first * half + b
+        weights = over_blocks(
+            column_ref,
+            m_ref.shape[0],
+            lambda c, column: jnp.exp2(
+                m_ref[c : c + LANES, a : a + step] + column - row_ref[:, a : a + step]
+            ).astype(jnp.bfloat16),
+        )
         out_ref[b : b + step, :] = lax.dot_general(
             weights, x_ref[...], (((0,), (0,)), ((), ())), preferred_element_type=jnp.float32
         ).astype(jnp.bfloat16)
@@ -183,6 +195,7 @@
     *pieces, lse_ref, row_ref = refs
     put_row(row_ref, log_mass - combine(aligned([c0[...], c1[...], c2[...], c3[...]])))
     rows = pieces[0].shape[0]
+    found = []
     for place, a in enumerate(a for q in blocks for a in range(q * rows, (q + 1) * rows, STEP)):
         scores = m_ref[a : a + STEP, :] + row_ref[...]
         highest = jnp.max(scores, axis=1, keepdims=True)
@@ -190,7 +203,8 @@
         total = jnp.sum(raised, axis=1, keepdims=True)
         mapped = jnp.dot(raised.astype(jnp.bfloat16), y_ref[...], preferred_element_type=jnp.float32)
         pieces[place * STEP // rows][a % rows : a % rows + STEP, :] = (mapped / total).astype(jnp.bfloat16)
-        lse_ref[place : place + 1, :] = compact(highest + jnp.log2(total))
+        found.append(highest + jnp.log2(total))
+    lse_ref[...] = compact(found)
 
 
 def join_kernel(p_ref, near_ref, c0, c1, c2, c3, out_ref, far_ref, own_ref, mate_ref):
@@ -200,8 +214,14 @@
     top = whole.shape[0] // 2
     put_column(own_ref, jnp.exp2(parts[0] - whole)[:top])
     put_column(mate_ref, jnp.exp2(parts[2] - whole)[:top])
-    mine = p_ref[...].astype(jnp.float32) * own_ref[...]
-    joined = (mine + near_ref[...].astype(jnp.float32) * mate_ref[...]).astype(jnp.bfloat16)
+    joined = over_blocks(
+        own_ref,
+        2 * rows,
+        lambda a, column: (
+            p_ref[a : a + LANES, :].astype(jnp.float32) * column
+            + near_ref[a : a + LANES, :].astype(jnp.float32) * column_of(mate_ref, a, LANES)
+        ).astype(jnp.bfloat16),
+    )
     out_ref[...] = joined[:rows]
     far_ref[...] = joined[rows:]
 
@@ -217,7 +237,9 @@
     total = None
     for piece, part, column in zip((s0, s1, s2, s3), parts, (w0, w1, w2, w3)):
         put_column(column, jnp.exp2(part - whole))
-        term = piece[...].astype(jnp.float32) * column[...]
+        term = over_blocks(
+            column, rows, lambda a, weight, piece=piece: piece[a : a + LANES, :].astype(jnp.float32) * weight
+        )
         total = term if total is None else total + term
     total = total.astype(jnp.bfloat16)
     summed = (t_ref[...].astype(jnp.float32) + far_ref[...].astype(jnp.float32)).astype(jnp.bfloat16)
@@ -279,7 +301,7 @@
         )(*args)
 
     def column(n):
-        return pltpu.VMEM((n, 1), f32)
+        return pltpu.VMEM((LANES, n // LANES), f32)
 
     def line(n):
         return pltpu.VMEM((1, n), f32)
@@ -315,15 +337,17 @@
         3 * flops // 4,
         area,
     )
-    matrix, all_sources, row_part = call(
-        functools.partial(second_kernel, scale),
-        [out((side, side), f32), out((side, width), bf16), out(tile, f32)],
-        [],
-        [all_targets, norms, part, s3a, s3b, matrix, all_sources],
-        flops // 4,
-        area // 4,
-        {5: 0, 6: 1},
-    )
+    row_part = part
+    for ready, block in ((3 * rows + half, s3b), (3 * rows, s3a)):
+        matrix, all_sources, row_part = call(
+            functools.partial(second_kernel, scale, ready),
+            [out((side, side), f32), out((side, width), bf16), out(tile, f32)],
+            [],
+            [all_targets, norms, row_part, block, matrix, all_sources],
+            flops // 8,
+            area // 8,
+            {4: 0, 5: 1},
+        )
 
     def exchange(value, slow, fast):
         both = swap(value, (slow, fast), ACROSS)
@@ -351,14 +375,17 @@
                 area,
             )
 
-    target_near, target_far = call(
-        target_kernel,
-        [out((2 * rows, width), bf16)] * 2,
-        [column(side), line(side)],
-        [matrix, all_sources, source_potential, column_part],
-        flops,
-        area,
-    )
+    target_near, target_far = [
+        call(
+            functools.partial(target_kernel, first),
+            [out((2 * rows, width), bf16)],
+            [column(side), line(side)],
+            [matrix, all_sources, source_potential, column_part],
+            flops // 2,
+            area // 2,
+        )[0]
+        for first in (0, 1)
+    ]
     near = swap(target_far, "core")
     made = {}
     lines = []

time: 120 us -> 121 us (level)
  waiting for transfers between devices: 34.4 us -> 37 us
  starting transfers between devices: 28.8 us -> 26.6 us
    ppermute x33, waiting for transfers between devices: 34.4 us -> 37 us  [swap(): return lax.ppermute(value, axis, pairs)]
    ppermute x33, starting transfers between devices: 28.8 us -> 26.6 us  [swap(): return lax.ppermute(value, axis, pairs)]
    pallas_call x14 -> x17, Pallas kernels: 18.6 us -> 19.4 us  [call(): pl.pallas_call(kernel, out_shape=outs, in_specs=[spec] * len(args), out_s...]
  transfers between devices with their start and end apart: 33 -> 33, of which waited for: 21 -> 18; matrix products, arithmetic and copies ran while one was open for 0% -> 0% of each run, Pallas kernels for 4% -> 6%
where the time goes in v3:
time: 121 us
  blocking collectives  37.2 us (31%)
  waiting for transfers between devices  37 us (31%)
  starting transfers between devices  26.6 us (22%)
  Pallas kernels  19.4 us (16%)
    all_to_all x2, blocking collectives, across(): lax.all_to_all(value, AXES, split_axis=0, concat_axis=0, axis_index_group...  37.2 us
    ppermute x33, waiting for transfers between devices, swap(): return lax.ppermute(value, axis, pairs)  37 us
    ppermute x33, starting transfers between devices, swap(): return lax.ppermute(value, axis, pairs)  26.6 us
    pallas_call x17, Pallas kernels, call(): pl.pallas_call(kernel, out_shape=outs, in_specs=[spec] * len(args), out_s...  19.4 us
  transfers between devices with their start and end apart: 33, of which 18 were waited for; matrix products, arithmetic and copies ran while one was open for 0% of the time, Pallas kernels for 6%

profile of v3, /device:TPU:0, one launch (start us, length us, event | category | flops | bytes accessed | tf_op | source)
XLA Modules:
  0.0 121.2 jit_solution(1057799252225376626)
XLA Ops:
  0.6 2.3 %shard_map.59 = bf16[8,64,512]{2,1,0:T(8,128)(2,1)} custom-call(s32[1,256]{1,0:T(1,128)} %bitcast.10, bf16[256,512]{1,0:T(8,128)(2,1)} %s_hbm.1, s32[1,256]{1,0:T(1,128)} %bitcast.12, bf16[256,512]{1,0:T(8,128)(2,1)} %t_hbm.1), custom_call_target="tpu_custom_call" | custom-call | bytes 4194304 | tf_op jit(solution)/shard_map/pallas_call | solution.py:292
  2.9 23.1 %all_to_all.10 = bf16[8,64,512]{2,1,0:T(8,128)(2,1)S(1)} all-to-all(bf16[8,64,512]{2,1,0:T(8,128)(2,1)} %shard_map.59), channel_id=1, replica_groups={{0,3,12,15,96,99,108,111},{1,2,13,14,97,98,109,110},{4,7,8,11,100,103,1..., dimensions={0} | all-to-all | bytes 1048576 | tf_op jit(solution)/shard_map/all_to_all | solution.py:273
  26.5 6.3 %collective-permute-done.2.t1 = bf16[256,512]{1,0:T(8,128)(2,1)S(1)} collective-permute-done((bf16[256,512]{1,0:T(8,128)(2,1)S(1)}, bf16[256,512]{1,0:T(8,128)(2,1)S(1)}, u32[]{:S(2)}, u32[]{:S(2)}) %collective-permute-start.2) | collective-permute-done | bytes 262176 | tf_op jit(solution)/shard_map/ppermute | solution.py:252
  32.9 1.8 %collective-permute-start.6 = (bf16[128,512]{1,0:T(8,128)(2,1)S(1)}, bf16[128,512]{1,0:T(8,128)(2,1)S(1)}, u32[]{:S(2)}, u32[]{:S(2)}) collective-permute-start(bf16[128,512]{1,0:T(8,128)(2,1)S(1)} %slice.35), channel_id=1, source_target_pairs={{0,1},{1,0},{2,3},{3,2},{4,5},{5,4},{6,7},{7,6},{8,9},{9,8},{10,11... | collective-permute-start | bytes 393224 | tf_op jit(solution)/shard_map/ppermute | solution.py:252
  34.8 2.6 %shard_map.60 = (f32[1024,1024]{1,0:T(8,128)S(1)}, bf16[1024,512]{1,0:T(8,128)(2,1)S(1)}, bf16[1024,512]{1,0:T(8,128)(2,1)S(1)}, f32[8,128]{1,0:T(8,128)S(1)}, f32[1,1024]{1,0:T(1,128)S(1)}) custom-call(bf16[256,512]{1,0:T(8,128)(2,1)S(1)} %bitcast.9, bf16[256,512]{1,0:T(8,128)(2,1)S(1)} %collective-permute-done.s1, ...), custom_call_target="tpu_custom_call" | custom-call | flops 805306368 | bytes 4194304 | tf_op jit(solution)/shard_map/pallas_call | solution.py:292
  37.3 1.4 %collective-permute-done.5.sb = bf16[128,512]{1,0:T(8,128)(2,1)S(1)} collective-permute-done((bf16[128,512]{1,0:T(8,128)(2,1)S(1)}, bf16[128,512]{1,0:T(8,128)(2,1)S(1)}, u32[]{:S(2)}, u32[]{:S(2)}) %collective-permute-start.5) | collective-permute-done | bytes 131104 | tf_op jit(solution)/shard_map/ppermute | solution.py:252
  41.9 1.8 %collective-permute-start.7 = (f32[8,128]{1,0:T(8,128)S(1)}, f32[8,128]{1,0:T(8,128)S(1)}, u32[]{:S(2)}, u32[]{:S(2)}) collective-permute-start(f32[8,128]{1,0:T(8,128)S(1)} %get-tuple-element.36.r0), channel_id=1, source_target_pairs={{0,1},{1,0},{2,3},{3,2},{4,5},{5,4},{6,7},{7,6},{8,9},{9,8},{10,11... | collective-permute-start | bytes 12296 | tf_op jit(solution)/shard_map/ppermute | solution.py:252
  43.7 1.0 collective-permute-done.9.r3
  45.6 1.1 shard_map.63
  46.8 3.4 %collective-permute-start.11 = (f32[8,128]{1,0:T(8,128)S(1)}, f32[8,128]{1,0:T(8,128)S(1)}, u32[]{:S(2)}, u32[]{:S(2)}) collective-permute-start(f32[8,128]{1,0:T(8,128)S(1)} %get-tuple-element.37.c0), channel_id=1, source_target_pairs={{0,16},{16,0},{1,17},{17,1},{2,18},{18,2},{3,19},{19,3},{4,20},{20... | collective-permute-start | bytes 12296 | tf_op jit(solution)/shard_map/ppermute | solution.py:252
  51.0 2.8 %collective-permute-done.10.c1 = f32[8,128]{1,0:T(8,128)S(1)} collective-permute-done((f32[8,128]{1,0:T(8,128)S(1)}, f32[8,128]{1,0:T(8,128)S(1)}, u32[]{:S(2)}, u32[]{:S(2)}) %collective-permute-start.10) | collective-permute-done | bytes 4128 | tf_op jit(solution)/shard_map/ppermute | solution.py:252
  53.8 1.2 shard_map.64.r0
  55.2 1.7 %collective-permute-start.14 = (f32[8,128]{1,0:T(8,128)S(1)}, f32[8,128]{1,0:T(8,128)S(1)}, u32[]{:S(2)}, u32[]{:S(2)}) collective-permute-start(f32[8,128]{1,0:T(8,128)S(1)} %shard_map.64.r0), channel_id=1, source_target_pairs={{0,32},{32,0},{1,33},{33,1},{2,34},{34,2},{3,35},{35,3},{4,36},{36... | collective-permute-start | bytes 12296 | tf_op jit(solution)/shard_map/ppermute | solution.py:252
  56.9 1.6 %collective-permute-start.13 = (f32[8,128]{1,0:T(8,128)S(1)}, f32[8,128]{1,0:T(8,128)S(1)}, u32[]{:S(2)}, u32[]{:S(2)}) collective-permute-start(f32[8,128]{1,0:T(8,128)S(1)} %shard_map.64.r0), channel_id=1, source_target_pairs={{0,1},{1,0},{2,3},{3,2},{4,5},{5,4},{6,7},{7,6},{8,9},{9,8},{10,11... | collective-permute-start | bytes 12296 | tf_op jit(solution)/shard_map/ppermute | solution.py:252
  60.5 1.1 shard_map.65
  61.9 2.0 %collective-permute-start.16 = (f32[8,128]{1,0:T(8,128)S(1)}, f32[8,128]{1,0:T(8,128)S(1)}, u32[]{:S(2)}, u32[]{:S(2)}) collective-permute-start(f32[8,128]{1,0:T(8,128)S(1)} %get-tuple-element.38.c0), channel_id=1, source_target_pairs={{0,4},{4,0},{1,5},{5,1},{2,6},{6,2},{3,7},{7,3},{8,12},{12,8},{9,1... | collective-permute-start | bytes 12296 | tf_op jit(solution)/shard_map/ppermute | solution.py:252
  65.7 1.2 shard_map.66.r0
  66.9 1.1 collective-permute-start.21
  68.0 2.0 %collective-permute-start.20 = (f32[8,128]{1,0:T(8,128)S(1)}, f32[8,128]{1,0:T(8,128)S(1)}, u32[]{:S(2)}, u32[]{:S(2)}) collective-permute-start(f32[8,128]{1,0:T(8,128)S(1)} %shard_map.66.r0), channel_id=1, source_target_pairs={{0,32},{32,0},{1,33},{33,1},{2,34},{34,2},{3,35},{35,3},{4,36},{36... | collective-permute-start | bytes 12296 | tf_op jit(solution)/shard_map/ppermute | solution.py:252
  71.6 2.0 %collective-permute-done.19.r1 = f32[8,128]{1,0:T(8,128)S(1)} collective-permute-done((f32[8,128]{1,0:T(8,128)S(1)}, f32[8,128]{1,0:T(8,128)S(1)}, u32[]{:S(2)}, u32[]{:S(2)}) %collective-permute-start.19) | collective-permute-done | bytes 4128 | tf_op jit(solution)/shard_map/ppermute | solution.py:252
  73.6 1.1 shard_map.67
  74.7 1.4 %shard_map.69 = bf16[512,512]{1,0:T(8,128)(2,1)S(1)} custom-call(f32[1024,1024]{1,0:T(8,128)S(1)} %get-tuple-element.34.m_ref, bf16[1024,512]{1,0:T(8,128)(2,1)S(1)} %get-tuple-element.35.x_ref, f32[8,128]{1,0:T(8,128)S(1)} %get-tuple-element.39.f, f32[8,128]{1,0:T(8,128)S(1)} %get-tuple-element.40.c.c0), custom_call_target="tpu_custom_call" | custom-call | flops 536870912 | bytes 4194304 | tf_op jit(solution)/shard_map/pallas_call | solution.py:292
  76.3 1.9 %collective-permute-start.25 = (f32[8,128]{1,0:T(8,128)S(1)}, f32[8,128]{1,0:T(8,128)S(1)}, u32[]{:S(2)}, u32[]{:S(2)}) collective-permute-start(f32[8,128]{1,0:T(8,128)S(1)} %get-tuple-element.40.c.c0), channel_id=1, source_target_pairs={{0,20},{4,16},{16,4},{20,0},{1,21},{5,17},{17,5},{21,1},{2,22},{6,... | collective-permute-start | bytes 12296 | tf_op jit(solution)/shard_map/ppermute | solution.py:252
  78.6 1.4 %shard_map.68.p_ref = bf16[512,512]{1,0:T(8,128)(2,1)S(1)} custom-call(f32[1024,1024]{1,0:T(8,128)S(1)} %get-tuple-element.34.m_ref, bf16[1024,512]{1,0:T(8,128)(2,1)S(1)} %get-tuple-element.35.x_ref, f32[8,128]{1,0:T(8,128)S(1)} %get-tuple-element.39.f, f32[8,128]{1,0:T(8,128)S(1)} %get-tuple-element.40.c.c0), custom_call_target="tpu_custom_call" | custom-call | flops 536870912 | bytes 4194304 | tf_op jit(solution)/shard_map/pallas_call | solution.py:292
  80.0 1.8 %collective-permute-done.23.c1 = f32[8,128]{1,0:T(8,128)S(1)} collective-permute-done((f32[8,128]{1,0:T(8,128)S(1)}, f32[8,128]{1,0:T(8,128)S(1)}, u32[]{:S(2)}, u32[]{:S(2)}) %collective-permute-start.23) | collective-permute-done | bytes 4128 | tf_op jit(solution)/shard_map/ppermute | solution.py:252
  83.0 1.2 shard_map.71
  85.2 2.8 %collective-permute-start.29 = (bf16[256,512]{1,0:T(8,128)(2,1)S(1)}, bf16[256,512]{1,0:T(8,128)(2,1)S(1)}, u32[]{:S(2)}, u32[]{:S(2)}) collective-permute-start(bf16[256,512]{1,0:T(8,128)(2,1)S(1)} %get-tuple-element.46), channel_id=1, source_target_pairs={{0,33},{1,32},{32,1},{33,0},{2,35},{3,34},{34,3},{35,2},{4,37},{5,... | collective-permute-start | bytes 786440 | tf_op jit(solution)/shard_map/ppermute | solution.py:252
  89.7 8.5 %collective-permute-done.32.r3 = f32[8,128]{1,0:T(8,128)S(1)} collective-permute-done((f32[8,128]{1,0:T(8,128)S(1)}, f32[8,128]{1,0:T(8,128)S(1)}, u32[]{:S(2)}, u32[]{:S(2)}) %collective-permute-start.32) | collective-permute-done | bytes 4128 | tf_op jit(solution)/shard_map/ppermute | solution.py:252
  98.5 3.3 %collective-permute-done.31.r2 = f32[8,128]{1,0:T(8,128)S(1)} collective-permute-done((f32[8,128]{1,0:T(8,128)S(1)}, f32[8,128]{1,0:T(8,128)S(1)}, u32[]{:S(2)}, u32[]{:S(2)}) %collective-permute-start.31) | collective-permute-done | bytes 4128 | tf_op jit(solution)/shard_map/ppermute | solution.py:252
  102.2 3.2 %collective-permute-done.30.r1 = f32[8,128]{1,0:T(8,128)S(1)} collective-permute-done((f32[8,128]{1,0:T(8,128)S(1)}, f32[8,128]{1,0:T(8,128)S(1)}, u32[]{:S(2)}, u32[]{:S(2)}) %collective-permute-start.30) | collective-permute-done | bytes 4128 | tf_op jit(solution)/shard_map/ppermute | solution.py:252
  106.1 14.1 %all_to_all.11.back_ref = bf16[8,64,512]{2,1,0:T(8,128)(2,1)S(1)} all-to-all(bf16[8,64,512]{2,1,0:T(8,128)(2,1)S(1)} %shard_map.74), channel_id=1, replica_groups={{0,3,12,15,96,99,108,111},{1,2,13,14,97,98,109,110},{4,7,8,11,100,103,1..., dimensions={0} | all-to-all | bytes 1048576 | tf_op jit(solution)/shard_map/all_to_all | solution.py:273
  120.2 1.0 shard_map.75
  (62 shorter events, 17.0 us)
Async XLA Ops:
  26.1 6.6 %collective-permute-start.2 = (bf16[256,512]{1,0:T(8,128)(2,1)S(1)}, bf16[256,512]{1,0:T(8,128)(2,1)S(1)}, u32[]{:S(2)}, u32[]{:S(2)}) collective-permute-start(bf16[256,512]{1,0:T(8,128)(2,1)S(1)} %bitcast.4), channel_id=1, source_target_pairs={{0,4},{4,0},{1,5},{5,1},{2,6},{6,2},{3,7},{7,3},{8,12},{12,8},{9,1... | collective-permute-start | bytes 786440 | tf_op jit(solution)/shard_map/ppermute | solution.py:252
  26.2 6.6 %collective-permute-start = (bf16[256,512]{1,0:T(8,128)(2,1)S(1)}, bf16[256,512]{1,0:T(8,128)(2,1)S(1)}, u32[]{:S(2)}, u32[]{:S(2)}) collective-permute-start(bf16[256,512]{1,0:T(8,128)(2,1)S(1)} %bitcast.7), channel_id=1, source_target_pairs={{0,1},{1,0},{2,3},{3,2},{4,5},{5,4},{6,7},{7,6},{8,9},{9,8},{10,11... | collective-permute-start | bytes 786440 | tf_op jit(solution)/shard_map/ppermute | solution.py:252
  26.3 6.6 %collective-permute-start.1 = (bf16[256,512]{1,0:T(8,128)(2,1)S(1)}, bf16[256,512]{1,0:T(8,128)(2,1)S(1)}, u32[]{:S(2)}, u32[]{:S(2)}) collective-permute-start(bf16[256,512]{1,0:T(8,128)(2,1)S(1)} %bitcast.8), channel_id=1, source_target_pairs={{0,32},{32,0},{1,33},{33,1},{2,34},{34,2},{3,35},{35,3},{4,36},{36... | collective-permute-start | bytes 786440 | tf_op jit(solution)/shard_map/ppermute | solution.py:252
  26.4 8.4 %collective-permute-start.3 = (bf16[256,512]{1,0:T(8,128)(2,1)S(1)}, bf16[256,512]{1,0:T(8,128)(2,1)S(1)}, u32[]{:S(2)}, u32[]{:S(2)}) collective-permute-start(bf16[256,512]{1,0:T(8,128)(2,1)S(1)} %bitcast.5), channel_id=1, source_target_pairs={{0,16},{16,0},{1,17},{17,1},{2,18},{18,2},{3,19},{19,3},{4,20},{20... | collective-permute-start | bytes 786440 | tf_op jit(solution)/shard_map/ppermute | solution.py:252
  32.7 2.0 %collective-permute-start.4 = (bf16[256,512]{1,0:T(8,128)(2,1)S(1)}, bf16[256,512]{1,0:T(8,128)(2,1)S(1)}, u32[]{:S(2)}, u32[]{:S(2)}) collective-permute-start(bf16[256,512]{1,0:T(8,128)(2,1)S(1)} %collective-permute-done.2.t1), channel_id=1, source_target_pairs={{0,16},{16,0},{1,17},{17,1},{2,18},{18,2},{3,19},{19,3},{4,20},{20... | collective-permute-start | bytes 786440 | tf_op jit(solution)/shard_map/ppermute | solution.py:252
  32.8 5.9 %collective-permute-start.5 = (bf16[128,512]{1,0:T(8,128)(2,1)S(1)}, bf16[128,512]{1,0:T(8,128)(2,1)S(1)}, u32[]{:S(2)}, u32[]{:S(2)}) collective-permute-start(bf16[128,512]{1,0:T(8,128)(2,1)S(1)} %slice.34), channel_id=1, source_target_pairs={{0,32},{32,0},{1,33},{33,1},{2,34},{34,2},{3,35},{35,3},{4,36},{36... | collective-permute-start | bytes 393224 | tf_op jit(solution)/shard_map/ppermute | solution.py:252
  32.9 6.5 %collective-permute-start.6 = (bf16[128,512]{1,0:T(8,128)(2,1)S(1)}, bf16[128,512]{1,0:T(8,128)(2,1)S(1)}, u32[]{:S(2)}, u32[]{:S(2)}) collective-permute-start(bf16[128,512]{1,0:T(8,128)(2,1)S(1)} %slice.35), channel_id=1, source_target_pairs={{0,1},{1,0},{2,3},{3,2},{4,5},{5,4},{6,7},{7,6},{8,9},{9,8},{10,11... | collective-permute-start | bytes 393224 | tf_op jit(solution)/shard_map/ppermute | solution.py:252
  40.2 4.6 %collective-permute-start.9 = (f32[8,128]{1,0:T(8,128)S(1)}, f32[8,128]{1,0:T(8,128)S(1)}, u32[]{:S(2)}, u32[]{:S(2)}) collective-permute-start(f32[8,128]{1,0:T(8,128)S(1)} %get-tuple-element.36.r0), channel_id=1, source_target_pairs={{0,33},{1,32},{32,1},{33,0},{2,35},{3,34},{34,3},{35,2},{4,37},{5,... | collective-permute-start | bytes 12296 | tf_op jit(solution)/shard_map/ppermute | solution.py:252
  41.1 3.7 %collective-permute-start.8 = (f32[8,128]{1,0:T(8,128)S(1)}, f32[8,128]{1,0:T(8,128)S(1)}, u32[]{:S(2)}, u32[]{:S(2)}) collective-permute-start(f32[8,128]{1,0:T(8,128)S(1)} %get-tuple-element.36.r0), channel_id=1, source_target_pairs={{0,32},{32,0},{1,33},{33,1},{2,34},{34,2},{3,35},{35,3},{4,36},{36... | collective-permute-start | bytes 12296 | tf_op jit(solution)/shard_map/ppermute | solution.py:252
  41.9 3.6 %collective-permute-start.7 = (f32[8,128]{1,0:T(8,128)S(1)}, f32[8,128]{1,0:T(8,128)S(1)}, u32[]{:S(2)}, u32[]{:S(2)}) collective-permute-start(f32[8,128]{1,0:T(8,128)S(1)} %get-tuple-element.36.r0), channel_id=1, source_target_pairs={{0,1},{1,0},{2,3},{3,2},{4,5},{5,4},{6,7},{7,6},{8,9},{9,8},{10,11... | collective-permute-start | bytes 12296 | tf_op jit(solution)/shard_map/ppermute | solution.py:252
  46.7 3.6 %collective-permute-start.12 = (f32[8,128]{1,0:T(8,128)S(1)}, f32[8,128]{1,0:T(8,128)S(1)}, u32[]{:S(2)}, u32[]{:S(2)}) collective-permute-start(f32[8,128]{1,0:T(8,128)S(1)} %get-tuple-element.37.c0), channel_id=1, source_target_pairs={{0,20},{4,16},{16,4},{20,0},{1,21},{5,17},{17,5},{21,1},{2,22},{6,... | collective-permute-start | bytes 12296 | tf_op jit(solution)/shard_map/ppermute | solution.py:252
  46.8 4.3 %collective-permute-start.11 = (f32[8,128]{1,0:T(8,128)S(1)}, f32[8,128]{1,0:T(8,128)S(1)}, u32[]{:S(2)}, u32[]{:S(2)}) collective-permute-start(f32[8,128]{1,0:T(8,128)S(1)} %get-tuple-element.37.c0), channel_id=1, source_target_pairs={{0,16},{16,0},{1,17},{17,1},{2,18},{18,2},{3,19},{19,3},{4,20},{20... | collective-permute-start | bytes 12296 | tf_op jit(solution)/shard_map/ppermute | solution.py:252
  50.2 3.6 %collective-permute-start.10 = (f32[8,128]{1,0:T(8,128)S(1)}, f32[8,128]{1,0:T(8,128)S(1)}, u32[]{:S(2)}, u32[]{:S(2)}) collective-permute-start(f32[8,128]{1,0:T(8,128)S(1)} %get-tuple-element.37.c0), channel_id=1, source_target_pairs={{0,4},{4,0},{1,5},{5,1},{2,6},{6,2},{3,7},{7,3},{8,12},{12,8},{9,1... | collective-permute-start | bytes 12296 | tf_op jit(solution)/shard_map/ppermute | solution.py:252
  55.0 4.6 %collective-permute-start.15 = (f32[8,128]{1,0:T(8,128)S(1)}, f32[8,128]{1,0:T(8,128)S(1)}, u32[]{:S(2)}, u32[]{:S(2)}) collective-permute-start(f32[8,128]{1,0:T(8,128)S(1)} %shard_map.64.r0), channel_id=1, source_target_pairs={{0,33},{1,32},{32,1},{33,0},{2,35},{3,34},{34,3},{35,2},{4,37},{5,... | collective-permute-start | bytes 12296 | tf_op jit(solution)/shard_map/ppermute | solution.py:252
  55.2 4.4 %collective-permute-start.14 = (f32[8,128]{1,0:T(8,128)S(1)}, f32[8,128]{1,0:T(8,128)S(1)}, u32[]{:S(2)}, u32[]{:S(2)}) collective-permute-start(f32[8,128]{1,0:T(8,128)S(1)} %shard_map.64.r0), channel_id=1, source_target_pairs={{0,32},{32,0},{1,33},{33,1},{2,34},{34,2},{3,35},{35,3},{4,36},{36... | collective-permute-start | bytes 12296 | tf_op jit(solution)/shard_map/ppermute | solution.py:252
  56.9 3.6 %collective-permute-start.13 = (f32[8,128]{1,0:T(8,128)S(1)}, f32[8,128]{1,0:T(8,128)S(1)}, u32[]{:S(2)}, u32[]{:S(2)}) collective-permute-start(f32[8,128]{1,0:T(8,128)S(1)} %shard_map.64.r0), channel_id=1, source_target_pairs={{0,1},{1,0},{2,3},{3,2},{4,5},{5,4},{6,7},{7,6},{8,9},{9,8},{10,11... | collective-permute-start | bytes 12296 | tf_op jit(solution)/shard_map/ppermute | solution.py:252
  61.6 3.1 %collective-permute-start.18 = (f32[8,128]{1,0:T(8,128)S(1)}, f32[8,128]{1,0:T(8,128)S(1)}, u32[]{:S(2)}, u32[]{:S(2)}) collective-permute-start(f32[8,128]{1,0:T(8,128)S(1)} %get-tuple-element.38.c0), channel_id=1, source_target_pairs={{0,20},{4,16},{16,4},{20,0},{1,21},{5,17},{17,5},{21,1},{2,22},{6,... | collective-permute-start | bytes 12296 | tf_op jit(solution)/shard_map/ppermute | solution.py:252
  61.7 3.0 %collective-permute-start.17 = (f32[8,128]{1,0:T(8,128)S(1)}, f32[8,128]{1,0:T(8,128)S(1)}, u32[]{:S(2)}, u32[]{:S(2)}) collective-permute-start(f32[8,128]{1,0:T(8,128)S(1)} %get-tuple-element.38.c0), channel_id=1, source_target_pairs={{0,16},{16,0},{1,17},{17,1},{2,18},{18,2},{3,19},{19,3},{4,20},{20... | collective-permute-start | bytes 12296 | tf_op jit(solution)/shard_map/ppermute | solution.py:252
  61.9 3.8 %collective-permute-start.16 = (f32[8,128]{1,0:T(8,128)S(1)}, f32[8,128]{1,0:T(8,128)S(1)}, u32[]{:S(2)}, u32[]{:S(2)}) collective-permute-start(f32[8,128]{1,0:T(8,128)S(1)} %get-tuple-element.38.c0), channel_id=1, source_target_pairs={{0,4},{4,0},{1,5},{5,1},{2,6},{6,2},{3,7},{7,3},{8,12},{12,8},{9,1... | collective-permute-start | bytes 12296 | tf_op jit(solution)/shard_map/ppermute | solution.py:252
  66.9 4.6 %collective-permute-start.21 = (f32[8,128]{1,0:T(8,128)S(1)}, f32[8,128]{1,0:T(8,128)S(1)}, u32[]{:S(2)}, u32[]{:S(2)}) collective-permute-start(f32[8,128]{1,0:T(8,128)S(1)} %shard_map.66.r0), channel_id=1, source_target_pairs={{0,33},{1,32},{32,1},{33,0},{2,35},{3,34},{34,3},{35,2},{4,37},{5,... | collective-permute-start | bytes 12296 | tf_op jit(solution)/shard_map/ppermute | solution.py:252
  68.0 3.6 %collective-permute-start.20 = (f32[8,128]{1,0:T(8,128)S(1)}, f32[8,128]{1,0:T(8,128)S(1)}, u32[]{:S(2)}, u32[]{:S(2)}) collective-permute-start(f32[8,128]{1,0:T(8,128)S(1)} %shard_map.66.r0), channel_id=1, source_target_pairs={{0,32},{32,0},{1,33},{33,1},{2,34},{34,2},{3,35},{35,3},{4,36},{36... | collective-permute-start | bytes 12296 | tf_op jit(solution)/shard_map/ppermute | solution.py:252
  70.0 3.6 %collective-permute-start.19 = (f32[8,128]{1,0:T(8,128)S(1)}, f32[8,128]{1,0:T(8,128)S(1)}, u32[]{:S(2)}, u32[]{:S(2)}) collective-permute-start(f32[8,128]{1,0:T(8,128)S(1)} %shard_map.66.r0), channel_id=1, source_target_pairs={{0,1},{1,0},{2,3},{3,2},{4,5},{5,4},{6,7},{7,6},{8,9},{9,8},{10,11... | collective-permute-start | bytes 12296 | tf_op jit(solution)/shard_map/ppermute | solution.py:252
  76.2 11.9 %collective-permute-start.22 = (bf16[512,512]{1,0:T(8,128)(2,1)S(1)}, bf16[512,512]{1,0:T(8,128)(2,1)S(1)}, u32[]{:S(2)}, u32[]{:S(2)}) collective-permute-start(bf16[512,512]{1,0:T(8,128)(2,1)S(1)} %shard_map.69), channel_id=1, source_target_pairs={{0,16},{16,0},{1,17},{17,1},{2,18},{18,2},{3,19},{19,3},{4,20},{20... | collective-permute-start | bytes 1572872 | tf_op jit(solution)/shard_map/ppermute | solution.py:252
  76.3 3.7 %collective-permute-start.25 = (f32[8,128]{1,0:T(8,128)S(1)}, f32[8,128]{1,0:T(8,128)S(1)}, u32[]{:S(2)}, u32[]{:S(2)}) collective-permute-start(f32[8,128]{1,0:T(8,128)S(1)} %get-tuple-element.40.c.c0), channel_id=1, source_target_pairs={{0,20},{4,16},{16,4},{20,0},{1,21},{5,17},{17,5},{21,1},{2,22},{6,... | collective-permute-start | bytes 12296 | tf_op jit(solution)/shard_map/ppermute | solution.py:252
  78.2 3.6 %collective-permute-start.23 = (f32[8,128]{1,0:T(8,128)S(1)}, f32[8,128]{1,0:T(8,128)S(1)}, u32[]{:S(2)}, u32[]{:S(2)}) collective-permute-start(f32[8,128]{1,0:T(8,128)S(1)} %get-tuple-element.40.c.c0), channel_id=1, source_target_pairs={{0,4},{4,0},{1,5},{5,1},{2,6},{6,2},{3,7},{7,3},{8,12},{12,8},{9,1... | collective-permute-start | bytes 12296 | tf_op jit(solution)/shard_map/ppermute | solution.py:252
  82.5 22.9 %collective-permute-start.27 = (bf16[256,512]{1,0:T(8,128)(2,1)S(1)}, bf16[256,512]{1,0:T(8,128)(2,1)S(1)}, u32[]{:S(2)}, u32[]{:S(2)}) collective-permute-start(bf16[256,512]{1,0:T(8,128)(2,1)S(1)} %get-tuple-element.44), channel_id=1, source_target_pairs={{0,1},{1,0},{2,3},{3,2},{4,5},{5,4},{6,7},{7,6},{8,9},{9,8},{10,11... | collective-permute-start | bytes 786440 | tf_op jit(solution)/shard_map/ppermute | solution.py:252
  84.2 21.3 %collective-permute-start.28 = (bf16[256,512]{1,0:T(8,128)(2,1)S(1)}, bf16[256,512]{1,0:T(8,128)(2,1)S(1)}, u32[]{:S(2)}, u32[]{:S(2)}) collective-permute-start(bf16[256,512]{1,0:T(8,128)(2,1)S(1)} %get-tuple-element.45), channel_id=1, source_target_pairs={{0,32},{32,0},{1,33},{33,1},{2,34},{34,2},{3,35},{35,3},{4,36},{36... | collective-permute-start | bytes 786440 | tf_op jit(solution)/shard_map/ppermute | solution.py:252
  85.2 20.2 %collective-permute-start.29 = (bf16[256,512]{1,0:T(8,128)(2,1)S(1)}, bf16[256,512]{1,0:T(8,128)(2,1)S(1)}, u32[]{:S(2)}, u32[]{:S(2)}) collective-permute-start(bf16[256,512]{1,0:T(8,128)(2,1)S(1)} %get-tuple-element.46), channel_id=1, source_target_pairs={{0,33},{1,32},{32,1},{33,0},{2,35},{3,34},{34,3},{35,2},{4,37},{5,... | collective-permute-start | bytes 786440 | tf_op jit(solution)/shard_map/ppermute | solution.py:252
  88.6 16.9 %collective-permute-start.26 = (bf16[256,512]{1,0:T(8,128)(2,1)S(1)}, bf16[256,512]{1,0:T(8,128)(2,1)S(1)}, u32[]{:S(2)}, u32[]{:S(2)}) collective-permute-start(bf16[256,512]{1,0:T(8,128)(2,1)S(1)} %get-tuple-element.42), channel_id=1, source_target_pairs={{0,4},{4,0},{1,5},{5,1},{2,6},{6,2},{3,7},{7,3},{8,12},{12,8},{9,1... | collective-permute-start | bytes 786440 | tf_op jit(solution)/shard_map/ppermute | solution.py:252
  89.0 9.3 %collective-permute-start.32 = (f32[8,128]{1,0:T(8,128)S(1)}, f32[8,128]{1,0:T(8,128)S(1)}, u32[]{:S(2)}, u32[]{:S(2)}) collective-permute-start(f32[8,128]{1,0:T(8,128)S(1)} %pad_maximum_fusion.r0), channel_id=1, source_target_pairs={{0,33},{1,32},{32,1},{33,0},{2,35},{3,34},{34,3},{35,2},{4,37},{5,... | collective-permute-start | bytes 12296 | tf_op jit(solution)/shard_map/ppermute | solution.py:252
  98.2 3.6 %collective-permute-start.31 = (f32[8,128]{1,0:T(8,128)S(1)}, f32[8,128]{1,0:T(8,128)S(1)}, u32[]{:S(2)}, u32[]{:S(2)}) collective-permute-start(f32[8,128]{1,0:T(8,128)S(1)} %pad_maximum_fusion.r0), channel_id=1, source_target_pairs={{0,32},{32,0},{1,33},{33,1},{2,34},{34,2},{3,35},{35,3},{4,36},{36... | collective-permute-start | bytes 12296 | tf_op jit(solution)/shard_map/ppermute | solution.py:252
  101.8 3.6 %collective-permute-start.30 = (f32[8,128]{1,0:T(8,128)S(1)}, f32[8,128]{1,0:T(8,128)S(1)}, u32[]{:S(2)}, u32[]{:S(2)}) collective-permute-start(f32[8,128]{1,0:T(8,128)S(1)} %pad_maximum_fusion.r0), channel_id=1, source_target_pairs={{0,1},{1,0},{2,3},{3,2},{4,5},{5,4},{6,7},{7,6},{8,9},{9,8},{10,11... | collective-permute-start | bytes 12296 | tf_op jit(solution)/shard_map/ppermute | solution.py:252
  (3 other events, 73.9 us)

commit v4 on v3

--- a/solution.py
+++ b/solution.py
@@ -19,7 +19,7 @@
 VMEM_LIMIT = 24 * 1024 * 1024
 LANES = 128
 STEP = 128
-SPLIT = ((3,), (1,), (2, 0))
+SPLIT = ((3,), (1,), (2,), (0,))
 
 
 def compact(columns):
@@ -135,11 +135,14 @@
     score_rows(scale, range(0, 3 * rows, STEP), x_ref, y_ref, line_ref, m_ref, lse_ref)
 
 
-def second_kernel(scale, ready, y_ref, line_ref, part_ref, sb, m_in, x_in, m_ref, x_ref, lse_ref):
-    half = sb.shape[0]
-    x_ref[ready : ready + half, :] = sb[...]
-    lse_ref[...] = part_ref[...]
-    score_rows(scale, range(ready, ready + half, STEP), x_ref, y_ref, line_ref, m_ref, lse_ref)
+def second_kernel(scale, y_ref, line_ref, part_ref, sa, sb, m_in, x_in, m_ref, x_ref, lse_ref):
+    half = sa.shape[0]
+    ready = 6 * half
+    x_ref[ready : ready + half, :] = sa[...]
+    x_ref[ready + half : ready + 2 * half, :] = sb[...]
+    lines = ready // LANES
+    lse_ref[0:lines, :] = part_ref[0:lines, :]
+    score_rows(scale, range(ready, ready + 2 * half, STEP), x_ref, y_ref, line_ref, m_ref, lse_ref)
 
 
 def row_kernel(log_mass, m_ref, c0, c1, c2, c3, lse_ref, row_ref):
@@ -337,17 +340,15 @@
         3 * flops // 4,
         area,
     )
-    row_part = part
-    for ready, block in ((3 * rows + half, s3b), (3 * rows, s3a)):
-        matrix, all_sources, row_part = call(
-            functools.partial(second_kernel, scale, ready),
-            [out((side, side), f32), out((side, width), bf16), out(tile, f32)],
-            [],
-            [all_targets, norms, row_part, block, matrix, all_sources],
-            flops // 8,
-            area // 8,
-            {4: 0, 5: 1},
-        )
+    matrix, all_sources, row_part = call(
+        functools.partial(second_kernel, scale),
+        [out((side, side), f32), out((side, width), bf16), out(tile, f32)],
+        [],
+        [all_targets, norms, part, s3a, s3b, matrix, all_sources],
+        flops // 4,
+        area // 4,
+        {5: 0, 6: 1},
+    )
 
     def exchange(value, slow, fast):
         both = swap(value, (slow, fast), ACROSS)

time: 121 us -> 120 us (level)
  waiting for transfers between devices: 37 us -> 32.8 us
  starting transfers between devices: 26.6 us -> 29.6 us
    ppermute x33, waiting for transfers between devices: 37 us -> 32.8 us  [swap(): return lax.ppermute(value, axis, pairs)]
    ppermute x33, starting transfers between devices: 26.6 us -> 29.6 us  [swap(): return lax.ppermute(value, axis, pairs)]
  transfers between devices with their start and end apart: 33 -> 33, of which waited for: 18 -> 20; matrix products, arithmetic and copies ran while one was open for 0% -> 0% of each run, Pallas kernels for 6% -> 6%
where the time goes in v4:
time: 120 us
  blocking collectives  37.2 us (31%)
  waiting for transfers between devices  32.8 us (27%)
  starting transfers between devices  29.6 us (25%)
  Pallas kernels  19 us (16%)
    all_to_all x2, blocking collectives, across(): lax.all_to_all(value, AXES, split_axis=0, concat_axis=0, axis_index_group...  37.2 us
    ppermute x33, waiting for transfers between devices, swap(): return lax.ppermute(value, axis, pairs)  32.8 us
    ppermute x33, starting transfers between devices, swap(): return lax.ppermute(value, axis, pairs)  29.6 us
    pallas_call x17, Pallas kernels, call(): pl.pallas_call(kernel, out_shape=outs, in_specs=[spec] * len(args), out_s...  19 us
  transfers between devices with their start and end apart: 33, of which 20 were waited for; matrix products, arithmetic and copies ran while one was open for 0% of the time, Pallas kernels for 6%

profile of v4, /device:TPU:0, one launch (start us, length us, event | category | flops | bytes accessed | tf_op | source)
XLA Modules:
  0.0 119.5 jit_solution(6169142473316451592)
XLA Ops:
  0.6 2.3 %shard_map.59 = bf16[8,64,512]{2,1,0:T(8,128)(2,1)} custom-call(s32[1,256]{1,0:T(1,128)} %bitcast.10, bf16[256,512]{1,0:T(8,128)(2,1)} %s_hbm.1, s32[1,256]{1,0:T(1,128)} %bitcast.12, bf16[256,512]{1,0:T(8,128)(2,1)} %t_hbm.1), custom_call_target="tpu_custom_call" | custom-call | bytes 4194304 | tf_op jit(solution)/shard_map/pallas_call | solution.py:295
  2.9 23.1 %all_to_all.10 = bf16[8,64,512]{2,1,0:T(8,128)(2,1)S(1)} all-to-all(bf16[8,64,512]{2,1,0:T(8,128)(2,1)} %shard_map.59), channel_id=1, replica_groups={{0,3,12,15,96,99,108,111},{1,2,13,14,97,98,109,110},{4,7,8,11,100,103,1..., dimensions={0} | all-to-all | bytes 1048576 | tf_op jit(solution)/shard_map/all_to_all | solution.py:276
  26.4 6.3 %collective-permute-done.2.t1 = bf16[256,512]{1,0:T(8,128)(2,1)S(1)} collective-permute-done((bf16[256,512]{1,0:T(8,128)(2,1)S(1)}, bf16[256,512]{1,0:T(8,128)(2,1)S(1)}, u32[]{:S(2)}, u32[]{:S(2)}) %collective-permute-start.2) | collective-permute-done | bytes 262176 | tf_op jit(solution)/shard_map/ppermute | solution.py:255
  32.9 1.8 %collective-permute-start.6 = (bf16[128,512]{1,0:T(8,128)(2,1)S(1)}, bf16[128,512]{1,0:T(8,128)(2,1)S(1)}, u32[]{:S(2)}, u32[]{:S(2)}) collective-permute-start(bf16[128,512]{1,0:T(8,128)(2,1)S(1)} %slice.27), channel_id=1, source_target_pairs={{0,32},{32,0},{1,33},{33,1},{2,34},{34,2},{3,35},{35,3},{4,36},{36... | collective-permute-start | bytes 393224 | tf_op jit(solution)/shard_map/ppermute | solution.py:255
  34.7 2.5 %shard_map.60 = (f32[1024,1024]{1,0:T(8,128)S(1)}, bf16[1024,512]{1,0:T(8,128)(2,1)S(1)}, bf16[1024,512]{1,0:T(8,128)(2,1)S(1)}, f32[8,128]{1,0:T(8,128)S(1)}, f32[1,1024]{1,0:T(1,128)S(1)}) custom-call(bf16[256,512]{1,0:T(8,128)(2,1)S(1)} %bitcast.9, bf16[256,512]{1,0:T(8,128)(2,1)S(1)} %collective-permute-done.s1, ...), custom_call_target="tpu_custom_call" | custom-call | flops 805306368 | bytes 4194304 | tf_op jit(solution)/shard_map/pallas_call | solution.py:295
  37.3 1.4 %collective-permute-done.5.sa = bf16[128,512]{1,0:T(8,128)(2,1)S(1)} collective-permute-done((bf16[128,512]{1,0:T(8,128)(2,1)S(1)}, bf16[128,512]{1,0:T(8,128)(2,1)S(1)}, u32[]{:S(2)}, u32[]{:S(2)}) %collective-permute-start.5) | collective-permute-done | bytes 131104 | tf_op jit(solution)/shard_map/ppermute | solution.py:255
  39.9 1.5 %collective-permute-start.9 = (f32[8,128]{1,0:T(8,128)S(1)}, f32[8,128]{1,0:T(8,128)S(1)}, u32[]{:S(2)}, u32[]{:S(2)}) collective-permute-start(f32[8,128]{1,0:T(8,128)S(1)} %get-tuple-element.31.r0), channel_id=1, source_target_pairs={{0,33},{1,32},{32,1},{33,0},{2,35},{3,34},{34,3},{35,2},{4,37},{5,... | collective-permute-start | bytes 12296 | tf_op jit(solution)/shard_map/ppermute | solution.py:255
  41.4 1.7 %collective-permute-start.8 = (f32[8,128]{1,0:T(8,128)S(1)}, f32[8,128]{1,0:T(8,128)S(1)}, u32[]{:S(2)}, u32[]{:S(2)}) collective-permute-start(f32[8,128]{1,0:T(8,128)S(1)} %get-tuple-element.31.r0), channel_id=1, source_target_pairs={{0,32},{32,0},{1,33},{33,1},{2,34},{34,2},{3,35},{35,3},{4,36},{36... | collective-permute-start | bytes 12296 | tf_op jit(solution)/shard_map/ppermute | solution.py:255
  45.0 1.7 %collective-permute-done.7.r1 = f32[8,128]{1,0:T(8,128)S(1)} collective-permute-done((f32[8,128]{1,0:T(8,128)S(1)}, f32[8,128]{1,0:T(8,128)S(1)}, u32[]{:S(2)}, u32[]{:S(2)}) %collective-permute-start.7) | collective-permute-done | bytes 4128 | tf_op jit(solution)/shard_map/ppermute | solution.py:255
  47.9 1.3 %collective-permute-start.11 = (f32[8,128]{1,0:T(8,128)S(1)}, f32[8,128]{1,0:T(8,128)S(1)}, u32[]{:S(2)}, u32[]{:S(2)}) collective-permute-start(f32[8,128]{1,0:T(8,128)S(1)} %get-tuple-element.32.c0), channel_id=1, source_target_pairs={{0,16},{16,0},{1,17},{17,1},{2,18},{18,2},{3,19},{19,3},{4,20},{20... | collective-permute-start | bytes 12296 | tf_op jit(solution)/shard_map/ppermute | solution.py:255
  51.0 1.9 %collective-permute-done.10.c1 = f32[8,128]{1,0:T(8,128)S(1)} collective-permute-done((f32[8,128]{1,0:T(8,128)S(1)}, f32[8,128]{1,0:T(8,128)S(1)}, u32[]{:S(2)}, u32[]{:S(2)}) %collective-permute-start.10) | collective-permute-done | bytes 4128 | tf_op jit(solution)/shard_map/ppermute | solution.py:255
  52.8 1.2 shard_map.63.r0
  54.0 2.8 %collective-permute-start.15 = (f32[8,128]{1,0:T(8,128)S(1)}, f32[8,128]{1,0:T(8,128)S(1)}, u32[]{:S(2)}, u32[]{:S(2)}) collective-permute-start(f32[8,128]{1,0:T(8,128)S(1)} %shard_map.63.r0), channel_id=1, source_target_pairs={{0,33},{1,32},{32,1},{33,0},{2,35},{3,34},{34,3},{35,2},{4,37},{5,... | collective-permute-start | bytes 12296 | tf_op jit(solution)/shard_map/ppermute | solution.py:255
  58.5 1.8 %collective-permute-done.14.r2 = f32[8,128]{1,0:T(8,128)S(1)} collective-permute-done((f32[8,128]{1,0:T(8,128)S(1)}, f32[8,128]{1,0:T(8,128)S(1)}, u32[]{:S(2)}, u32[]{:S(2)}) %collective-permute-start.14) | collective-permute-done | bytes 4128 | tf_op jit(solution)/shard_map/ppermute | solution.py:255
  61.7 2.0 %collective-permute-start.16 = (f32[8,128]{1,0:T(8,128)S(1)}, f32[8,128]{1,0:T(8,128)S(1)}, u32[]{:S(2)}, u32[]{:S(2)}) collective-permute-start(f32[8,128]{1,0:T(8,128)S(1)} %get-tuple-element.33.c0), channel_id=1, source_target_pairs={{0,4},{4,0},{1,5},{5,1},{2,6},{6,2},{3,7},{7,3},{8,12},{12,8},{9,1... | collective-permute-start | bytes 12296 | tf_op jit(solution)/shard_map/ppermute | solution.py:255
  65.5 1.2 shard_map.65.r0
  66.7 1.5 %collective-permute-start.21 = (f32[8,128]{1,0:T(8,128)S(1)}, f32[8,128]{1,0:T(8,128)S(1)}, u32[]{:S(2)}, u32[]{:S(2)}) collective-permute-start(f32[8,128]{1,0:T(8,128)S(1)} %shard_map.65.r0), channel_id=1, source_target_pairs={{0,33},{1,32},{32,1},{33,0},{2,35},{3,34},{34,3},{35,2},{4,37},{5,... | collective-permute-start | bytes 12296 | tf_op jit(solution)/shard_map/ppermute | solution.py:255
  68.2 1.4 %collective-permute-start.20 = (f32[8,128]{1,0:T(8,128)S(1)}, f32[8,128]{1,0:T(8,128)S(1)}, u32[]{:S(2)}, u32[]{:S(2)}) collective-permute-start(f32[8,128]{1,0:T(8,128)S(1)} %shard_map.65.r0), channel_id=1, source_target_pairs={{0,32},{32,0},{1,33},{33,1},{2,34},{34,2},{3,35},{35,3},{4,36},{36... | collective-permute-start | bytes 12296 | tf_op jit(solution)/shard_map/ppermute | solution.py:255
  71.8 1.4 %collective-permute-done.19.r1 = f32[8,128]{1,0:T(8,128)S(1)} collective-permute-done((f32[8,128]{1,0:T(8,128)S(1)}, f32[8,128]{1,0:T(8,128)S(1)}, u32[]{:S(2)}, u32[]{:S(2)}) %collective-permute-start.19) | collective-permute-done | bytes 4128 | tf_op jit(solution)/shard_map/ppermute | solution.py:255
  74.2 1.4 %shard_map.68 = bf16[512,512]{1,0:T(8,128)(2,1)S(1)} custom-call(f32[1024,1024]{1,0:T(8,128)S(1)} %get-tuple-element.29.m_ref, bf16[1024,512]{1,0:T(8,128)(2,1)S(1)} %get-tuple-element.30.x_ref, f32[8,128]{1,0:T(8,128)S(1)} %get-tuple-element.34.f, f32[8,128]{1,0:T(8,128)S(1)} %get-tuple-element.35.c.c0), custom_call_target="tpu_custom_call" | custom-call | flops 536870912 | bytes 4194304 | tf_op jit(solution)/shard_map/pallas_call | solution.py:295
  75.8 1.3 %collective-permute-start.25 = (f32[8,128]{1,0:T(8,128)S(1)}, f32[8,128]{1,0:T(8,128)S(1)}, u32[]{:S(2)}, u32[]{:S(2)}) collective-permute-start(f32[8,128]{1,0:T(8,128)S(1)} %get-tuple-element.35.c.c0), channel_id=1, source_target_pairs={{0,20},{4,16},{16,4},{20,0},{1,21},{5,17},{17,5},{21,1},{2,22},{6,... | collective-permute-start | bytes 12296 | tf_op jit(solution)/shard_map/ppermute | solution.py:255
  78.0 1.4 %shard_map.67.p_ref = bf16[512,512]{1,0:T(8,128)(2,1)S(1)} custom-call(f32[1024,1024]{1,0:T(8,128)S(1)} %get-tuple-element.29.m_ref, bf16[1024,512]{1,0:T(8,128)(2,1)S(1)} %get-tuple-element.30.x_ref, f32[8,128]{1,0:T(8,128)S(1)} %get-tuple-element.34.f, f32[8,128]{1,0:T(8,128)S(1)} %get-tuple-element.35.c.c0), custom_call_target="tpu_custom_call" | custom-call | flops 536870912 | bytes 4194304 | tf_op jit(solution)/shard_map/pallas_call | solution.py:295
  79.5 1.3 %collective-permute-done.23.c1 = f32[8,128]{1,0:T(8,128)S(1)} collective-permute-done((f32[8,128]{1,0:T(8,128)S(1)}, f32[8,128]{1,0:T(8,128)S(1)}, u32[]{:S(2)}, u32[]{:S(2)}) %collective-permute-start.23) | collective-permute-done | bytes 4128 | tf_op jit(solution)/shard_map/ppermute | solution.py:255
  81.4 1.3 %collective-permute-start.27 = (bf16[256,512]{1,0:T(8,128)(2,1)S(1)}, bf16[256,512]{1,0:T(8,128)(2,1)S(1)}, u32[]{:S(2)}, u32[]{:S(2)}) collective-permute-start(bf16[256,512]{1,0:T(8,128)(2,1)S(1)} %get-tuple-element.39), channel_id=1, source_target_pairs={{0,1},{1,0},{2,3},{3,2},{4,5},{5,4},{6,7},{7,6},{8,9},{9,8},{10,11... | collective-permute-start | bytes 786440 | tf_op jit(solution)/shard_map/ppermute | solution.py:255
  83.4 2.1 %collective-permute-start.28 = (bf16[256,512]{1,0:T(8,128)(2,1)S(1)}, bf16[256,512]{1,0:T(8,128)(2,1)S(1)}, u32[]{:S(2)}, u32[]{:S(2)}) collective-permute-start(bf16[256,512]{1,0:T(8,128)(2,1)S(1)} %get-tuple-element.40), channel_id=1, source_target_pairs={{0,32},{32,0},{1,33},{33,1},{2,34},{34,2},{3,35},{35,3},{4,36},{36... | collective-permute-start | bytes 786440 | tf_op jit(solution)/shard_map/ppermute | solution.py:255
  88.5 2.2 %collective-permute-start.32 = (f32[8,128]{1,0:T(8,128)S(1)}, f32[8,128]{1,0:T(8,128)S(1)}, u32[]{:S(2)}, u32[]{:S(2)}) collective-permute-start(f32[8,128]{1,0:T(8,128)S(1)} %pad_maximum_fusion.r0), channel_id=1, source_target_pairs={{0,33},{1,32},{32,1},{33,0},{2,35},{3,34},{34,3},{35,2},{4,37},{5,... | collective-permute-start | bytes 12296 | tf_op jit(solution)/shard_map/ppermute | solution.py:255
  90.7 5.8 %collective-permute-done.32.r3 = f32[8,128]{1,0:T(8,128)S(1)} collective-permute-done((f32[8,128]{1,0:T(8,128)S(1)}, f32[8,128]{1,0:T(8,128)S(1)}, u32[]{:S(2)}, u32[]{:S(2)}) %collective-permute-start.32) | collective-permute-done | bytes 4128 | tf_op jit(solution)/shard_map/ppermute | solution.py:255
  96.6 1.6 %collective-permute-start.31 = (f32[8,128]{1,0:T(8,128)S(1)}, f32[8,128]{1,0:T(8,128)S(1)}, u32[]{:S(2)}, u32[]{:S(2)}) collective-permute-start(f32[8,128]{1,0:T(8,128)S(1)} %pad_maximum_fusion.r0), channel_id=1, source_target_pairs={{0,32},{32,0},{1,33},{33,1},{2,34},{34,2},{3,35},{35,3},{4,36},{36... | collective-permute-start | bytes 12296 | tf_op jit(solution)/shard_map/ppermute | solution.py:255
  98.1 2.0 %collective-permute-done.31.r2 = f32[8,128]{1,0:T(8,128)S(1)} collective-permute-done((f32[8,128]{1,0:T(8,128)S(1)}, f32[8,128]{1,0:T(8,128)S(1)}, u32[]{:S(2)}, u32[]{:S(2)}) %collective-permute-start.31) | collective-permute-done | bytes 4128 | tf_op jit(solution)/shard_map/ppermute | solution.py:255
  100.2 1.5 %collective-permute-start.30 = (f32[8,128]{1,0:T(8,128)S(1)}, f32[8,128]{1,0:T(8,128)S(1)}, u32[]{:S(2)}, u32[]{:S(2)}) collective-permute-start(f32[8,128]{1,0:T(8,128)S(1)} %pad_maximum_fusion.r0), channel_id=1, source_target_pairs={{0,1},{1,0},{2,3},{3,2},{4,5},{5,4},{6,7},{7,6},{8,9},{9,8},{10,11... | collective-permute-start | bytes 12296 | tf_op jit(solution)/shard_map/ppermute | solution.py:255
  101.7 2.1 %collective-permute-done.30.r1 = f32[8,128]{1,0:T(8,128)S(1)} collective-permute-done((f32[8,128]{1,0:T(8,128)S(1)}, f32[8,128]{1,0:T(8,128)S(1)}, u32[]{:S(2)}, u32[]{:S(2)}) %collective-permute-start.30) | collective-permute-done | bytes 4128 | tf_op jit(solution)/shard_map/ppermute | solution.py:255
  104.4 14.1 %all_to_all.11.back_ref = bf16[8,64,512]{2,1,0:T(8,128)(2,1)S(1)} all-to-all(bf16[8,64,512]{2,1,0:T(8,128)(2,1)S(1)} %shard_map.74), channel_id=1, replica_groups={{0,3,12,15,96,99,108,111},{1,2,13,14,97,98,109,110},{4,7,8,11,100,103,1..., dimensions={0} | all-to-all | bytes 1048576 | tf_op jit(solution)/shard_map/all_to_all | solution.py:276
  (61 shorter events, 21.8 us)
Async XLA Ops:
  26.1 6.6 %collective-permute-start.2 = (bf16[256,512]{1,0:T(8,128)(2,1)S(1)}, bf16[256,512]{1,0:T(8,128)(2,1)S(1)}, u32[]{:S(2)}, u32[]{:S(2)}) collective-permute-start(bf16[256,512]{1,0:T(8,128)(2,1)S(1)} %bitcast.4), channel_id=1, source_target_pairs={{0,4},{4,0},{1,5},{5,1},{2,6},{6,2},{3,7},{7,3},{8,12},{12,8},{9,1... | collective-permute-start | bytes 786440 | tf_op jit(solution)/shard_map/ppermute | solution.py:255
  26.2 6.6 %collective-permute-start.1 = (bf16[256,512]{1,0:T(8,128)(2,1)S(1)}, bf16[256,512]{1,0:T(8,128)(2,1)S(1)}, u32[]{:S(2)}, u32[]{:S(2)}) collective-permute-start(bf16[256,512]{1,0:T(8,128)(2,1)S(1)} %bitcast.7), channel_id=1, source_target_pairs={{0,32},{32,0},{1,33},{33,1},{2,34},{34,2},{3,35},{35,3},{4,36},{36... | collective-permute-start | bytes 786440 | tf_op jit(solution)/shard_map/ppermute | solution.py:255
  26.2 6.6 %collective-permute-start = (bf16[256,512]{1,0:T(8,128)(2,1)S(1)}, bf16[256,512]{1,0:T(8,128)(2,1)S(1)}, u32[]{:S(2)}, u32[]{:S(2)}) collective-permute-start(bf16[256,512]{1,0:T(8,128)(2,1)S(1)} %bitcast.8), channel_id=1, source_target_pairs={{0,1},{1,0},{2,3},{3,2},{4,5},{5,4},{6,7},{7,6},{8,9},{9,8},{10,11... | collective-permute-start | bytes 786440 | tf_op jit(solution)/shard_map/ppermute | solution.py:255
  26.3 8.4 %collective-permute-start.3 = (bf16[256,512]{1,0:T(8,128)(2,1)S(1)}, bf16[256,512]{1,0:T(8,128)(2,1)S(1)}, u32[]{:S(2)}, u32[]{:S(2)}) collective-permute-start(bf16[256,512]{1,0:T(8,128)(2,1)S(1)} %bitcast.5), channel_id=1, source_target_pairs={{0,16},{16,0},{1,17},{17,1},{2,18},{18,2},{3,19},{19,3},{4,20},{20... | collective-permute-start | bytes 786440 | tf_op jit(solution)/shard_map/ppermute | solution.py:255
  32.8 5.9 %collective-permute-start.5 = (bf16[128,512]{1,0:T(8,128)(2,1)S(1)}, bf16[128,512]{1,0:T(8,128)(2,1)S(1)}, u32[]{:S(2)}, u32[]{:S(2)}) collective-permute-start(bf16[128,512]{1,0:T(8,128)(2,1)S(1)} %slice.26), channel_id=1, source_target_pairs={{0,1},{1,0},{2,3},{3,2},{4,5},{5,4},{6,7},{7,6},{8,9},{9,8},{10,11... | collective-permute-start | bytes 393224 | tf_op jit(solution)/shard_map/ppermute | solution.py:255
  32.9 5.9 %collective-permute-start.6 = (bf16[128,512]{1,0:T(8,128)(2,1)S(1)}, bf16[128,512]{1,0:T(8,128)(2,1)S(1)}, u32[]{:S(2)}, u32[]{:S(2)}) collective-permute-start(bf16[128,512]{1,0:T(8,128)(2,1)S(1)} %slice.27), channel_id=1, source_target_pairs={{0,32},{32,0},{1,33},{33,1},{2,34},{34,2},{3,35},{35,3},{4,36},{36... | collective-permute-start | bytes 393224 | tf_op jit(solution)/shard_map/ppermute | solution.py:255
  39.9 4.6 %collective-permute-start.9 = (f32[8,128]{1,0:T(8,128)S(1)}, f32[8,128]{1,0:T(8,128)S(1)}, u32[]{:S(2)}, u32[]{:S(2)}) collective-permute-start(f32[8,128]{1,0:T(8,128)S(1)} %get-tuple-element.31.r0), channel_id=1, source_target_pairs={{0,33},{1,32},{32,1},{33,0},{2,35},{3,34},{34,3},{35,2},{4,37},{5,... | collective-permute-start | bytes 12296 | tf_op jit(solution)/shard_map/ppermute | solution.py:255
  41.4 3.6 %collective-permute-start.8 = (f32[8,128]{1,0:T(8,128)S(1)}, f32[8,128]{1,0:T(8,128)S(1)}, u32[]{:S(2)}, u32[]{:S(2)}) collective-permute-start(f32[8,128]{1,0:T(8,128)S(1)} %get-tuple-element.31.r0), channel_id=1, source_target_pairs={{0,32},{32,0},{1,33},{33,1},{2,34},{34,2},{3,35},{35,3},{4,36},{36... | collective-permute-start | bytes 12296 | tf_op jit(solution)/shard_map/ppermute | solution.py:255
  43.1 3.6 %collective-permute-start.7 = (f32[8,128]{1,0:T(8,128)S(1)}, f32[8,128]{1,0:T(8,128)S(1)}, u32[]{:S(2)}, u32[]{:S(2)}) collective-permute-start(f32[8,128]{1,0:T(8,128)S(1)} %get-tuple-element.31.r0), channel_id=1, source_target_pairs={{0,1},{1,0},{2,3},{3,2},{4,5},{5,4},{6,7},{7,6},{8,9},{9,8},{10,11... | collective-permute-start | bytes 12296 | tf_op jit(solution)/shard_map/ppermute | solution.py:255
  47.8 3.1 %collective-permute-start.12 = (f32[8,128]{1,0:T(8,128)S(1)}, f32[8,128]{1,0:T(8,128)S(1)}, u32[]{:S(2)}, u32[]{:S(2)}) collective-permute-start(f32[8,128]{1,0:T(8,128)S(1)} %get-tuple-element.32.c0), channel_id=1, source_target_pairs={{0,20},{4,16},{16,4},{20,0},{1,21},{5,17},{17,5},{21,1},{2,22},{6,... | collective-permute-start | bytes 12296 | tf_op jit(solution)/shard_map/ppermute | solution.py:255
  47.9 3.0 %collective-permute-start.11 = (f32[8,128]{1,0:T(8,128)S(1)}, f32[8,128]{1,0:T(8,128)S(1)}, u32[]{:S(2)}, u32[]{:S(2)}) collective-permute-start(f32[8,128]{1,0:T(8,128)S(1)} %get-tuple-element.32.c0), channel_id=1, source_target_pairs={{0,16},{16,0},{1,17},{17,1},{2,18},{18,2},{3,19},{19,3},{4,20},{20... | collective-permute-start | bytes 12296 | tf_op jit(solution)/shard_map/ppermute | solution.py:255
  49.2 3.6 %collective-permute-start.10 = (f32[8,128]{1,0:T(8,128)S(1)}, f32[8,128]{1,0:T(8,128)S(1)}, u32[]{:S(2)}, u32[]{:S(2)}) collective-permute-start(f32[8,128]{1,0:T(8,128)S(1)} %get-tuple-element.32.c0), channel_id=1, source_target_pairs={{0,4},{4,0},{1,5},{5,1},{2,6},{6,2},{3,7},{7,3},{8,12},{12,8},{9,1... | collective-permute-start | bytes 12296 | tf_op jit(solution)/shard_map/ppermute | solution.py:255
  54.0 4.6 %collective-permute-start.15 = (f32[8,128]{1,0:T(8,128)S(1)}, f32[8,128]{1,0:T(8,128)S(1)}, u32[]{:S(2)}, u32[]{:S(2)}) collective-permute-start(f32[8,128]{1,0:T(8,128)S(1)} %shard_map.63.r0), channel_id=1, source_target_pairs={{0,33},{1,32},{32,1},{33,0},{2,35},{3,34},{34,3},{35,2},{4,37},{5,... | collective-permute-start | bytes 12296 | tf_op jit(solution)/shard_map/ppermute | solution.py:255
  56.7 3.6 %collective-permute-start.14 = (f32[8,128]{1,0:T(8,128)S(1)}, f32[8,128]{1,0:T(8,128)S(1)}, u32[]{:S(2)}, u32[]{:S(2)}) collective-permute-start(f32[8,128]{1,0:T(8,128)S(1)} %shard_map.63.r0), channel_id=1, source_target_pairs={{0,32},{32,0},{1,33},{33,1},{2,34},{34,2},{3,35},{35,3},{4,36},{36... | collective-permute-start | bytes 12296 | tf_op jit(solution)/shard_map/ppermute | solution.py:255
  56.8 3.6 %collective-permute-start.13 = (f32[8,128]{1,0:T(8,128)S(1)}, f32[8,128]{1,0:T(8,128)S(1)}, u32[]{:S(2)}, u32[]{:S(2)}) collective-permute-start(f32[8,128]{1,0:T(8,128)S(1)} %shard_map.63.r0), channel_id=1, source_target_pairs={{0,1},{1,0},{2,3},{3,2},{4,5},{5,4},{6,7},{7,6},{8,9},{9,8},{10,11... | collective-permute-start | bytes 12296 | tf_op jit(solution)/shard_map/ppermute | solution.py:255
  61.5 3.1 %collective-permute-start.18 = (f32[8,128]{1,0:T(8,128)S(1)}, f32[8,128]{1,0:T(8,128)S(1)}, u32[]{:S(2)}, u32[]{:S(2)}) collective-permute-start(f32[8,128]{1,0:T(8,128)S(1)} %get-tuple-element.33.c0), channel_id=1, source_target_pairs={{0,20},{4,16},{16,4},{20,0},{1,21},{5,17},{17,5},{21,1},{2,22},{6,... | collective-permute-start | bytes 12296 | tf_op jit(solution)/shard_map/ppermute | solution.py:255
  61.6 3.0 %collective-permute-start.17 = (f32[8,128]{1,0:T(8,128)S(1)}, f32[8,128]{1,0:T(8,128)S(1)}, u32[]{:S(2)}, u32[]{:S(2)}) collective-permute-start(f32[8,128]{1,0:T(8,128)S(1)} %get-tuple-element.33.c0), channel_id=1, source_target_pairs={{0,16},{16,0},{1,17},{17,1},{2,18},{18,2},{3,19},{19,3},{4,20},{20... | collective-permute-start | bytes 12296 | tf_op jit(solution)/shard_map/ppermute | solution.py:255
  61.7 3.8 %collective-permute-start.16 = (f32[8,128]{1,0:T(8,128)S(1)}, f32[8,128]{1,0:T(8,128)S(1)}, u32[]{:S(2)}, u32[]{:S(2)}) collective-permute-start(f32[8,128]{1,0:T(8,128)S(1)} %get-tuple-element.33.c0), channel_id=1, source_target_pairs={{0,4},{4,0},{1,5},{5,1},{2,6},{6,2},{3,7},{7,3},{8,12},{12,8},{9,1... | collective-permute-start | bytes 12296 | tf_op jit(solution)/shard_map/ppermute | solution.py:255
  66.7 4.6 %collective-permute-start.21 = (f32[8,128]{1,0:T(8,128)S(1)}, f32[8,128]{1,0:T(8,128)S(1)}, u32[]{:S(2)}, u32[]{:S(2)}) collective-permute-start(f32[8,128]{1,0:T(8,128)S(1)} %shard_map.65.r0), channel_id=1, source_target_pairs={{0,33},{1,32},{32,1},{33,0},{2,35},{3,34},{34,3},{35,2},{4,37},{5,... | collective-permute-start | bytes 12296 | tf_op jit(solution)/shard_map/ppermute | solution.py:255
  68.2 3.6 %collective-permute-start.20 = (f32[8,128]{1,0:T(8,128)S(1)}, f32[8,128]{1,0:T(8,128)S(1)}, u32[]{:S(2)}, u32[]{:S(2)}) collective-permute-start(f32[8,128]{1,0:T(8,128)S(1)} %shard_map.65.r0), channel_id=1, source_target_pairs={{0,32},{32,0},{1,33},{33,1},{2,34},{34,2},{3,35},{35,3},{4,36},{36... | collective-permute-start | bytes 12296 | tf_op jit(solution)/shard_map/ppermute | solution.py:255
  69.5 3.6 %collective-permute-start.19 = (f32[8,128]{1,0:T(8,128)S(1)}, f32[8,128]{1,0:T(8,128)S(1)}, u32[]{:S(2)}, u32[]{:S(2)}) collective-permute-start(f32[8,128]{1,0:T(8,128)S(1)} %shard_map.65.r0), channel_id=1, source_target_pairs={{0,1},{1,0},{2,3},{3,2},{4,5},{5,4},{6,7},{7,6},{8,9},{9,8},{10,11... | collective-permute-start | bytes 12296 | tf_op jit(solution)/shard_map/ppermute | solution.py:255
  75.7 10.7 %collective-permute-start.22 = (bf16[512,512]{1,0:T(8,128)(2,1)S(1)}, bf16[512,512]{1,0:T(8,128)(2,1)S(1)}, u32[]{:S(2)}, u32[]{:S(2)}) collective-permute-start(bf16[512,512]{1,0:T(8,128)(2,1)S(1)} %shard_map.68), channel_id=1, source_target_pairs={{0,16},{16,0},{1,17},{17,1},{2,18},{18,2},{3,19},{19,3},{4,20},{20... | collective-permute-start | bytes 1572872 | tf_op jit(solution)/shard_map/ppermute | solution.py:255
  75.8 3.7 %collective-permute-start.25 = (f32[8,128]{1,0:T(8,128)S(1)}, f32[8,128]{1,0:T(8,128)S(1)}, u32[]{:S(2)}, u32[]{:S(2)}) collective-permute-start(f32[8,128]{1,0:T(8,128)S(1)} %get-tuple-element.35.c.c0), channel_id=1, source_target_pairs={{0,20},{4,16},{16,4},{20,0},{1,21},{5,17},{17,5},{21,1},{2,22},{6,... | collective-permute-start | bytes 12296 | tf_op jit(solution)/shard_map/ppermute | solution.py:255
  77.1 2.4 %collective-permute-start.24 = (f32[8,128]{1,0:T(8,128)S(1)}, f32[8,128]{1,0:T(8,128)S(1)}, u32[]{:S(2)}, u32[]{:S(2)}) collective-permute-start(f32[8,128]{1,0:T(8,128)S(1)} %get-tuple-element.35.c.c0), channel_id=1, source_target_pairs={{0,16},{16,0},{1,17},{17,1},{2,18},{18,2},{3,19},{19,3},{4,20},{20... | collective-permute-start | bytes 12296 | tf_op jit(solution)/shard_map/ppermute | solution.py:255
  77.2 3.6 %collective-permute-start.23 = (f32[8,128]{1,0:T(8,128)S(1)}, f32[8,128]{1,0:T(8,128)S(1)}, u32[]{:S(2)}, u32[]{:S(2)}) collective-permute-start(f32[8,128]{1,0:T(8,128)S(1)} %get-tuple-element.35.c.c0), channel_id=1, source_target_pairs={{0,4},{4,0},{1,5},{5,1},{2,6},{6,2},{3,7},{7,3},{8,12},{12,8},{9,1... | collective-permute-start | bytes 12296 | tf_op jit(solution)/shard_map/ppermute | solution.py:255
  81.4 22.4 %collective-permute-start.27 = (bf16[256,512]{1,0:T(8,128)(2,1)S(1)}, bf16[256,512]{1,0:T(8,128)(2,1)S(1)}, u32[]{:S(2)}, u32[]{:S(2)}) collective-permute-start(bf16[256,512]{1,0:T(8,128)(2,1)S(1)} %get-tuple-element.39), channel_id=1, source_target_pairs={{0,1},{1,0},{2,3},{3,2},{4,5},{5,4},{6,7},{7,6},{8,9},{9,8},{10,11... | collective-permute-start | bytes 786440 | tf_op jit(solution)/shard_map/ppermute | solution.py:255
  83.4 20.4 %collective-permute-start.28 = (bf16[256,512]{1,0:T(8,128)(2,1)S(1)}, bf16[256,512]{1,0:T(8,128)(2,1)S(1)}, u32[]{:S(2)}, u32[]{:S(2)}) collective-permute-start(bf16[256,512]{1,0:T(8,128)(2,1)S(1)} %get-tuple-element.40), channel_id=1, source_target_pairs={{0,32},{32,0},{1,33},{33,1},{2,34},{34,2},{3,35},{35,3},{4,36},{36... | collective-permute-start | bytes 786440 | tf_op jit(solution)/shard_map/ppermute | solution.py:255
  86.1 17.7 %collective-permute-start.29 = (bf16[256,512]{1,0:T(8,128)(2,1)S(1)}, bf16[256,512]{1,0:T(8,128)(2,1)S(1)}, u32[]{:S(2)}, u32[]{:S(2)}) collective-permute-start(bf16[256,512]{1,0:T(8,128)(2,1)S(1)} %get-tuple-element.41), channel_id=1, source_target_pairs={{0,33},{1,32},{32,1},{33,0},{2,35},{3,34},{34,3},{35,2},{4,37},{5,... | collective-permute-start | bytes 786440 | tf_op jit(solution)/shard_map/ppermute | solution.py:255
  86.9 16.9 %collective-permute-start.26 = (bf16[256,512]{1,0:T(8,128)(2,1)S(1)}, bf16[256,512]{1,0:T(8,128)(2,1)S(1)}, u32[]{:S(2)}, u32[]{:S(2)}) collective-permute-start(bf16[256,512]{1,0:T(8,128)(2,1)S(1)} %get-tuple-element.37), channel_id=1, source_target_pairs={{0,4},{4,0},{1,5},{5,1},{2,6},{6,2},{3,7},{7,3},{8,12},{12,8},{9,1... | collective-permute-start | bytes 786440 | tf_op jit(solution)/shard_map/ppermute | solution.py:255
  88.5 8.1 %collective-permute-start.32 = (f32[8,128]{1,0:T(8,128)S(1)}, f32[8,128]{1,0:T(8,128)S(1)}, u32[]{:S(2)}, u32[]{:S(2)}) collective-permute-start(f32[8,128]{1,0:T(8,128)S(1)} %pad_maximum_fusion.r0), channel_id=1, source_target_pairs={{0,33},{1,32},{32,1},{33,0},{2,35},{3,34},{34,3},{35,2},{4,37},{5,... | collective-permute-start | bytes 12296 | tf_op jit(solution)/shard_map/ppermute | solution.py:255
  96.6 3.6 %collective-permute-start.31 = (f32[8,128]{1,0:T(8,128)S(1)}, f32[8,128]{1,0:T(8,128)S(1)}, u32[]{:S(2)}, u32[]{:S(2)}) collective-permute-start(f32[8,128]{1,0:T(8,128)S(1)} %pad_maximum_fusion.r0), channel_id=1, source_target_pairs={{0,32},{32,0},{1,33},{33,1},{2,34},{34,2},{3,35},{35,3},{4,36},{36... | collective-permute-start | bytes 12296 | tf_op jit(solution)/shard_map/ppermute | solution.py:255
  100.2 3.6 %collective-permute-start.30 = (f32[8,128]{1,0:T(8,128)S(1)}, f32[8,128]{1,0:T(8,128)S(1)}, u32[]{:S(2)}, u32[]{:S(2)}) collective-permute-start(f32[8,128]{1,0:T(8,128)S(1)} %pad_maximum_fusion.r0), channel_id=1, source_target_pairs={{0,1},{1,0},{2,3},{3,2},{4,5},{5,4},{6,7},{7,6},{8,9},{9,8},{10,11... | collective-permute-start | bytes 12296 | tf_op jit(solution)/shard_map/ppermute | solution.py:255
  (3 other events, 65.3 us)

commit v5 on v4

--- a/solution.py
+++ b/solution.py
@@ -125,11 +125,11 @@
     lse_ref[first : first + len(found), :] = compact(found)
 
 
-def first_kernel(scale, s0, s1, s2, t0, t1, t2, t3, m_ref, x_ref, y_ref, lse_ref, line_ref):
+def first_kernel(scale, s0, s1, s2, t0, t1, t23, m_ref, x_ref, y_ref, lse_ref, line_ref):
     rows = s0.shape[0]
     for q, s in enumerate((s0, s1, s2)):
         x_ref[q * rows : (q + 1) * rows, :] = s[...]
-    for q, t in enumerate((t0, t1, t2, t3)):
+    for q, t in enumerate((t0, t1, t23.at[pl.ds(0, rows)], t23.at[pl.ds(rows, rows)])):
         y_ref[q * rows : (q + 1) * rows, :] = t[...]
         target_norms(line_ref, t, q * rows)
     score_rows(scale, range(0, 3 * rows, STEP), x_ref, y_ref, line_ref, m_ref, lse_ref)
@@ -328,15 +328,14 @@
     s1 = swap(mine, "yl")
     s2 = swap(mine, "xl")
     t1 = swap(aims, "zl")
-    t2 = swap(aims, "core")
-    t3 = swap(t1, "core")
+    t23 = swap(jnp.concatenate([aims, t1], axis=0), "core")
     s3a = swap(s2[:half], "yl")
     s3b = swap(s1[half:], "xl")
     matrix, all_sources, all_targets, part, norms = call(
         functools.partial(first_kernel, scale),
         [out((side, side), f32), out((side, width), bf16), out((side, width), bf16), out(tile, f32), out((1, side), f32)],
         [],
-        [mine, s1, s2, aims, t1, t2, t3],
+        [mine, s1, s2, aims, t1, t23],
         3 * flops // 4,
         area,
     )

time: 120 us -> 128 us (1.067)
  waiting for transfers between devices: 32.8 us -> 43.3 us
  starting transfers between devices: 29.6 us -> 26.8 us
    ppermute x33 -> x32, waiting for transfers between devices: 32.8 us -> 43.3 us  [swap(): return lax.ppermute(value, axis, pairs)]
    ppermute x33 -> x32, starting transfers between devices: 29.6 us -> 26.8 us  [swap(): return lax.ppermute(value, axis, pairs)]
  transfers between devices with their start and end apart: 33 -> 32, of which waited for: 20 -> 21; matrix products, arithmetic and copies ran while one was open for 0% -> 0% of each run, Pallas kernels for 6% -> 6%
where the time goes in v5:
time: 128 us; the launch traced here: 127 us
  waiting for transfers between devices  43.3 us (34%)
  blocking collectives  37.2 us (29%)
  starting transfers between devices  26.8 us (21%)
  Pallas kernels  19.2 us (15%)
    ppermute x32, waiting for transfers between devices, swap(): return lax.ppermute(value, axis, pairs)  43.3 us
    all_to_all x2, blocking collectives, across(): lax.all_to_all(value, AXES, split_axis=0, concat_axis=0, axis_index_group...  37.2 us
    ppermute x32, starting transfers between devices, swap(): return lax.ppermute(value, axis, pairs)  26.8 us
    pallas_call x17, Pallas kernels, call(): pl.pallas_call(kernel, out_shape=outs, in_specs=[spec] * len(args), out_s...  19.2 us
  transfers between devices with their start and end apart: 32, of which 21 were waited for; matrix products, arithmetic and copies ran while one was open for 0% of the time, Pallas kernels for 6%

profile of v5, /device:TPU:0, one launch (start us, length us, event | category | flops | bytes accessed | tf_op | source)
XLA Modules:
  0.0 127.4 jit_solution(6726606596495710653)
XLA Ops:
  0.6 2.3 %shard_map.59 = bf16[8,64,512]{2,1,0:T(8,128)(2,1)} custom-call(s32[1,256]{1,0:T(1,128)} %bitcast.10, bf16[256,512]{1,0:T(8,128)(2,1)} %s_hbm.1, s32[1,256]{1,0:T(1,128)} %bitcast.12, bf16[256,512]{1,0:T(8,128)(2,1)} %t_hbm.1), custom_call_target="tpu_custom_call" | custom-call | bytes 4194304 | tf_op jit(solution)/shard_map/pallas_call | solution.py:295
  2.9 23.1 %all_to_all.10 = bf16[8,64,512]{2,1,0:T(8,128)(2,1)S(1)} all-to-all(bf16[8,64,512]{2,1,0:T(8,128)(2,1)} %shard_map.59), channel_id=1, replica_groups={{0,3,12,15,96,99,108,111},{1,2,13,14,97,98,109,110},{4,7,8,11,100,103,1..., dimensions={0} | all-to-all | bytes 1048576 | tf_op jit(solution)/shard_map/all_to_all | solution.py:276
  26.2 6.5 %collective-permute-done.2.t1 = bf16[256,512]{1,0:T(8,128)(2,1)S(1)} collective-permute-done((bf16[256,512]{1,0:T(8,128)(2,1)S(1)}, bf16[256,512]{1,0:T(8,128)(2,1)S(1)}, u32[]{:S(2)}, u32[]{:S(2)}) %collective-permute-start.2) | collective-permute-done | bytes 262176 | tf_op jit(solution)/shard_map/ppermute | solution.py:255
  33.0 8.5 %collective-permute-done.1.s2 = bf16[256,512]{1,0:T(8,128)(2,1)S(1)} collective-permute-done((bf16[256,512]{1,0:T(8,128)(2,1)S(1)}, bf16[256,512]{1,0:T(8,128)(2,1)S(1)}, u32[]{:S(2)}, u32[]{:S(2)}) %collective-permute-start.1) | collective-permute-done | bytes 262176 | tf_op jit(solution)/shard_map/ppermute | solution.py:255
  41.7 1.7 %collective-permute-start.5 = (bf16[128,512]{1,0:T(8,128)(2,1)S(1)}, bf16[128,512]{1,0:T(8,128)(2,1)S(1)}, u32[]{:S(2)}, u32[]{:S(2)}) collective-permute-start(bf16[128,512]{1,0:T(8,128)(2,1)S(1)} %slice.27), channel_id=1, source_target_pairs={{0,32},{32,0},{1,33},{33,1},{2,34},{34,2},{3,35},{35,3},{4,36},{36... | collective-permute-start | bytes 393224 | tf_op jit(solution)/shard_map/ppermute | solution.py:255
  43.4 2.6 %shard_map.60 = (f32[1024,1024]{1,0:T(8,128)S(1)}, bf16[1024,512]{1,0:T(8,128)(2,1)S(1)}, bf16[1024,512]{1,0:T(8,128)(2,1)S(1)}, f32[8,128]{1,0:T(8,128)S(1)}, f32[1,1024]{1,0:T(1,128)S(1)}) custom-call(bf16[256,512]{1,0:T(8,128)(2,1)S(1)} %bitcast.9, bf16[256,512]{1,0:T(8,128)(2,1)S(1)} %collective-permute-done.s1, ...), custom_call_target="tpu_custom_call" | custom-call | flops 805306368 | bytes 4194304 | tf_op jit(solution)/shard_map/pallas_call | solution.py:295
  47.8 1.8 %collective-permute-start.8 = (f32[8,128]{1,0:T(8,128)S(1)}, f32[8,128]{1,0:T(8,128)S(1)}, u32[]{:S(2)}, u32[]{:S(2)}) collective-permute-start(f32[8,128]{1,0:T(8,128)S(1)} %get-tuple-element.31.r0), channel_id=1, source_target_pairs={{0,33},{1,32},{32,1},{33,0},{2,35},{3,34},{34,3},{35,2},{4,37},{5,... | collective-permute-start | bytes 12296 | tf_op jit(solution)/shard_map/ppermute | solution.py:255
  49.6 1.7 %collective-permute-start.7 = (f32[8,128]{1,0:T(8,128)S(1)}, f32[8,128]{1,0:T(8,128)S(1)}, u32[]{:S(2)}, u32[]{:S(2)}) collective-permute-start(f32[8,128]{1,0:T(8,128)S(1)} %get-tuple-element.31.r0), channel_id=1, source_target_pairs={{0,32},{32,0},{1,33},{33,1},{2,34},{34,2},{3,35},{35,3},{4,36},{36... | collective-permute-start | bytes 12296 | tf_op jit(solution)/shard_map/ppermute | solution.py:255
  53.2 1.7 %collective-permute-done.6.r1 = f32[8,128]{1,0:T(8,128)S(1)} collective-permute-done((f32[8,128]{1,0:T(8,128)S(1)}, f32[8,128]{1,0:T(8,128)S(1)}, u32[]{:S(2)}, u32[]{:S(2)}) %collective-permute-start.6) | collective-permute-done | bytes 4128 | tf_op jit(solution)/shard_map/ppermute | solution.py:255
  54.9 1.1 shard_map.62
  56.5 1.7 %collective-permute-start.9 = (f32[8,128]{1,0:T(8,128)S(1)}, f32[8,128]{1,0:T(8,128)S(1)}, u32[]{:S(2)}, u32[]{:S(2)}) collective-permute-start(f32[8,128]{1,0:T(8,128)S(1)} %get-tuple-element.32.c0), channel_id=1, source_target_pairs={{0,4},{4,0},{1,5},{5,1},{2,6},{6,2},{3,7},{7,3},{8,12},{12,8},{9,1... | collective-permute-start | bytes 12296 | tf_op jit(solution)/shard_map/ppermute | solution.py:255
  60.1 1.2 shard_map.63.r0
  61.3 1.1 collective-permute-start.14
  62.9 2.0 %collective-permute-start.12 = (f32[8,128]{1,0:T(8,128)S(1)}, f32[8,128]{1,0:T(8,128)S(1)}, u32[]{:S(2)}, u32[]{:S(2)}) collective-permute-start(f32[8,128]{1,0:T(8,128)S(1)} %shard_map.63.r0), channel_id=1, source_target_pairs={{0,1},{1,0},{2,3},{3,2},{4,5},{5,4},{6,7},{7,6},{8,9},{9,8},{10,11... | collective-permute-start | bytes 12296 | tf_op jit(solution)/shard_map/ppermute | solution.py:255
  66.5 1.1 shard_map.64
  67.7 1.8 %collective-permute-start.16 = (f32[8,128]{1,0:T(8,128)S(1)}, f32[8,128]{1,0:T(8,128)S(1)}, u32[]{:S(2)}, u32[]{:S(2)}) collective-permute-start(f32[8,128]{1,0:T(8,128)S(1)} %get-tuple-element.33.c0), channel_id=1, source_target_pairs={{0,16},{16,0},{1,17},{17,1},{2,18},{18,2},{3,19},{19,3},{4,20},{20... | collective-permute-start | bytes 12296 | tf_op jit(solution)/shard_map/ppermute | solution.py:255
  70.7 2.4 %collective-permute-done.15.c1 = f32[8,128]{1,0:T(8,128)S(1)} collective-permute-done((f32[8,128]{1,0:T(8,128)S(1)}, f32[8,128]{1,0:T(8,128)S(1)}, u32[]{:S(2)}, u32[]{:S(2)}) %collective-permute-start.15) | collective-permute-done | bytes 4128 | tf_op jit(solution)/shard_map/ppermute | solution.py:255
  73.1 1.2 shard_map.65.r0
  74.3 1.8 %collective-permute-start.20 = (f32[8,128]{1,0:T(8,128)S(1)}, f32[8,128]{1,0:T(8,128)S(1)}, u32[]{:S(2)}, u32[]{:S(2)}) collective-permute-start(f32[8,128]{1,0:T(8,128)S(1)} %shard_map.65.r0), channel_id=1, source_target_pairs={{0,33},{1,32},{32,1},{33,0},{2,35},{3,34},{34,3},{35,2},{4,37},{5,... | collective-permute-start | bytes 12296 | tf_op jit(solution)/shard_map/ppermute | solution.py:255
  76.1 1.7 %collective-permute-start.19 = (f32[8,128]{1,0:T(8,128)S(1)}, f32[8,128]{1,0:T(8,128)S(1)}, u32[]{:S(2)}, u32[]{:S(2)}) collective-permute-start(f32[8,128]{1,0:T(8,128)S(1)} %shard_map.65.r0), channel_id=1, source_target_pairs={{0,32},{32,0},{1,33},{33,1},{2,34},{34,2},{3,35},{35,3},{4,36},{36... | collective-permute-start | bytes 12296 | tf_op jit(solution)/shard_map/ppermute | solution.py:255
  79.7 1.7 %collective-permute-done.18.r1 = f32[8,128]{1,0:T(8,128)S(1)} collective-permute-done((f32[8,128]{1,0:T(8,128)S(1)}, f32[8,128]{1,0:T(8,128)S(1)}, u32[]{:S(2)}, u32[]{:S(2)}) %collective-permute-start.18) | collective-permute-done | bytes 4128 | tf_op jit(solution)/shard_map/ppermute | solution.py:255
  82.5 1.4 %shard_map.68 = bf16[512,512]{1,0:T(8,128)(2,1)S(1)} custom-call(f32[1024,1024]{1,0:T(8,128)S(1)} %get-tuple-element.29.m_ref, bf16[1024,512]{1,0:T(8,128)(2,1)S(1)} %get-tuple-element.30.x_ref, f32[8,128]{1,0:T(8,128)S(1)} %get-tuple-element.34.f, f32[8,128]{1,0:T(8,128)S(1)} %get-tuple-element.35.c.c0), custom_call_target="tpu_custom_call" | custom-call | flops 536870912 | bytes 4194304 | tf_op jit(solution)/shard_map/pallas_call | solution.py:295
  84.6 1.7 %collective-permute-start.22 = (f32[8,128]{1,0:T(8,128)S(1)}, f32[8,128]{1,0:T(8,128)S(1)}, u32[]{:S(2)}, u32[]{:S(2)}) collective-permute-start(f32[8,128]{1,0:T(8,128)S(1)} %get-tuple-element.35.c.c0), channel_id=1, source_target_pairs={{0,4},{4,0},{1,5},{5,1},{2,6},{6,2},{3,7},{7,3},{8,12},{12,8},{9,1... | collective-permute-start | bytes 12296 | tf_op jit(solution)/shard_map/ppermute | solution.py:255
  86.3 1.4 %shard_map.67.p_ref = bf16[512,512]{1,0:T(8,128)(2,1)S(1)} custom-call(f32[1024,1024]{1,0:T(8,128)S(1)} %get-tuple-element.29.m_ref, bf16[1024,512]{1,0:T(8,128)(2,1)S(1)} %get-tuple-element.30.x_ref, f32[8,128]{1,0:T(8,128)S(1)} %get-tuple-element.34.f, f32[8,128]{1,0:T(8,128)S(1)} %get-tuple-element.35.c.c0), custom_call_target="tpu_custom_call" | custom-call | flops 536870912 | bytes 4194304 | tf_op jit(solution)/shard_map/pallas_call | solution.py:295
  89.6 1.7 %collective-permute-start.27 = (bf16[256,512]{1,0:T(8,128)(2,1)S(1)}, bf16[256,512]{1,0:T(8,128)(2,1)S(1)}, u32[]{:S(2)}, u32[]{:S(2)}) collective-permute-start(bf16[256,512]{1,0:T(8,128)(2,1)S(1)} %get-tuple-element.40), channel_id=1, source_target_pairs={{0,32},{32,0},{1,33},{33,1},{2,34},{34,2},{3,35},{35,3},{4,36},{36... | collective-permute-start | bytes 786440 | tf_op jit(solution)/shard_map/ppermute | solution.py:255
  91.9 1.9 %collective-permute-start.28 = (bf16[256,512]{1,0:T(8,128)(2,1)S(1)}, bf16[256,512]{1,0:T(8,128)(2,1)S(1)}, u32[]{:S(2)}, u32[]{:S(2)}) collective-permute-start(bf16[256,512]{1,0:T(8,128)(2,1)S(1)} %get-tuple-element.41), channel_id=1, source_target_pairs={{0,33},{1,32},{32,1},{33,0},{2,35},{3,34},{34,3},{35,2},{4,37},{5,... | collective-permute-start | bytes 786440 | tf_op jit(solution)/shard_map/ppermute | solution.py:255
  94.4 1.8 %collective-permute-start.25 = (bf16[256,512]{1,0:T(8,128)(2,1)S(1)}, bf16[256,512]{1,0:T(8,128)(2,1)S(1)}, u32[]{:S(2)}, u32[]{:S(2)}) collective-permute-start(bf16[256,512]{1,0:T(8,128)(2,1)S(1)} %get-tuple-element.37), channel_id=1, source_target_pairs={{0,4},{4,0},{1,5},{5,1},{2,6},{6,2},{3,7},{7,3},{8,12},{12,8},{9,1... | collective-permute-start | bytes 786440 | tf_op jit(solution)/shard_map/ppermute | solution.py:255
  96.8 1.2 collective-permute-start.31
  98.0 6.5 %collective-permute-done.31.r3 = f32[8,128]{1,0:T(8,128)S(1)} collective-permute-done((f32[8,128]{1,0:T(8,128)S(1)}, f32[8,128]{1,0:T(8,128)S(1)}, u32[]{:S(2)}, u32[]{:S(2)}) %collective-permute-start.31) | collective-permute-done | bytes 4128 | tf_op jit(solution)/shard_map/ppermute | solution.py:255
  104.8 3.3 %collective-permute-done.30.r2 = f32[8,128]{1,0:T(8,128)S(1)} collective-permute-done((f32[8,128]{1,0:T(8,128)S(1)}, f32[8,128]{1,0:T(8,128)S(1)}, u32[]{:S(2)}, u32[]{:S(2)}) %collective-permute-start.30) | collective-permute-done | bytes 4128 | tf_op jit(solution)/shard_map/ppermute | solution.py:255
  108.4 3.3 %collective-permute-done.29.r1 = f32[8,128]{1,0:T(8,128)S(1)} collective-permute-done((f32[8,128]{1,0:T(8,128)S(1)}, f32[8,128]{1,0:T(8,128)S(1)}, u32[]{:S(2)}, u32[]{:S(2)}) %collective-permute-start.29) | collective-permute-done | bytes 4128 | tf_op jit(solution)/shard_map/ppermute | solution.py:255
  112.3 14.1 %all_to_all.11.back_ref = bf16[8,64,512]{2,1,0:T(8,128)(2,1)S(1)} all-to-all(bf16[8,64,512]{2,1,0:T(8,128)(2,1)S(1)} %shard_map.74), channel_id=1, replica_groups={{0,3,12,15,96,99,108,111},{1,2,13,14,97,98,109,110},{4,7,8,11,100,103,1..., dimensions={0} | all-to-all | bytes 1048576 | tf_op jit(solution)/shard_map/all_to_all | solution.py:276
  (60 shorter events, 19.2 us)
Async XLA Ops:
  26.1 6.6 %collective-permute-start.2 = (bf16[256,512]{1,0:T(8,128)(2,1)S(1)}, bf16[256,512]{1,0:T(8,128)(2,1)S(1)}, u32[]{:S(2)}, u32[]{:S(2)}) collective-permute-start(bf16[256,512]{1,0:T(8,128)(2,1)S(1)} %bitcast.4), channel_id=1, source_target_pairs={{0,4},{4,0},{1,5},{5,1},{2,6},{6,2},{3,7},{7,3},{8,12},{12,8},{9,1... | collective-permute-start | bytes 786440 | tf_op jit(solution)/shard_map/ppermute | solution.py:255
  32.7 10.6 %collective-permute-start.3 = (bf16[512,512]{1,0:T(8,128)(2,1)S(1)}, bf16[512,512]{1,0:T(8,128)(2,1)S(1)}, u32[]{:S(2)}, u32[]{:S(2)}) collective-permute-start(bf16[512,512]{1,0:T(8,128)(2,1)S(1)} %pad_maximum_fusion), channel_id=1, source_target_pairs={{0,16},{16,0},{1,17},{17,1},{2,18},{18,2},{3,19},{19,3},{4,20},{20... | collective-permute-start | bytes 1572872 | tf_op jit(solution)/shard_map/ppermute | solution.py:255
  32.8 8.7 %collective-permute-start.1 = (bf16[256,512]{1,0:T(8,128)(2,1)S(1)}, bf16[256,512]{1,0:T(8,128)(2,1)S(1)}, u32[]{:S(2)}, u32[]{:S(2)}) collective-permute-start(bf16[256,512]{1,0:T(8,128)(2,1)S(1)} %bitcast.7), channel_id=1, source_target_pairs={{0,32},{32,0},{1,33},{33,1},{2,34},{34,2},{3,35},{35,3},{4,36},{36... | collective-permute-start | bytes 786440 | tf_op jit(solution)/shard_map/ppermute | solution.py:255
  32.9 8.7 %collective-permute-start = (bf16[256,512]{1,0:T(8,128)(2,1)S(1)}, bf16[256,512]{1,0:T(8,128)(2,1)S(1)}, u32[]{:S(2)}, u32[]{:S(2)}) collective-permute-start(bf16[256,512]{1,0:T(8,128)(2,1)S(1)} %bitcast.8), channel_id=1, source_target_pairs={{0,1},{1,0},{2,3},{3,2},{4,5},{5,4},{6,7},{7,6},{8,9},{9,8},{10,11... | collective-permute-start | bytes 786440 | tf_op jit(solution)/shard_map/ppermute | solution.py:255
  41.6 5.0 %collective-permute-start.4 = (bf16[128,512]{1,0:T(8,128)(2,1)S(1)}, bf16[128,512]{1,0:T(8,128)(2,1)S(1)}, u32[]{:S(2)}, u32[]{:S(2)}) collective-permute-start(bf16[128,512]{1,0:T(8,128)(2,1)S(1)} %slice.26), channel_id=1, source_target_pairs={{0,1},{1,0},{2,3},{3,2},{4,5},{5,4},{6,7},{7,6},{8,9},{9,8},{10,11... | collective-permute-start | bytes 393224 | tf_op jit(solution)/shard_map/ppermute | solution.py:255
  41.7 5.0 %collective-permute-start.5 = (bf16[128,512]{1,0:T(8,128)(2,1)S(1)}, bf16[128,512]{1,0:T(8,128)(2,1)S(1)}, u32[]{:S(2)}, u32[]{:S(2)}) collective-permute-start(bf16[128,512]{1,0:T(8,128)(2,1)S(1)} %slice.27), channel_id=1, source_target_pairs={{0,32},{32,0},{1,33},{33,1},{2,34},{34,2},{3,35},{35,3},{4,36},{36... | collective-permute-start | bytes 393224 | tf_op jit(solution)/shard_map/ppermute | solution.py:255
  47.8 4.6 %collective-permute-start.8 = (f32[8,128]{1,0:T(8,128)S(1)}, f32[8,128]{1,0:T(8,128)S(1)}, u32[]{:S(2)}, u32[]{:S(2)}) collective-permute-start(f32[8,128]{1,0:T(8,128)S(1)} %get-tuple-element.31.r0), channel_id=1, source_target_pairs={{0,33},{1,32},{32,1},{33,0},{2,35},{3,34},{34,3},{35,2},{4,37},{5,... | collective-permute-start | bytes 12296 | tf_op jit(solution)/shard_map/ppermute | solution.py:255
  49.6 3.6 %collective-permute-start.7 = (f32[8,128]{1,0:T(8,128)S(1)}, f32[8,128]{1,0:T(8,128)S(1)}, u32[]{:S(2)}, u32[]{:S(2)}) collective-permute-start(f32[8,128]{1,0:T(8,128)S(1)} %get-tuple-element.31.r0), channel_id=1, source_target_pairs={{0,32},{32,0},{1,33},{33,1},{2,34},{34,2},{3,35},{35,3},{4,36},{36... | collective-permute-start | bytes 12296 | tf_op jit(solution)/shard_map/ppermute | solution.py:255
  51.3 3.6 %collective-permute-start.6 = (f32[8,128]{1,0:T(8,128)S(1)}, f32[8,128]{1,0:T(8,128)S(1)}, u32[]{:S(2)}, u32[]{:S(2)}) collective-permute-start(f32[8,128]{1,0:T(8,128)S(1)} %get-tuple-element.31.r0), channel_id=1, source_target_pairs={{0,1},{1,0},{2,3},{3,2},{4,5},{5,4},{6,7},{7,6},{8,9},{9,8},{10,11... | collective-permute-start | bytes 12296 | tf_op jit(solution)/shard_map/ppermute | solution.py:255
  56.0 3.1 %collective-permute-start.11 = (f32[8,128]{1,0:T(8,128)S(1)}, f32[8,128]{1,0:T(8,128)S(1)}, u32[]{:S(2)}, u32[]{:S(2)}) collective-permute-start(f32[8,128]{1,0:T(8,128)S(1)} %get-tuple-element.32.c0), channel_id=1, source_target_pairs={{0,20},{4,16},{16,4},{20,0},{1,21},{5,17},{17,5},{21,1},{2,22},{6,... | collective-permute-start | bytes 12296 | tf_op jit(solution)/shard_map/ppermute | solution.py:255
  56.1 3.0 %collective-permute-start.10 = (f32[8,128]{1,0:T(8,128)S(1)}, f32[8,128]{1,0:T(8,128)S(1)}, u32[]{:S(2)}, u32[]{:S(2)}) collective-permute-start(f32[8,128]{1,0:T(8,128)S(1)} %get-tuple-element.32.c0), channel_id=1, source_target_pairs={{0,16},{16,0},{1,17},{17,1},{2,18},{18,2},{3,19},{19,3},{4,20},{20... | collective-permute-start | bytes 12296 | tf_op jit(solution)/shard_map/ppermute | solution.py:255
  56.5 3.6 %collective-permute-start.9 = (f32[8,128]{1,0:T(8,128)S(1)}, f32[8,128]{1,0:T(8,128)S(1)}, u32[]{:S(2)}, u32[]{:S(2)}) collective-permute-start(f32[8,128]{1,0:T(8,128)S(1)} %get-tuple-element.32.c0), channel_id=1, source_target_pairs={{0,4},{4,0},{1,5},{5,1},{2,6},{6,2},{3,7},{7,3},{8,12},{12,8},{9,1... | collective-permute-start | bytes 12296 | tf_op jit(solution)/shard_map/ppermute | solution.py:255
  61.3 4.6 %collective-permute-start.14 = (f32[8,128]{1,0:T(8,128)S(1)}, f32[8,128]{1,0:T(8,128)S(1)}, u32[]{:S(2)}, u32[]{:S(2)}) collective-permute-start(f32[8,128]{1,0:T(8,128)S(1)} %shard_map.63.r0), channel_id=1, source_target_pairs={{0,33},{1,32},{32,1},{33,0},{2,35},{3,34},{34,3},{35,2},{4,37},{5,... | collective-permute-start | bytes 12296 | tf_op jit(solution)/shard_map/ppermute | solution.py:255
  62.5 3.6 %collective-permute-start.13 = (f32[8,128]{1,0:T(8,128)S(1)}, f32[8,128]{1,0:T(8,128)S(1)}, u32[]{:S(2)}, u32[]{:S(2)}) collective-permute-start(f32[8,128]{1,0:T(8,128)S(1)} %shard_map.63.r0), channel_id=1, source_target_pairs={{0,32},{32,0},{1,33},{33,1},{2,34},{34,2},{3,35},{35,3},{4,36},{36... | collective-permute-start | bytes 12296 | tf_op jit(solution)/shard_map/ppermute | solution.py:255
  62.9 3.6 %collective-permute-start.12 = (f32[8,128]{1,0:T(8,128)S(1)}, f32[8,128]{1,0:T(8,128)S(1)}, u32[]{:S(2)}, u32[]{:S(2)}) collective-permute-start(f32[8,128]{1,0:T(8,128)S(1)} %shard_map.63.r0), channel_id=1, source_target_pairs={{0,1},{1,0},{2,3},{3,2},{4,5},{5,4},{6,7},{7,6},{8,9},{9,8},{10,11... | collective-permute-start | bytes 12296 | tf_op jit(solution)/shard_map/ppermute | solution.py:255
  67.6 3.1 %collective-permute-start.17 = (f32[8,128]{1,0:T(8,128)S(1)}, f32[8,128]{1,0:T(8,128)S(1)}, u32[]{:S(2)}, u32[]{:S(2)}) collective-permute-start(f32[8,128]{1,0:T(8,128)S(1)} %get-tuple-element.33.c0), channel_id=1, source_target_pairs={{0,20},{4,16},{16,4},{20,0},{1,21},{5,17},{17,5},{21,1},{2,22},{6,... | collective-permute-start | bytes 12296 | tf_op jit(solution)/shard_map/ppermute | solution.py:255
  67.7 3.0 %collective-permute-start.16 = (f32[8,128]{1,0:T(8,128)S(1)}, f32[8,128]{1,0:T(8,128)S(1)}, u32[]{:S(2)}, u32[]{:S(2)}) collective-permute-start(f32[8,128]{1,0:T(8,128)S(1)} %get-tuple-element.33.c0), channel_id=1, source_target_pairs={{0,16},{16,0},{1,17},{17,1},{2,18},{18,2},{3,19},{19,3},{4,20},{20... | collective-permute-start | bytes 12296 | tf_op jit(solution)/shard_map/ppermute | solution.py:255
  69.5 3.6 %collective-permute-start.15 = (f32[8,128]{1,0:T(8,128)S(1)}, f32[8,128]{1,0:T(8,128)S(1)}, u32[]{:S(2)}, u32[]{:S(2)}) collective-permute-start(f32[8,128]{1,0:T(8,128)S(1)} %get-tuple-element.33.c0), channel_id=1, source_target_pairs={{0,4},{4,0},{1,5},{5,1},{2,6},{6,2},{3,7},{7,3},{8,12},{12,8},{9,1... | collective-permute-start | bytes 12296 | tf_op jit(solution)/shard_map/ppermute | solution.py:255
  74.3 4.6 %collective-permute-start.20 = (f32[8,128]{1,0:T(8,128)S(1)}, f32[8,128]{1,0:T(8,128)S(1)}, u32[]{:S(2)}, u32[]{:S(2)}) collective-permute-start(f32[8,128]{1,0:T(8,128)S(1)} %shard_map.65.r0), channel_id=1, source_target_pairs={{0,33},{1,32},{32,1},{33,0},{2,35},{3,34},{34,3},{35,2},{4,37},{5,... | collective-permute-start | bytes 12296 | tf_op jit(solution)/shard_map/ppermute | solution.py:255
  76.1 3.6 %collective-permute-start.19 = (f32[8,128]{1,0:T(8,128)S(1)}, f32[8,128]{1,0:T(8,128)S(1)}, u32[]{:S(2)}, u32[]{:S(2)}) collective-permute-start(f32[8,128]{1,0:T(8,128)S(1)} %shard_map.65.r0), channel_id=1, source_target_pairs={{0,32},{32,0},{1,33},{33,1},{2,34},{34,2},{3,35},{35,3},{4,36},{36... | collective-permute-start | bytes 12296 | tf_op jit(solution)/shard_map/ppermute | solution.py:255
  77.8 3.6 %collective-permute-start.18 = (f32[8,128]{1,0:T(8,128)S(1)}, f32[8,128]{1,0:T(8,128)S(1)}, u32[]{:S(2)}, u32[]{:S(2)}) collective-permute-start(f32[8,128]{1,0:T(8,128)S(1)} %shard_map.65.r0), channel_id=1, source_target_pairs={{0,1},{1,0},{2,3},{3,2},{4,5},{5,4},{6,7},{7,6},{8,9},{9,8},{10,11... | collective-permute-start | bytes 12296 | tf_op jit(solution)/shard_map/ppermute | solution.py:255
  84.0 9.9 %collective-permute-start.21 = (bf16[512,512]{1,0:T(8,128)(2,1)S(1)}, bf16[512,512]{1,0:T(8,128)(2,1)S(1)}, u32[]{:S(2)}, u32[]{:S(2)}) collective-permute-start(bf16[512,512]{1,0:T(8,128)(2,1)S(1)} %shard_map.68), channel_id=1, source_target_pairs={{0,16},{16,0},{1,17},{17,1},{2,18},{18,2},{3,19},{19,3},{4,20},{20... | collective-permute-start | bytes 1572872 | tf_op jit(solution)/shard_map/ppermute | solution.py:255
  84.1 3.7 %collective-permute-start.24 = (f32[8,128]{1,0:T(8,128)S(1)}, f32[8,128]{1,0:T(8,128)S(1)}, u32[]{:S(2)}, u32[]{:S(2)}) collective-permute-start(f32[8,128]{1,0:T(8,128)S(1)} %get-tuple-element.35.c.c0), channel_id=1, source_target_pairs={{0,20},{4,16},{16,4},{20,0},{1,21},{5,17},{17,5},{21,1},{2,22},{6,... | collective-permute-start | bytes 12296 | tf_op jit(solution)/shard_map/ppermute | solution.py:255
  84.5 3.3 %collective-permute-start.23 = (f32[8,128]{1,0:T(8,128)S(1)}, f32[8,128]{1,0:T(8,128)S(1)}, u32[]{:S(2)}, u32[]{:S(2)}) collective-permute-start(f32[8,128]{1,0:T(8,128)S(1)} %get-tuple-element.35.c.c0), channel_id=1, source_target_pairs={{0,16},{16,0},{1,17},{17,1},{2,18},{18,2},{3,19},{19,3},{4,20},{20... | collective-permute-start | bytes 12296 | tf_op jit(solution)/shard_map/ppermute | solution.py:255
  84.6 3.6 %collective-permute-start.22 = (f32[8,128]{1,0:T(8,128)S(1)}, f32[8,128]{1,0:T(8,128)S(1)}, u32[]{:S(2)}, u32[]{:S(2)}) collective-permute-start(f32[8,128]{1,0:T(8,128)S(1)} %get-tuple-element.35.c.c0), channel_id=1, source_target_pairs={{0,4},{4,0},{1,5},{5,1},{2,6},{6,2},{3,7},{7,3},{8,12},{12,8},{9,1... | collective-permute-start | bytes 12296 | tf_op jit(solution)/shard_map/ppermute | solution.py:255
  88.8 22.8 %collective-permute-start.26 = (bf16[256,512]{1,0:T(8,128)(2,1)S(1)}, bf16[256,512]{1,0:T(8,128)(2,1)S(1)}, u32[]{:S(2)}, u32[]{:S(2)}) collective-permute-start(bf16[256,512]{1,0:T(8,128)(2,1)S(1)} %get-tuple-element.39), channel_id=1, source_target_pairs={{0,1},{1,0},{2,3},{3,2},{4,5},{5,4},{6,7},{7,6},{8,9},{9,8},{10,11... | collective-permute-start | bytes 786440 | tf_op jit(solution)/shard_map/ppermute | solution.py:255
  89.6 22.1 %collective-permute-start.27 = (bf16[256,512]{1,0:T(8,128)(2,1)S(1)}, bf16[256,512]{1,0:T(8,128)(2,1)S(1)}, u32[]{:S(2)}, u32[]{:S(2)}) collective-permute-start(bf16[256,512]{1,0:T(8,128)(2,1)S(1)} %get-tuple-element.40), channel_id=1, source_target_pairs={{0,32},{32,0},{1,33},{33,1},{2,34},{34,2},{3,35},{35,3},{4,36},{36... | collective-permute-start | bytes 786440 | tf_op jit(solution)/shard_map/ppermute | solution.py:255
  91.9 19.7 %collective-permute-start.28 = (bf16[256,512]{1,0:T(8,128)(2,1)S(1)}, bf16[256,512]{1,0:T(8,128)(2,1)S(1)}, u32[]{:S(2)}, u32[]{:S(2)}) collective-permute-start(bf16[256,512]{1,0:T(8,128)(2,1)S(1)} %get-tuple-element.41), channel_id=1, source_target_pairs={{0,33},{1,32},{32,1},{33,0},{2,35},{3,34},{34,3},{35,2},{4,37},{5,... | collective-permute-start | bytes 786440 | tf_op jit(solution)/shard_map/ppermute | solution.py:255
  94.4 17.3 %collective-permute-start.25 = (bf16[256,512]{1,0:T(8,128)(2,1)S(1)}, bf16[256,512]{1,0:T(8,128)(2,1)S(1)}, u32[]{:S(2)}, u32[]{:S(2)}) collective-permute-start(bf16[256,512]{1,0:T(8,128)(2,1)S(1)} %get-tuple-element.37), channel_id=1, source_target_pairs={{0,4},{4,0},{1,5},{5,1},{2,6},{6,2},{3,7},{7,3},{8,12},{12,8},{9,1... | collective-permute-start | bytes 786440 | tf_op jit(solution)/shard_map/ppermute | solution.py:255
  96.8 7.6 %collective-permute-start.31 = (f32[8,128]{1,0:T(8,128)S(1)}, f32[8,128]{1,0:T(8,128)S(1)}, u32[]{:S(2)}, u32[]{:S(2)}) collective-permute-start(f32[8,128]{1,0:T(8,128)S(1)} %pad_maximum_fusion.1.r0), channel_id=1, source_target_pairs={{0,33},{1,32},{32,1},{33,0},{2,35},{3,34},{34,3},{35,2},{4,37},{5,... | collective-permute-start | bytes 12296 | tf_op jit(solution)/shard_map/ppermute | solution.py:255
  104.5 3.6 %collective-permute-start.30 = (f32[8,128]{1,0:T(8,128)S(1)}, f32[8,128]{1,0:T(8,128)S(1)}, u32[]{:S(2)}, u32[]{:S(2)}) collective-permute-start(f32[8,128]{1,0:T(8,128)S(1)} %pad_maximum_fusion.1.r0), channel_id=1, source_target_pairs={{0,32},{32,0},{1,33},{33,1},{2,34},{34,2},{3,35},{35,3},{4,36},{36... | collective-permute-start | bytes 12296 | tf_op jit(solution)/shard_map/ppermute | solution.py:255
  108.1 3.6 %collective-permute-start.29 = (f32[8,128]{1,0:T(8,128)S(1)}, f32[8,128]{1,0:T(8,128)S(1)}, u32[]{:S(2)}, u32[]{:S(2)}) collective-permute-start(f32[8,128]{1,0:T(8,128)S(1)} %pad_maximum_fusion.1.r0), channel_id=1, source_target_pairs={{0,1},{1,0},{2,3},{3,2},{4,5},{5,4},{6,7},{7,6},{8,9},{9,8},{10,11... | collective-permute-start | bytes 12296 | tf_op jit(solution)/shard_map/ppermute | solution.py:255
  (2 other events, 64.1 us)
